TPU v7x, 256 devices: a whole 4x4x8 slice. The times are simulated.
256 devices in a mesh: seq: 32 (over z_hi, y, core), head: 8 (over x, z_lo).
Axes of the slice: x: 4, y: 4, z: 8 (z_hi: 4, z_lo: 2; z = z_hi * 2 + z_lo), core: 2. Of those that a mesh axis runs over, the one named last changes fastest.
Arguments:
- sequence: bfloat16 [16384, 2048], P('seq'), may hold values from -6 to 6
- input_weight: bfloat16 [2048, 4096], P(None, 'head'), may hold values from -0.125 to 0.125
- gate_weight: bfloat16 [2048, 4096], P(None, 'head'), may hold values from -0.125 to 0.125
- state_weight: bfloat16 [2048, 256], replicated, may hold values from -0.015625 to 0.015625
- step_weight: bfloat16 [2048, 64], P(None, 'head'), may hold values from -0.125 to 0.125
- step_bias: float32 [64], P('head'), may hold values from -2 to 0
- decay_rate: float32 [64], P('head'), may hold values from 3.0517578e-05 to 0.1
- skip_gain: float32 [64], P('head'), may hold values from 0.5 to 1.5
- output_weight: bfloat16 [4096, 2048], P('head'), may hold values from -0.09375 to 0.09375
Outputs:
- encoded: bfloat16 [16384, 2048], P('seq', 'head')
All inputs are finite; a program needn't handle non-finite values.
Results may differ from a plain program's by a relative error of at most 0.014.
Values sent between devices are 32-bit elements; how exact they have to be, the bound alone decides.
No kernel may reach another device: no remote copies, remote signals or barrier semaphores. Data moves between devices by JAX's collectives and lax.ppermute only.
A program may use at most 128 MiB of HBM per device.

v0:
```python
import jax
import jax.numpy as jnp
from jax import lax
from jax.experimental import pallas as pl
from jax.experimental.pallas import tpu as pltpu
from jax.sharding import Mesh
from jax.sharding import PartitionSpec as P


F32 = jnp.float32
BF16 = jnp.bfloat16
FLIPS = (
    ("x", ((0, 1), (1, 0), (2, 3), (3, 2))),
    ("x", ((0, 3), (3, 0), (1, 2), (2, 1))),
    ("z_lo", ((0, 1), (1, 0))),
)


def dot(a, b, dims=((1,), (0,))):
    return lax.dot_general(a, b, (dims, ((), ())), preferred_element_type=F32)


def anti_identity(n):
    rows = lax.broadcasted_iota(jnp.int32, (n, n), 0)
    cols = lax.broadcasted_iota(jnp.int32, (n, n), 1)
    return jnp.where(rows + cols == n - 1, F32(1), F32(0)).astype(BF16)


def reverse_features(source, target, block):
    swap = anti_identity(block)
    count = source.shape[1] // block
    for k in range(count):
        piece = source[:, (count - 1 - k) * block : (count - k) * block]
        target[:, k * block : (k + 1) * block] = dot(piece, swap).astype(BF16)


def softplus(a):
    return jnp.maximum(a, F32(0)) + jnp.log1p(jnp.exp(-jnp.abs(a)))


def head_pick(heads, width, dtype):
    row = lax.broadcasted_iota(jnp.int32, (heads, heads * width), 0) * width
    col = lax.broadcasted_iota(jnp.int32, (heads, heads * width), 1)
    return jnp.where((col >= row) & (col < row + width), F32(1), F32(0)).astype(dtype)


def head_column(ref, rows):
    count = ref.shape[0]
    row = lax.broadcasted_iota(jnp.int32, (rows, 1), 0)
    out = jnp.zeros((rows, 1), F32)
    for h in range(count):
        out = jnp.where(lax.rem(row, count) == h, ref[h], out)
    return out


def local_kernel(
    seq_hbm, state_hbm, step_w, bias, rate, input_hbm,
    seq, flipped, in_f, in_b, proj_f, proj_b, step_out, log_out, log_cols, keep, send,
    state_w, input_w, step_both, sems,
):
    copies = [
        pltpu.make_async_copy(a, b, sems.at[k])
        for k, (a, b) in enumerate(((seq_hbm, seq), (state_hbm, state_w), (input_hbm, input_w)))
    ]
    for c in copies:
        c.start()
    rows, width = seq.shape
    heads = rate.shape[0]
    inner = input_w.shape[1]
    size = state_w.shape[1] // 2
    half = size // 2
    swap = anti_identity(256)
    step_both[:heads, :] = step_w[...].astype(F32)
    for k in range(width // 256):
        piece = step_w[:, width - (k + 1) * 256 : width - k * 256]
        step_both[heads:, k * 256 : (k + 1) * 256] = dot(piece, swap)
    r = lax.broadcasted_iota(jnp.int32, (rows, rows), 0)
    c = lax.broadcasted_iota(jnp.int32, (rows, rows), 1)
    upper = jnp.where(r <= c, F32(1), F32(0)).astype(BF16)
    lower = jnp.where(r >= c, F32(1), F32(0)).astype(BF16)
    ahead = lax.broadcasted_iota(jnp.int32, (2 * heads, 1), 0) < heads
    bias_col, rate_col = head_column(bias, 2 * heads), head_column(rate, 2 * heads)
    pick = head_pick(heads, inner // heads, F32)
    copies[0].wait()
    raw = dot(step_both[...].astype(BF16), seq[...], ((1,), (1,))) + bias_col
    steps = softplus(raw).astype(BF16)
    step = steps.astype(F32)
    step_out[...] = step
    log = -rate_col * jnp.where(ahead, dot(steps, upper), dot(steps, lower))
    log_out[...] = log
    log_cols[...] = jnp.transpose(jnp.concatenate([log] * (128 // (2 * heads)), axis=0))
    total = jnp.where(ahead, log[:, rows - 1 :], log[:, :1])
    to_end = (jnp.exp(total - log) * step).astype(BF16)
    decay = jnp.exp(total)
    d_fwd = jnp.sum(pick * decay[:heads], axis=0, keepdims=True)
    d_bwd = jnp.sum(pick * decay[heads:], axis=0, keepdims=True)
    line = lax.broadcasted_iota(jnp.int32, (8, inner), 0)
    decays = jnp.where(line == 0, d_fwd, jnp.where(line == 1, d_bwd, F32(0)))
    keep[size:, :] = decays
    send[size:, :] = decays
    reverse_features(seq, flipped, 256)
    copies[1].wait()
    for source, proj in ((seq, proj_f), (flipped, proj_b)):
        proj[...] = dot(source[...], state_w[...]).astype(BF16)
    copies[2].wait()
    mine = lax.axis_index("core") == 0
    for source, inputs, proj, b in ((seq, in_f, proj_f, 0), (flipped, in_b, proj_b, 1)):
        weight = dot(to_end[b * heads : (b + 1) * heads], pick.astype(BF16), ((0,), (0,)))
        values = dot(source[...], input_w[...]).astype(BF16)
        inputs[...] = values
        weighted = (values.astype(F32) * weight).astype(BF16)
        state = dot(proj[:, :size], weighted, ((0,), (0,)))
        at = slice(b * half, (b + 1) * half)
        keep[at, :] = jnp.where(mine, state[:half], state[half:])
        send[at, :] = jnp.where(mine, state[half:], state[:half])


def inside_kernel(b, source, gate_w, inputs, proj, step, log, log_cols, gain, base, slope, pair):
    rows = source.shape[0]
    heads = gain.shape[0]
    width = gate_w.shape[1] // heads
    size = proj.shape[1] // 2
    block = 128
    count = rows // block
    later = b == 1
    mine = slice(b * heads, (b + 1) * heads)
    pair[...] = dot(proj[:, size:], proj[:, :size], ((1,), (1,)))
    lane = lax.broadcasted_iota(jnp.int32, (block, 128), 1)
    r = lax.broadcasted_iota(jnp.int32, (block, block), 0)
    c = lax.broadcasted_iota(jnp.int32, (block, block), 1)
    pick = head_pick(heads, width, F32)
    gain_row = jnp.sum(pick * head_column(gain, heads), axis=0, keepdims=True)
    pick = pick.astype(BF16)
    gates = dot(source[...], gate_w[...]).astype(BF16).astype(F32)
    gates = gates / (1.0 + jnp.exp(-gates))
    values = inputs[...].astype(F32)
    steps = dot(step[mine, :].astype(BF16), pick, ((0,), (0,)))
    scaled = (values * steps).astype(BF16)
    ahead = dot(jnp.exp(log[mine, :]).astype(BF16), pick, ((0,), (0,)))
    slope[...] = (ahead * gates).astype(BF16)
    for k in range(count):
        at = slice(k * block, (k + 1) * block)
        lo, hi = (k * block, rows) if later else (0, (k + 1) * block)
        for p in range(heads // 2):
            cols = slice(p * 128, (p + 1) * 128)
            found = []
            for h in (2 * p, 2 * p + 1):
                row = b * heads + h
                mixed = []
                for s in range(lo // block, hi // block):
                    span = slice(s * block, (s + 1) * block)
                    spread = log_cols[at, row : row + 1] - log[row : row + 1, span]
                    if s == k:
                        spread = jnp.where((c >= r) if later else (c <= r), spread, F32(-1e30))
                    mixed.append((pair[at, span] * jnp.exp(spread)).astype(BF16))
                mixed = jnp.concatenate(mixed, axis=1) if len(mixed) > 1 else mixed[0]
                found.append(dot(mixed, scaled[lo:hi, cols]))
            inside = jnp.where(lane < width, found[0], found[1])
            total = inside + gain_row[:, cols] * values[at, cols]
            base[at, cols] = (total * gates[at, cols]).astype(BF16)


def flip_kernel(out_w, plain, flipped):
    count = plain.shape[0]
    swap = anti_identity(256)
    for j in range(count):
        piece = out_w[:, j * 256 : (j + 1) * 256]
        plain[j] = piece
        flipped[count - 1 - j] = dot(piece, swap).astype(BF16)


BLOCKS = 4
ROWS = 16


def chip_kernel(keep, got, own, to1, to2, to3, total):
    first = lax.axis_index("core") == 0
    y = lax.axis_index("y")
    size = 128
    half = size // 2
    decays = keep[size:, :] * got[size:, :]
    for b in range(2):
        at = slice(b * half, (b + 1) * half)
        mine, other = keep[at, :], got[at, :]
        d_mine, d_other = keep[size + b : size + b + 1, :], got[size + b : size + b + 1, :]
        last = first if b else jnp.logical_not(first)
        total[at, :] = jnp.where(last, d_mine * other + mine, d_other * mine + other)
    for k, ref in enumerate((own, to1, to2, to3)):
        to = lax.rem(y + k, 4)
        for b in range(2):
            start = pl.multiple_of(b * half + to * ROWS, ROWS)
            piece = total[pl.ds(start, ROWS), :]
            for j in range(BLOCKS):
                cols = slice(j * 128, (j + 1) * 128)
                row = (b * BLOCKS + j) * ROWS
                ref[row : row + ROWS, :] = piece[:, cols]
                row = 2 * BLOCKS * ROWS + b * BLOCKS + j
                ref[row : row + 1, :] = decays[b : b + 1, cols]


def state_at(ref, b, j):
    row = (b * BLOCKS + j) * ROWS
    return ref[row : row + ROWS, :]


def decay_at(ref, b, j):
    row = 2 * BLOCKS * ROWS + b * BLOCKS + j
    return ref[row : row + 1, :]


def group_kernel(own, got1, got2, got3, to1, to2, to3, ordered):
    y, z = lax.axis_index("y"), lax.axis_index("z_hi")
    for k, ref in enumerate((own, got1, got2, got3)):
        ordered[lax.rem(y + 4 - k, 4)] = ref[...]
    for j in range(BLOCKS):
        sums = []
        for b in range(2):
            state, decay = jnp.zeros((ROWS, 128), F32), jnp.ones((1, 128), F32)
            for k in (3, 2, 1, 0) if b else (0, 1, 2, 3):
                piece = ordered.at[k]
                state = decay_at(piece, b, j) * state + state_at(piece, b, j)
                decay = decay * decay_at(piece, b, j)
            sums.append((state, decay))
        for k, ref in ((1, to1), (2, to2), (3, to3)):
            up = z + k < 4
            row = j * ROWS
            ref[row : row + ROWS, :] = jnp.where(up, sums[0][0], sums[1][0])
            row = BLOCKS * ROWS + j
            ref[row : row + 1, :] = jnp.where(up, sums[0][1], sums[1][1])


def carry_kernel(ordered, got1, got2, got3, own, to1, to2, to3, carries):
    y, z = lax.axis_index("y"), lax.axis_index("z_hi")
    got = (None, got1, got2, got3)
    for j in range(BLOCKS):
        row = BLOCKS * ROWS + j
        states = [None] + [g[j * ROWS : (j + 1) * ROWS, :] for g in got[1:]]
        decays = [None] + [g[row : row + 1, :] for g in got[1:]]
        fwd = bwd = jnp.zeros((ROWS, 128), F32)
        for k in (3, 2, 1):
            fwd = jnp.where(k <= z, decays[k] * fwd + states[k], fwd)
        for k in (1, 2, 3):
            bwd = jnp.where(k > z, decays[k] * bwd + states[k], bwd)
        for b, carry in ((0, fwd), (1, bwd)):
            at = slice((b * BLOCKS + j) * ROWS, (b * BLOCKS + j + 1) * ROWS)
            for k in (3, 2, 1, 0) if b else (0, 1, 2, 3):
                carries[k, at, :] = carry
                piece = ordered.at[k]
                carry = decay_at(piece, b, j) * carry + state_at(piece, b, j)
    for k, ref in enumerate((own, to1, to2, to3)):
        ref[...] = carries[lax.rem(y + k, 4)]


def core_kernel(own, got1, got2, got3, keep, other, mine_out, other_out, chip):
    y = lax.axis_index("y")
    first = lax.axis_index("core") == 0
    half = 64
    for k, ref in enumerate((own, got1, got2, got3)):
        source = lax.rem(y + 4 - k, 4)
        for b in range(2):
            start = pl.multiple_of(b * half + source * ROWS, ROWS)
            for j in range(BLOCKS):
                chip[pl.ds(start, ROWS), j * 128 : (j + 1) * 128] = state_at(ref, b, j)
    for b in range(2):
        at = slice(b * half, (b + 1) * half)
        d = 2 * half + b
        entering = chip[at, :]
        from_mine = keep[d : d + 1, :] * entering + keep[at, :]
        from_other = other[d : d + 1, :] * entering + other[at, :]
        leads = jnp.logical_not(first) if b else first
        mine_out[at, :] = jnp.where(leads, entering, from_other)
        other_out[at, :] = jnp.where(leads, from_mine, entering)


def target_block(q):
    x, z = lax.axis_index("x"), lax.axis_index("z_lo")
    b0 = ((x ^ (x >> 1)) ^ q) & 1
    b1 = ((x >> 1) ^ (q >> 1)) & 1
    return (b1 * 2 + (b1 ^ b0)) * 2 + ((z ^ (q >> 2)) & 1)


def products(side, gated, plain, flipped, outs):
    start = 0
    for p, out in enumerate(outs):
        rows = slice(start, start + out.shape[1])
        start += out.shape[1]
        for q in range(8):
            bits = [(q >> n) & 1 for n in range(3)]
            if bits[p] != side:
                continue
            j = target_block(q)
            value = dot(gated[0, rows], plain[j]) + dot(gated[1, rows], flipped[j])
            out[bits[(p + 1) % 3] * 2 + bits[(p + 2) % 3]] = value


def sent_kernel(
    base_f, base_b, slope_f, slope_b, proj_f, proj_b, carry, got, plain, flipped,
    out0, out1, out2, gated,
):
    size = proj_f.shape[1] // 2
    half = size // 2
    first = lax.axis_index("core") == 0
    for b, base, slope, proj in ((0, base_f, slope_f, proj_f), (1, base_b, slope_b, proj_b)):
        rows = slice(b * half, (b + 1) * half)
        low = jnp.where(first, carry[rows, :], got[rows, :])
        high = jnp.where(first, got[rows, :], carry[rows, :])
        entering = jnp.concatenate([low, high], axis=0).astype(BF16)
        carried = dot(proj[:, size:], entering)
        total = base[...].astype(F32) + slope[...].astype(F32) * carried
        gated[b] = total.astype(BF16)
    products(1, gated, plain, flipped, (out0, out1, out2))


def kept_kernel(gated, plain, flipped, out0, out1, out2):
    products(0, gated, plain, flipped, (out0, out1, out2))


VMEM_SPEC = pl.BlockSpec(memory_space=pltpu.VMEM)
SMEM_SPEC = pl.BlockSpec(memory_space=pltpu.SMEM)
HBM_SPEC = pl.BlockSpec(memory_space=pl.ANY)


def near(dims, dtype=F32):
    return pltpu.VMEM(dims, dtype)


def call(kernel, args, outs, specs=None, scratch=(), flops=0):
    specs = specs or [VMEM_SPEC] * len(args)
    args = [
        pltpu.with_memory_space_constraint(a, pltpu.VMEM) if s is VMEM_SPEC else a
        for a, s in zip(args, specs)
    ]
    moved = sum(a.size * a.dtype.itemsize for a in args)
    return pl.pallas_call(
        kernel,
        out_shape=outs,
        in_specs=specs,
        out_specs=[VMEM_SPEC] * len(outs),
        scratch_shapes=scratch,
        compiler_params=pltpu.CompilerParams(vmem_limit_bytes=24 << 20),
        cost_estimate=pl.CostEstimate(flops=flops, transcendentals=0, bytes_accessed=moved),
    )(*args)


def shifted(values, axis):
    return [
        lax.ppermute(v, axis, [(j, (j + k) % 4) for j in range(4)])
        for k, v in enumerate(values, 1)
    ]


def on_device(
    sequence, input_weight, gate_weight, state_weight, step_weight,
    step_bias, decay_rate, skip_gain, output_weight,
):
    rows, width = sequence.shape
    inner = input_weight.shape[1]
    heads = decay_rate.shape[0]
    size = state_weight.shape[1] // 2
    wide, proj_dims, flat = (rows, inner), (rows, 2 * size), (2 * heads, rows)
    half_state = (size + 8, inner)
    seq, rev, in_f, in_b, proj_f, proj_b, step, log, log_cols, keep, send = call(
        local_kernel,
        (sequence, state_weight, step_weight.T, step_bias, decay_rate, input_weight),
        [near((rows, width), BF16)] * 2 + [near(wide, BF16)] * 2 + [near(proj_dims, BF16)] * 2
        + [near(flat)] * 2 + [near((rows, 128))] + [near(half_state)] * 2,
        specs=[HBM_SPEC, HBM_SPEC, VMEM_SPEC, SMEM_SPEC, SMEM_SPEC, HBM_SPEC],
        scratch=[
            pltpu.VMEM(state_weight.shape, BF16), pltpu.VMEM(input_weight.shape, BF16),
            pltpu.VMEM((2 * heads, width), F32), pltpu.SemaphoreType.DMA((3,)),
        ],
        flops=4 * rows * width * (inner + 2 * size),
    )
    swap = [(0, 1), (1, 0)]
    other = lax.ppermute(send, "core", swap)

    def inside(b, source, inputs, proj):
        return call(
            lambda *refs: inside_kernel(b, *refs),
            (source, gate_weight, inputs, proj, step, log, log_cols, skip_gain),
            [near(wide, BF16)] * 2,
            specs=[VMEM_SPEC] * 7 + [SMEM_SPEC],
            scratch=[pltpu.VMEM((rows, rows), F32)],
            flops=4 * rows * width * inner,
        )

    base_f, slope_f = inside(0, seq, in_f, proj_f)
    base_b, slope_b = inside(1, rev, in_b, proj_b)
    blocks = (8, inner, width // 8)
    plain, flipped = call(
        flip_kernel, (output_weight,), [near(blocks, BF16)] * 2, flops=inner * width * 512
    )
    message = near((2 * BLOCKS * ROWS + 8, 128))
    group = near((BLOCKS * ROWS + 8, 128))
    back = near((2 * BLOCKS * ROWS, 128))
    own, *pieces = call(chip_kernel, (keep, other), [message] * 4,
                        scratch=[pltpu.VMEM((size, inner), F32)])
    got = shifted(pieces, "y")
    *pieces, ordered = call(group_kernel, (own, *got),
                            [group] * 3 + [near((4, *message.shape))])
    far = shifted(pieces, "z_hi")
    own, *pieces = call(carry_kernel, (ordered, *far), [back] * 4,
                        scratch=[pltpu.VMEM((4, *back.shape), F32)])
    got = shifted(pieces, "y")
    carry, give = call(core_kernel, (own, *got, keep, other), [near((size, inner))] * 2,
                       scratch=[pltpu.VMEM((size, inner), F32)])
    arrived = lax.ppermute(give, "core", swap)

    parts = [near((4, r, width // 8)) for r in (176, 176, 160)]
    *sent, gated = call(
        sent_kernel,
        (base_f, base_b, slope_f, slope_b, proj_f, proj_b, carry, arrived, plain, flipped),
        parts + [near((2, rows, inner), BF16)],
        flops=2 * rows * inner * width,
    )
    kept = call(kept_kernel, (gated, plain, flipped), parts, flops=2 * rows * inner * width)
    for step in range(3):
        came = []
        for p in range(3):
            axis, pairs = FLIPS[(p + step) % 3]
            came.append(lax.ppermute(sent[p], axis, pairs))
        if step == 2:
            kept = [(a + b)[0] for a, b in zip(kept, came)]
        else:
            n = 2 - step
            sent = [a[n:] + b[n:] for a, b in zip(kept, came)]
            kept = [a[:n] + b[:n] for a, b in zip(kept, came)]
    return jnp.concatenate(kept, axis=0).astype(BF16)


def solution(mesh):
    torus = Mesh(mesh.devices.reshape(4, 4, 2, 4, 2), ("z_hi", "y", "core", "x", "z_lo"))
    seq, head = ("z_hi", "y", "core"), ("x", "z_lo")
    placed = (
        P(seq, None), P(None, head), P(None, head), P(), P(None, head),
        P(head), P(head), P(head), P(head, None),
    )
    return jax.shard_map(
        on_device, mesh=torus, in_specs=placed, out_specs=P(seq, head), check_vma=False
    )
```

profile of v0, /device:TPU:8, one launch (start us, length us, event | category | flops | bytes accessed | tf_op | source)
XLA Modules:
  0.0 94.3 jit_solution(3922589039937726374)
XLA Ops:
  0.0 1.6 %copy-done.1 = bf16[512,2048]{1,0:T(8,128)(2,1)S(1)} copy-done((bf16[512,2048]{1,0:T(8,128)(2,1)S(1)}, bf16[512,2048]{1,0:T(8,128)(2,1)}, u32[]{:S(2)}) %copy-start.1) | copy-done | bytes 2097176
  1.6 1.6 %copy-done.2 = bf16[2048,512]{1,0:T(8,128)(2,1)S(1)} copy-done((bf16[2048,512]{1,0:T(8,128)(2,1)S(1)}, bf16[2048,512]{1,0:T(8,128)(2,1)}, u32[]{:S(2)}) %copy-start.2) | copy-done | bytes 2097176
  3.2 1.2 %copy-done.4 = bf16[2048,256]{1,0:T(8,128)(2,1)S(1)} copy-done((bf16[2048,256]{1,0:T(8,128)(2,1)S(1)}, bf16[2048,256]{1,0:T(8,128)(2,1)}, u32[]{:S(2)}) %copy-start.4) | copy-done | bytes 1048600
  4.4 0.8 copy-done.5
  5.2 0.7 copy-done.6
  5.8 0.7 copy-done.7
  6.5 6.9 %shard_map.91 = (bf16[512,2048]{1,0:T(8,128)(2,1)S(1)}, bf16[512,2048]{1,0:T(8,128)(2,1)S(1)}, bf16[512,512]{1,0:T(8,128)(2,1)S(1)}, bf16[512,512]{1,0:T(8,128)(...) custom-call(bf16[512,2048]{1,0:T(8,128)(2,1)S(1)} %copy-done.1, ...), custom_call_target="tpu_custom_call" | custom-call | flops 3221225472 | bytes 5275712 | tf_op jit(solution)/shard_map/pallas_call | solution.py:334
  13.5 1.5 %collective-permute-done.got.other = f32[136,512]{1,0:T(8,128)S(1)} collective-permute-done((f32[136,512]{1,0:T(8,128)S(1)}, f32[136,512]{1,0:T(8,128)S(1)}, u32[]{:S(2)}, u32[]{:S(2)}) %collective-permute-start) | collective-permute-done | bytes 278560 | tf_op jit(solution)/shard_map/ppermute | solution.py:375
  15.1 1.7 %collective-permute-start.1 = (f32[136,128]{1,0:T(8,128)S(1)}, f32[136,128]{1,0:T(8,128)S(1)}, u32[]{:S(2)}, u32[]{:S(2)}) collective-permute-start(f32[136,128]{1,0:T(8,128)S(1)} %get-tuple-element.59), channel_id=1, source_target_pairs={{0,16},{16,32},{32,48},{48,0},{1,17},{17,33},{33,49},{49,1},{2,18}... | collective-permute-start | bytes 208904 | tf_op jit(solution)/shard_map/ppermute | solution.py:347
  16.8 2.6 %collective-permute-start.2 = (f32[136,128]{1,0:T(8,128)S(1)}, f32[136,128]{1,0:T(8,128)S(1)}, u32[]{:S(2)}, u32[]{:S(2)}) collective-permute-start(f32[136,128]{1,0:T(8,128)S(1)} %get-tuple-element.60), channel_id=1, source_target_pairs={{0,32},{16,48},{32,0},{48,16},{1,33},{17,49},{33,1},{49,17},{2,34}... | collective-permute-start | bytes 208904 | tf_op jit(solution)/shard_map/ppermute | solution.py:347
  19.4 0.7 collective-permute-start.3
  20.1 2.9 %collective-permute-done.2.got2 = f32[136,128]{1,0:T(8,128)S(1)} collective-permute-done((f32[136,128]{1,0:T(8,128)S(1)}, f32[136,128]{1,0:T(8,128)S(1)}, u32[]{:S(2)}, u32[]{:S(2)}) %collective-permute-start.2) | collective-permute-done | bytes 69664 | tf_op jit(solution)/shard_map/ppermute | solution.py:347
  23.1 0.8 collective-permute-done.3.got3
  23.9 2.6 %collective-permute-start.4 = (f32[72,128]{1,0:T(8,128)S(1)}, f32[72,128]{1,0:T(8,128)S(1)}, u32[]{:S(2)}, u32[]{:S(2)}) collective-permute-start(f32[72,128]{1,0:T(8,128)S(1)} %get-tuple-element.63), channel_id=1, source_target_pairs={{0,64},{64,128},{128,192},{192,0},{1,65},{65,129},{129,193},{193,1... | collective-permute-start | bytes 110600 | tf_op jit(solution)/shard_map/ppermute | solution.py:347
  26.4 5.4 %collective-permute-start.5 = (f32[72,128]{1,0:T(8,128)S(1)}, f32[72,128]{1,0:T(8,128)S(1)}, u32[]{:S(2)}, u32[]{:S(2)}) collective-permute-start(f32[72,128]{1,0:T(8,128)S(1)} %get-tuple-element.64), channel_id=1, source_target_pairs={{0,128},{64,192},{128,0},{192,64},{1,129},{65,193},{129,1},{193,65... | collective-permute-start | bytes 110600 | tf_op jit(solution)/shard_map/ppermute | solution.py:347
  31.8 2.7 %collective-permute-start.6 = (f32[72,128]{1,0:T(8,128)S(1)}, f32[72,128]{1,0:T(8,128)S(1)}, u32[]{:S(2)}, u32[]{:S(2)}) collective-permute-start(f32[72,128]{1,0:T(8,128)S(1)} %get-tuple-element.65), channel_id=1, source_target_pairs={{0,192},{64,0},{128,64},{192,128},{1,193},{65,1},{129,65},{193,129... | collective-permute-start | bytes 110600 | tf_op jit(solution)/shard_map/ppermute | solution.py:347
  34.5 2.2 %collective-permute-done.6.got3 = f32[72,128]{1,0:T(8,128)S(1)} collective-permute-done((f32[72,128]{1,0:T(8,128)S(1)}, f32[72,128]{1,0:T(8,128)S(1)}, u32[]{:S(2)}, u32[]{:S(2)}) %collective-permute-start.6) | collective-permute-done | bytes 36896 | tf_op jit(solution)/shard_map/ppermute | solution.py:347
  36.8 1.5 %collective-permute-start.7 = (f32[128,128]{1,0:T(8,128)S(1)}, f32[128,128]{1,0:T(8,128)S(1)}, u32[]{:S(2)}, u32[]{:S(2)}) collective-permute-start(f32[128,128]{1,0:T(8,128)S(1)} %get-tuple-element.67), channel_id=1, source_target_pairs={{0,16},{16,32},{32,48},{48,0},{1,17},{17,33},{33,49},{49,1},{2,18}... | collective-permute-start | bytes 196616 | tf_op jit(solution)/shard_map/ppermute | solution.py:347
  38.2 2.8 %collective-permute-start.8 = (f32[128,128]{1,0:T(8,128)S(1)}, f32[128,128]{1,0:T(8,128)S(1)}, u32[]{:S(2)}, u32[]{:S(2)}) collective-permute-start(f32[128,128]{1,0:T(8,128)S(1)} %get-tuple-element.68), channel_id=1, source_target_pairs={{0,32},{16,48},{32,0},{48,16},{1,33},{17,49},{33,1},{49,17},{2,34}... | collective-permute-start | bytes 196616 | tf_op jit(solution)/shard_map/ppermute | solution.py:347
  41.1 1.2 %collective-permute-start.9 = (f32[128,128]{1,0:T(8,128)S(1)}, f32[128,128]{1,0:T(8,128)S(1)}, u32[]{:S(2)}, u32[]{:S(2)}) collective-permute-start(f32[128,128]{1,0:T(8,128)S(1)} %get-tuple-element.69), channel_id=1, source_target_pairs={{0,48},{16,0},{32,16},{48,32},{1,49},{17,1},{33,17},{49,33},{2,50}... | collective-permute-start | bytes 196616 | tf_op jit(solution)/shard_map/ppermute | solution.py:347
  42.3 1.7 %collective-permute-done.8.got2 = f32[128,128]{1,0:T(8,128)S(1)} collective-permute-done((f32[128,128]{1,0:T(8,128)S(1)}, f32[128,128]{1,0:T(8,128)S(1)}, u32[]{:S(2)}, u32[]{:S(2)}) %collective-permute-start.8) | collective-permute-done | bytes 65568 | tf_op jit(solution)/shard_map/ppermute | solution.py:347
  44.0 1.3 %collective-permute-done.9.got3 = f32[128,128]{1,0:T(8,128)S(1)} collective-permute-done((f32[128,128]{1,0:T(8,128)S(1)}, f32[128,128]{1,0:T(8,128)S(1)}, u32[]{:S(2)}, u32[]{:S(2)}) %collective-permute-start.9) | collective-permute-done | bytes 65568 | tf_op jit(solution)/shard_map/ppermute | solution.py:347
  45.3 0.1 shard_map.97
  45.5 0.3 collective-permute-start.10
  45.8 3.6 %shard_map.93 = (bf16[512,512]{1,0:T(8,128)(2,1)S(1)}, bf16[512,512]{1,0:T(8,128)(2,1)S(1)}) custom-call(bf16[512,2048]{1,0:T(8,128)(2,1)S(1)} %get-tuple-element.50.refs_0_, bf16[2048,512]{1,0:T(8,128)(2,1)S(1)} %copy-done.3, bf16[512,512]{1,0:T(8,128)(2,1)S(1)} %get-tuple-element.51.refs_2_, bf16[512,256]{1,0:T(8,128)(2,1)S(1)} %get-tuple-element.52.refs_3_.proj_b, ...), custom_call_target="tpu_custom_call" | custom-call | flops 2147483648 | bytes 5308448 | tf_op jit(solution)/shard_map/pallas_call | solution.py:334
  49.4 0.7 shard_map.98
  50.1 3.4 %shard_map.92 = (bf16[512,512]{1,0:T(8,128)(2,1)S(1)}, bf16[512,512]{1,0:T(8,128)(2,1)S(1)}) custom-call(bf16[512,2048]{1,0:T(8,128)(2,1)S(1)} %get-tuple-element.43.refs_0_, bf16[2048,512]{1,0:T(8,128)(2,1)S(1)} %copy-done.3, bf16[512,512]{1,0:T(8,128)(2,1)S(1)} %get-tuple-element.44.refs_2_, bf16[512,256]{1,0:T(8,128)(2,1)S(1)} %get-tuple-element.45.refs_3_.proj_f, ...), custom_call_target="tpu_custom_call" | custom-call | flops 2147483648 | bytes 5308448 | tf_op jit(solution)/shard_map/pallas_call | solution.py:334
  53.5 1.7 %shard_map.99 = (f32[4,176,256]{2,1,0:T(8,128)S(1)}, f32[4,176,256]{2,1,0:T(8,128)S(1)}, f32[4,160,256]{2,1,0:T(8,128)S(1)}, bf16[2,512,512]{2,1,0:T(8,128)(2,1)S(1)}) custom-call(bf16[512,512]{1,0:T(8,128)(2,1)S(1)} %get-tuple-element.49.base_f, bf16[512,512]{1,0:T(8,128)(2,1)S(1)} %get-tuple-element.53.base_b, ...), custom_call_target="tpu_custom_call" | custom-call | flops 1073741824 | bytes 7340032 | tf_op jit(solution)/shard_map/pallas_call | solution.py:334
  55.2 0.8 collective-permute-start.17
  56.0 1.5 %collective-permute-start.11 = (f32[4,176,256]{2,1,0:T(8,128)S(1)}, f32[4,176,256]{2,1,0:T(8,128)S(1)}, u32[]{:S(2)}, u32[]{:S(2)}) collective-permute-start(f32[4,176,256]{2,1,0:T(8,128)S(1)} %get-tuple-element.76), channel_id=1, source_target_pairs={{0,2},{2,0},{4,6},{6,4},{1,3},{3,1},{5,7},{7,5},{8,10},{10,8},{12,... | collective-permute-start | bytes 2162696 | tf_op jit(solution)/shard_map/ppermute | solution.py:421
  57.5 2.1 %collective-permute-start.14 = (f32[4,176,256]{2,1,0:T(8,128)S(1)}, f32[4,176,256]{2,1,0:T(8,128)S(1)}, u32[]{:S(2)}, u32[]{:S(2)}) collective-permute-start(f32[4,176,256]{2,1,0:T(8,128)S(1)} %get-tuple-element.78), channel_id=1, source_target_pairs={{0,6},{6,0},{2,4},{4,2},{1,7},{7,1},{3,5},{5,3},{8,14},{14,8},{10,... | collective-permute-start | bytes 2162696 | tf_op jit(solution)/shard_map/ppermute | solution.py:421
  59.6 1.3 %shard_map.100 = (f32[4,176,256]{2,1,0:T(8,128)S(1)}, f32[4,176,256]{2,1,0:T(8,128)S(1)}, f32[4,160,256]{2,1,0:T(8,128)S(1)}) custom-call(bf16[2,512,512]{2,1,0:T(8,128)(2,1)S(1)} %get-tuple-element.74.gated, bf16[8,512,256]{2,1,0:T(8,128)(2,1)S(1)} %get-tuple-element.72.plain, bf16[8,512,256]{2,1,0:T(8,128)(2,1)S(1)} %get-tuple-element.73.flipped), custom_call_target="tpu_custom_call" | custom-call | flops 1073741824 | bytes 5242880 | tf_op jit(solution)/shard_map/pallas_call | solution.py:334
  60.9 11.5 %collective-permute-done.17 = f32[4,160,256]{2,1,0:T(8,128)S(1)} collective-permute-done((f32[4,160,256]{2,1,0:T(8,128)S(1)}, f32[4,160,256]{2,1,0:T(8,128)S(1)}, u32[]{:S(2)}, u32[]{:S(2)}) %collective-permute-start.17) | collective-permute-done | bytes 655392 | tf_op jit(solution)/shard_map/ppermute | solution.py:421
  72.5 1.6 %collective-permute-start.18 = (f32[2,160,256]{2,1,0:T(8,128)S(1)}, f32[2,160,256]{2,1,0:T(8,128)S(1)}, u32[]{:S(2)}, u32[]{:S(2)}) collective-permute-start(f32[2,160,256]{2,1,0:T(8,128)S(1)} %get-tuple-element.86), channel_id=1, source_target_pairs={{0,2},{2,0},{4,6},{6,4},{1,3},{3,1},{5,7},{7,5},{8,10},{10,8},{12,... | collective-permute-start | bytes 983048 | tf_op jit(solution)/shard_map/ppermute | solution.py:421
  74.1 0.1 collective-permute-done.11
  74.2 0.1 slice_add_fusion.3
  74.3 2.9 %collective-permute-start.12 = (f32[2,176,256]{2,1,0:T(8,128)S(1)}, f32[2,176,256]{2,1,0:T(8,128)S(1)}, u32[]{:S(2)}, u32[]{:S(2)}) collective-permute-start(f32[2,176,256]{2,1,0:T(8,128)S(1)} %get-tuple-element.82), channel_id=1, source_target_pairs={{0,6},{6,0},{2,4},{4,2},{1,7},{7,1},{3,5},{5,3},{8,14},{14,8},{10,... | collective-permute-start | bytes 1081352 | tf_op jit(solution)/shard_map/ppermute | solution.py:421
  77.2 0.1 slice_add_fusion.1
  77.3 1.3 %collective-permute-start.15 = (f32[2,176,256]{2,1,0:T(8,128)S(1)}, f32[2,176,256]{2,1,0:T(8,128)S(1)}, u32[]{:S(2)}, u32[]{:S(2)}) collective-permute-start(f32[2,176,256]{2,1,0:T(8,128)S(1)} %get-tuple-element.84), channel_id=1, source_target_pairs={{0,1},{1,0},{2,3},{3,2},{4,5},{5,4},{6,7},{7,6},{8,9},{9,8},{10,11... | collective-permute-start | bytes 1081352 | tf_op jit(solution)/shard_map/ppermute | solution.py:421
  78.6 3.2 %collective-permute-done.18 = f32[2,160,256]{2,1,0:T(8,128)S(1)} collective-permute-done((f32[2,160,256]{2,1,0:T(8,128)S(1)}, f32[2,160,256]{2,1,0:T(8,128)S(1)}, u32[]{:S(2)}, u32[]{:S(2)}) %collective-permute-start.18) | collective-permute-done | bytes 327712 | tf_op jit(solution)/shard_map/ppermute | solution.py:421
  81.8 2.8 %collective-permute-start.19 = (f32[1,160,256]{2,1,0:T(8,128)S(1)}, f32[1,160,256]{2,1,0:T(8,128)S(1)}, u32[]{:S(2)}, u32[]{:S(2)}) collective-permute-start(f32[1,160,256]{2,1,0:T(8,128)S(1)} %slice_add_fusion.10), channel_id=1, source_target_pairs={{0,6},{6,0},{2,4},{4,2},{1,7},{7,1},{3,5},{5,3},{8,14},{14,8},{10,... | collective-permute-start | bytes 491528 | tf_op jit(solution)/shard_map/ppermute | solution.py:421
  84.6 1.5 %collective-permute-done.12 = f32[2,176,256]{2,1,0:T(8,128)S(1)} collective-permute-done((f32[2,176,256]{2,1,0:T(8,128)S(1)}, f32[2,176,256]{2,1,0:T(8,128)S(1)}, u32[]{:S(2)}, u32[]{:S(2)}) %collective-permute-start.12) | collective-permute-done | bytes 360480 | tf_op jit(solution)/shard_map/ppermute | solution.py:421
  86.1 1.9 %collective-permute-start.13 = (f32[1,176,256]{2,1,0:T(8,128)S(1)}, f32[1,176,256]{2,1,0:T(8,128)S(1)}, u32[]{:S(2)}, u32[]{:S(2)}) collective-permute-start(f32[1,176,256]{2,1,0:T(8,128)S(1)} %slice_add_fusion.8), channel_id=1, source_target_pairs={{0,1},{1,0},{2,3},{3,2},{4,5},{5,4},{6,7},{7,6},{8,9},{9,8},{10,11... | collective-permute-start | bytes 540680 | tf_op jit(solution)/shard_map/ppermute | solution.py:421
  88.0 0.4 collective-permute-start.16
  88.4 0.3 collective-permute-done.19
  88.8 2.9 %collective-permute-done.13 = f32[1,176,256]{2,1,0:T(8,128)S(1)} collective-permute-done((f32[1,176,256]{2,1,0:T(8,128)S(1)}, f32[1,176,256]{2,1,0:T(8,128)S(1)}, u32[]{:S(2)}, u32[]{:S(2)}) %collective-permute-start.13) | collective-permute-done | bytes 180256 | tf_op jit(solution)/shard_map/ppermute | solution.py:421
  91.7 1.9 %collective-permute-done.16 = f32[1,176,256]{2,1,0:T(8,128)S(1)} collective-permute-done((f32[1,176,256]{2,1,0:T(8,128)S(1)}, f32[1,176,256]{2,1,0:T(8,128)S(1)}, u32[]{:S(2)}, u32[]{:S(2)}) %collective-permute-start.16) | collective-permute-done | bytes 180256 | tf_op jit(solution)/shard_map/ppermute | solution.py:421
  93.6 0.7 pad_maximum_fusion
  (30 shorter events, 0.6 us)
Async XLA Ops:
  0.0 1.6 %copy-start.1 = (bf16[512,2048]{1,0:T(8,128)(2,1)S(1)}, bf16[512,2048]{1,0:T(8,128)(2,1)}, u32[]{:S(2)}) copy-start(bf16[512,2048]{1,0:T(8,128)(2,1)} %seq_hbm.1) | copy-start | bytes 6291460
  1.6 1.6 %copy-start.2 = (bf16[2048,512]{1,0:T(8,128)(2,1)S(1)}, bf16[2048,512]{1,0:T(8,128)(2,1)}, u32[]{:S(2)}) copy-start(bf16[2048,512]{1,0:T(8,128)(2,1)} %input_hbm.1) | copy-start | bytes 6291460
  3.2 1.2 %copy-start.4 = (bf16[2048,256]{1,0:T(8,128)(2,1)S(1)}, bf16[2048,256]{1,0:T(8,128)(2,1)}, u32[]{:S(2)}) copy-start(bf16[2048,256]{1,0:T(8,128)(2,1)} %state_hbm.1) | copy-start | bytes 3145732
  4.4 0.8 copy-start.5
  5.2 0.7 copy-start.6
  5.8 0.7 copy-start.7
  6.5 39.3 %copy-start.3 = (bf16[2048,512]{1,0:T(8,128)(2,1)S(1)}, bf16[2048,512]{1,0:T(8,128)(2,1)}, u32[]{:S(2)}) copy-start(bf16[2048,512]{1,0:T(8,128)(2,1)} %refs_1_.3) | copy-start | bytes 6291460
  6.5 39.3 %copy-start.8 = (f32[8]{0:T(128)S(1)}, f32[8]{0:T(128)}, u32[]{:S(2)}) copy-start(f32[8]{0:T(128)} %refs_7_.3) | copy-start | bytes 100
  13.4 1.6 %collective-permute-start = (f32[136,512]{1,0:T(8,128)S(1)}, f32[136,512]{1,0:T(8,128)S(1)}, u32[]{:S(2)}, u32[]{:S(2)}) collective-permute-start(f32[136,512]{1,0:T(8,128)S(1)} %get-tuple-element.57), channel_id=1, source_target_pairs={{0,8},{8,0},{1,9},{9,1},{2,10},{10,2},{3,11},{11,3},{4,12},{12,4},... | collective-permute-start | bytes 835592 | tf_op jit(solution)/shard_map/ppermute | solution.py:375
  15.1 5.0 %collective-permute-start.1 = (f32[136,128]{1,0:T(8,128)S(1)}, f32[136,128]{1,0:T(8,128)S(1)}, u32[]{:S(2)}, u32[]{:S(2)}) collective-permute-start(f32[136,128]{1,0:T(8,128)S(1)} %get-tuple-element.59), channel_id=1, source_target_pairs={{0,16},{16,32},{32,48},{48,0},{1,17},{17,33},{33,49},{49,1},{2,18}... | collective-permute-start | bytes 208904 | tf_op jit(solution)/shard_map/ppermute | solution.py:347
  16.8 6.3 %collective-permute-start.2 = (f32[136,128]{1,0:T(8,128)S(1)}, f32[136,128]{1,0:T(8,128)S(1)}, u32[]{:S(2)}, u32[]{:S(2)}) collective-permute-start(f32[136,128]{1,0:T(8,128)S(1)} %get-tuple-element.60), channel_id=1, source_target_pairs={{0,32},{16,48},{32,0},{48,16},{1,33},{17,49},{33,1},{49,17},{2,34}... | collective-permute-start | bytes 208904 | tf_op jit(solution)/shard_map/ppermute | solution.py:347
  19.4 4.4 %collective-permute-start.3 = (f32[136,128]{1,0:T(8,128)S(1)}, f32[136,128]{1,0:T(8,128)S(1)}, u32[]{:S(2)}, u32[]{:S(2)}) collective-permute-start(f32[136,128]{1,0:T(8,128)S(1)} %get-tuple-element.61), channel_id=1, source_target_pairs={{0,48},{16,0},{32,16},{48,32},{1,49},{17,1},{33,17},{49,33},{2,50}... | collective-permute-start | bytes 208904 | tf_op jit(solution)/shard_map/ppermute | solution.py:347
  23.9 10.6 %collective-permute-start.4 = (f32[72,128]{1,0:T(8,128)S(1)}, f32[72,128]{1,0:T(8,128)S(1)}, u32[]{:S(2)}, u32[]{:S(2)}) collective-permute-start(f32[72,128]{1,0:T(8,128)S(1)} %get-tuple-element.63), channel_id=1, source_target_pairs={{0,64},{64,128},{128,192},{192,0},{1,65},{65,129},{129,193},{193,1... | collective-permute-start | bytes 110600 | tf_op jit(solution)/shard_map/ppermute | solution.py:347
  26.4 8.1 %collective-permute-start.5 = (f32[72,128]{1,0:T(8,128)S(1)}, f32[72,128]{1,0:T(8,128)S(1)}, u32[]{:S(2)}, u32[]{:S(2)}) collective-permute-start(f32[72,128]{1,0:T(8,128)S(1)} %get-tuple-element.64), channel_id=1, source_target_pairs={{0,128},{64,192},{128,0},{192,64},{1,129},{65,193},{129,1},{193,65... | collective-permute-start | bytes 110600 | tf_op jit(solution)/shard_map/ppermute | solution.py:347
  31.8 4.9 %collective-permute-start.6 = (f32[72,128]{1,0:T(8,128)S(1)}, f32[72,128]{1,0:T(8,128)S(1)}, u32[]{:S(2)}, u32[]{:S(2)}) collective-permute-start(f32[72,128]{1,0:T(8,128)S(1)} %get-tuple-element.65), channel_id=1, source_target_pairs={{0,192},{64,0},{128,64},{192,128},{1,193},{65,1},{129,65},{193,129... | collective-permute-start | bytes 110600 | tf_op jit(solution)/shard_map/ppermute | solution.py:347
  36.8 5.5 %collective-permute-start.7 = (f32[128,128]{1,0:T(8,128)S(1)}, f32[128,128]{1,0:T(8,128)S(1)}, u32[]{:S(2)}, u32[]{:S(2)}) collective-permute-start(f32[128,128]{1,0:T(8,128)S(1)} %get-tuple-element.67), channel_id=1, source_target_pairs={{0,16},{16,32},{32,48},{48,0},{1,17},{17,33},{33,49},{49,1},{2,18}... | collective-permute-start | bytes 196616 | tf_op jit(solution)/shard_map/ppermute | solution.py:347
  38.2 5.8 %collective-permute-start.8 = (f32[128,128]{1,0:T(8,128)S(1)}, f32[128,128]{1,0:T(8,128)S(1)}, u32[]{:S(2)}, u32[]{:S(2)}) collective-permute-start(f32[128,128]{1,0:T(8,128)S(1)} %get-tuple-element.68), channel_id=1, source_target_pairs={{0,32},{16,48},{32,0},{48,16},{1,33},{17,49},{33,1},{49,17},{2,34}... | collective-permute-start | bytes 196616 | tf_op jit(solution)/shard_map/ppermute | solution.py:347
  41.1 4.3 %collective-permute-start.9 = (f32[128,128]{1,0:T(8,128)S(1)}, f32[128,128]{1,0:T(8,128)S(1)}, u32[]{:S(2)}, u32[]{:S(2)}) collective-permute-start(f32[128,128]{1,0:T(8,128)S(1)} %get-tuple-element.69), channel_id=1, source_target_pairs={{0,48},{16,0},{32,16},{48,32},{1,49},{17,1},{33,17},{49,33},{2,50}... | collective-permute-start | bytes 196616 | tf_op jit(solution)/shard_map/ppermute | solution.py:347
  45.5 8.1 %collective-permute-start.10 = (f32[128,512]{1,0:T(8,128)S(1)}, f32[128,512]{1,0:T(8,128)S(1)}, u32[]{:S(2)}, u32[]{:S(2)}) collective-permute-start(f32[128,512]{1,0:T(8,128)S(1)} %get-tuple-element.71), channel_id=1, source_target_pairs={{0,8},{8,0},{1,9},{9,1},{2,10},{10,2},{3,11},{11,3},{4,12},{12,4},... | collective-permute-start | bytes 786440 | tf_op jit(solution)/shard_map/ppermute | solution.py:407
  45.8 3.6 %copy-start = (bf16[512,2048]{1,0:T(8,128)(2,1)S(1)}, bf16[512,2048]{1,0:T(8,128)(2,1)}, u32[]{:S(2)}) copy-start(bf16[512,2048]{1,0:T(8,128)(2,1)} %out_w.1) | copy-start | bytes 6291460
  55.2 17.2 %collective-permute-start.17 = (f32[4,160,256]{2,1,0:T(8,128)S(1)}, f32[4,160,256]{2,1,0:T(8,128)S(1)}, u32[]{:S(2)}, u32[]{:S(2)}) collective-permute-start(f32[4,160,256]{2,1,0:T(8,128)S(1)} %get-tuple-element.80), channel_id=1, source_target_pairs={{0,1},{1,0},{2,3},{3,2},{4,5},{5,4},{6,7},{7,6},{8,9},{9,8},{10,11... | collective-permute-start | bytes 1966088 | tf_op jit(solution)/shard_map/ppermute | solution.py:421
  56.0 18.2 %collective-permute-start.11 = (f32[4,176,256]{2,1,0:T(8,128)S(1)}, f32[4,176,256]{2,1,0:T(8,128)S(1)}, u32[]{:S(2)}, u32[]{:S(2)}) collective-permute-start(f32[4,176,256]{2,1,0:T(8,128)S(1)} %get-tuple-element.76), channel_id=1, source_target_pairs={{0,2},{2,0},{4,6},{6,4},{1,3},{3,1},{5,7},{7,5},{8,10},{10,8},{12,... | collective-permute-start | bytes 2162696 | tf_op jit(solution)/shard_map/ppermute | solution.py:421
  57.5 19.7 %collective-permute-start.14 = (f32[4,176,256]{2,1,0:T(8,128)S(1)}, f32[4,176,256]{2,1,0:T(8,128)S(1)}, u32[]{:S(2)}, u32[]{:S(2)}) collective-permute-start(f32[4,176,256]{2,1,0:T(8,128)S(1)} %get-tuple-element.78), channel_id=1, source_target_pairs={{0,6},{6,0},{2,4},{4,2},{1,7},{7,1},{3,5},{5,3},{8,14},{14,8},{10,... | collective-permute-start | bytes 2162696 | tf_op jit(solution)/shard_map/ppermute | solution.py:421
  72.5 9.3 %collective-permute-start.18 = (f32[2,160,256]{2,1,0:T(8,128)S(1)}, f32[2,160,256]{2,1,0:T(8,128)S(1)}, u32[]{:S(2)}, u32[]{:S(2)}) collective-permute-start(f32[2,160,256]{2,1,0:T(8,128)S(1)} %get-tuple-element.86), channel_id=1, source_target_pairs={{0,2},{2,0},{4,6},{6,4},{1,3},{3,1},{5,7},{7,5},{8,10},{10,8},{12,... | collective-permute-start | bytes 983048 | tf_op jit(solution)/shard_map/ppermute | solution.py:421
  74.3 11.7 %collective-permute-start.12 = (f32[2,176,256]{2,1,0:T(8,128)S(1)}, f32[2,176,256]{2,1,0:T(8,128)S(1)}, u32[]{:S(2)}, u32[]{:S(2)}) collective-permute-start(f32[2,176,256]{2,1,0:T(8,128)S(1)} %get-tuple-element.82), channel_id=1, source_target_pairs={{0,6},{6,0},{2,4},{4,2},{1,7},{7,1},{3,5},{5,3},{8,14},{14,8},{10,... | collective-permute-start | bytes 1081352 | tf_op jit(solution)/shard_map/ppermute | solution.py:421
  77.3 10.7 %collective-permute-start.15 = (f32[2,176,256]{2,1,0:T(8,128)S(1)}, f32[2,176,256]{2,1,0:T(8,128)S(1)}, u32[]{:S(2)}, u32[]{:S(2)}) collective-permute-start(f32[2,176,256]{2,1,0:T(8,128)S(1)} %get-tuple-element.84), channel_id=1, source_target_pairs={{0,1},{1,0},{2,3},{3,2},{4,5},{5,4},{6,7},{7,6},{8,9},{9,8},{10,11... | collective-permute-start | bytes 1081352 | tf_op jit(solution)/shard_map/ppermute | solution.py:421
  81.8 6.9 %collective-permute-start.19 = (f32[1,160,256]{2,1,0:T(8,128)S(1)}, f32[1,160,256]{2,1,0:T(8,128)S(1)}, u32[]{:S(2)}, u32[]{:S(2)}) collective-permute-start(f32[1,160,256]{2,1,0:T(8,128)S(1)} %slice_add_fusion.10), channel_id=1, source_target_pairs={{0,6},{6,0},{2,4},{4,2},{1,7},{7,1},{3,5},{5,3},{8,14},{14,8},{10,... | collective-permute-start | bytes 491528 | tf_op jit(solution)/shard_map/ppermute | solution.py:421
  86.1 5.6 %collective-permute-start.13 = (f32[1,176,256]{2,1,0:T(8,128)S(1)}, f32[1,176,256]{2,1,0:T(8,128)S(1)}, u32[]{:S(2)}, u32[]{:S(2)}) collective-permute-start(f32[1,176,256]{2,1,0:T(8,128)S(1)} %slice_add_fusion.8), channel_id=1, source_target_pairs={{0,1},{1,0},{2,3},{3,2},{4,5},{5,4},{6,7},{7,6},{8,9},{9,8},{10,11... | collective-permute-start | bytes 540680 | tf_op jit(solution)/shard_map/ppermute | solution.py:421
  88.0 5.6 %collective-permute-start.16 = (f32[1,176,256]{2,1,0:T(8,128)S(1)}, f32[1,176,256]{2,1,0:T(8,128)S(1)}, u32[]{:S(2)}, u32[]{:S(2)}) collective-permute-start(f32[1,176,256]{2,1,0:T(8,128)S(1)} %slice_add_fusion.6), channel_id=1, source_target_pairs={{0,2},{2,0},{4,6},{6,4},{1,3},{3,1},{5,7},{7,5},{8,10},{10,8},{12,... | collective-permute-start | bytes 540680 | tf_op jit(solution)/shard_map/ppermute | solution.py:421
where the time goes:
time: 95.2 us; the launch traced here: 94.3 us
  starting transfers between devices  36.7 us (39%)
  waiting for transfers between devices  31.9 us (34%)
  Pallas kernels  17.9 us (19%)
  local copies, waits for them, and re-layouts  6.49 us (7%)
  other arithmetic  1.16 us (1%)
    ppermute x9, waiting for transfers between devices, on_device(): came.append(lax.ppermute(sent[p], axis, pairs))  21.4 us
    ppermute x9, starting transfers between devices, shifted(): lax.ppermute(v, axis, [(j, (j + k) % 4) for j in range(4)])  21.1 us
    pallas_call x10, Pallas kernels, call(): pl.pallas_call(kernel, out_shape=outs, in_specs=specs, out_specs=[VMEM_SP...  17.9 us
    ppermute x9, starting transfers between devices, on_device(): came.append(lax.ppermute(sent[p], axis, pairs))  15.2 us
    ppermute x9, waiting for transfers between devices, shifted(): lax.ppermute(v, axis, [(j, (j + k) % 4) for j in range(4)])  8.95 us
    unnamed x18, local copies, waits for them, and re-layouts  6.49 us
  transfers between devices with their start and end apart: 20, of which 13 were waited for; matrix products, arithmetic and copies ran while one was open for 0% of the time, Pallas kernels for 10%

commit v1 on v0

--- a/solution.py
+++ b/solution.py
@@ -26,14 +26,6 @@
     return jnp.where(rows + cols == n - 1, F32(1), F32(0)).astype(BF16)
 
 
-def reverse_features(source, target, block):
-    swap = anti_identity(block)
-    count = source.shape[1] // block
-    for k in range(count):
-        piece = source[:, (count - 1 - k) * block : (count - k) * block]
-        target[:, k * block : (k + 1) * block] = dot(piece, swap).astype(BF16)
-
-
 def softplus(a):
     return jnp.maximum(a, F32(0)) + jnp.log1p(jnp.exp(-jnp.abs(a)))
 
@@ -54,35 +46,46 @@
 
 
 def local_kernel(
-    seq_hbm, state_hbm, step_w, bias, rate, input_hbm,
+    seq_hbm, state_hbm, step_hbm, bias_hbm, rate_hbm, input_hbm,
     seq, flipped, in_f, in_b, proj_f, proj_b, step_out, log_out, log_cols, keep, send,
-    state_w, input_w, step_both, sems,
+    state_w, input_w, step_w, bias, rate, step_both, sems,
 ):
-    copies = [
-        pltpu.make_async_copy(a, b, sems.at[k])
-        for k, (a, b) in enumerate(((seq_hbm, seq), (state_hbm, state_w), (input_hbm, input_w)))
-    ]
-    for c in copies:
-        c.start()
     rows, width = seq.shape
     heads = rate.shape[0]
     inner = input_w.shape[1]
     size = state_w.shape[1] // 2
     half = size // 2
+    chunk = 512
+    chunks = [slice(k * chunk, (k + 1) * chunk) for k in range(width // chunk)]
+    moves = [(step_hbm, step_w), (bias_hbm, bias), (rate_hbm, rate)]
+    moves += [(seq_hbm.at[:, at], seq.at[:, at]) for at in chunks]
+    moves += [(state_hbm, state_w), (input_hbm, input_w)]
+    copies = [pltpu.make_async_copy(a, b, sems.at[k]) for k, (a, b) in enumerate(moves)]
+    for c in copies:
+        c.start()
     swap = anti_identity(256)
-    step_both[:heads, :] = step_w[...].astype(F32)
-    for k in range(width // 256):
-        piece = step_w[:, width - (k + 1) * 256 : width - k * 256]
-        step_both[heads:, k * 256 : (k + 1) * 256] = dot(piece, swap)
     r = lax.broadcasted_iota(jnp.int32, (rows, rows), 0)
     c = lax.broadcasted_iota(jnp.int32, (rows, rows), 1)
     upper = jnp.where(r <= c, F32(1), F32(0)).astype(BF16)
     lower = jnp.where(r >= c, F32(1), F32(0)).astype(BF16)
     ahead = lax.broadcasted_iota(jnp.int32, (2 * heads, 1), 0) < heads
+    pick = head_pick(heads, inner // heads, F32)
+    for k in range(3):
+        copies[k].wait()
     bias_col, rate_col = head_column(bias, 2 * heads), head_column(rate, 2 * heads)
-    pick = head_pick(heads, inner // heads, F32)
-    copies[0].wait()
-    raw = dot(step_both[...].astype(BF16), seq[...], ((1,), (1,))) + bias_col
+    step_both[:heads, :] = step_w[...].astype(F32)
+    for k in range(width // 256):
+        piece = step_w[:, width - (k + 1) * 256 : width - k * 256]
+        step_both[heads:, k * 256 : (k + 1) * 256] = dot(piece, swap)
+    raw = jnp.zeros((2 * heads, rows), F32) + bias_col
+    for k, at in enumerate(chunks):
+        copies[3 + k].wait()
+        raw = raw + dot(step_both[:, at].astype(BF16), seq[:, at], ((1,), (1,)))
+        for j in range(at.start, at.stop, 256):
+            flipped[:, width - j - 256 : width - j] = dot(seq[:, j : j + 256], swap).astype(BF16)
+    copies[3 + len(chunks)].wait()
+    for source, proj in ((seq, proj_f), (flipped, proj_b)):
+        proj[...] = dot(source[...], state_w[...]).astype(BF16)
     steps = softplus(raw).astype(BF16)
     step = steps.astype(F32)
     step_out[...] = step
@@ -98,11 +101,7 @@
     decays = jnp.where(line == 0, d_fwd, jnp.where(line == 1, d_bwd, F32(0)))
     keep[size:, :] = decays
     send[size:, :] = decays
-    reverse_features(seq, flipped, 256)
-    copies[1].wait()
-    for source, proj in ((seq, proj_f), (flipped, proj_b)):
-        proj[...] = dot(source[...], state_w[...]).astype(BF16)
-    copies[2].wait()
+    copies[4 + len(chunks)].wait()
     mine = lax.axis_index("core") == 0
     for source, inputs, proj, b in ((seq, in_f, proj_f, 0), (flipped, in_b, proj_b, 1)):
         weight = dot(to_end[b * heads : (b + 1) * heads], pick.astype(BF16), ((0,), (0,)))
@@ -279,45 +278,44 @@
     return (b1 * 2 + (b1 ^ b0)) * 2 + ((z ^ (q >> 2)) & 1)
 
 
-def products(side, gated, plain, flipped, outs):
-    start = 0
-    for p, out in enumerate(outs):
-        rows = slice(start, start + out.shape[1])
-        start += out.shape[1]
-        for q in range(8):
-            bits = [(q >> n) & 1 for n in range(3)]
-            if bits[p] != side:
-                continue
-            j = target_block(q)
-            value = dot(gated[0, rows], plain[j]) + dot(gated[1, rows], flipped[j])
-            out[bits[(p + 1) % 3] * 2 + bits[(p + 2) % 3]] = value
-
-
-def sent_kernel(
-    base_f, base_b, slope_f, slope_b, proj_f, proj_b, carry, got, plain, flipped,
-    out0, out1, out2, gated,
+def output_kernel(
+    first_row, base_f, base_b, slope_f, slope_b, proj_f, proj_b, carry, got, plain, flipped, *outs
 ):
+    count = sum(out.shape[1] for out in outs[:3])
+    at = slice(first_row, first_row + count)
     size = proj_f.shape[1] // 2
     half = size // 2
-    first = lax.axis_index("core") == 0
+    low_core = lax.axis_index("core") == 0
+    gated = []
     for b, base, slope, proj in ((0, base_f, slope_f, proj_f), (1, base_b, slope_b, proj_b)):
         rows = slice(b * half, (b + 1) * half)
-        low = jnp.where(first, carry[rows, :], got[rows, :])
-        high = jnp.where(first, got[rows, :], carry[rows, :])
+        low = jnp.where(low_core, carry[rows, :], got[rows, :])
+        high = jnp.where(low_core, got[rows, :], carry[rows, :])
         entering = jnp.concatenate([low, high], axis=0).astype(BF16)
-        carried = dot(proj[:, size:], entering)
-        total = base[...].astype(F32) + slope[...].astype(F32) * carried
-        gated[b] = total.astype(BF16)
-    products(1, gated, plain, flipped, (out0, out1, out2))
-
-
-def kept_kernel(gated, plain, flipped, out0, out1, out2):
-    products(0, gated, plain, flipped, (out0, out1, out2))
+        carried = dot(proj[at, size:], entering)
+        total = base[at, :].astype(F32) + slope[at, :].astype(F32) * carried
+        gated.append(total.astype(BF16))
+    for q in (7, 6, 5, 3, 4, 2, 1, 0):
+        bits = [(q >> n) & 1 for n in range(3)]
+        j = target_block(q)
+        value = dot(gated[0], plain[j]) + dot(gated[1], flipped[j])
+        start = 0
+        for p in range(3):
+            out = outs[3 * bits[p] + p]
+            stop = start + out.shape[1]
+            out[bits[(p + 1) % 3] * 2 + bits[(p + 2) % 3]] = value[start:stop]
+            start = stop
+
+
+def sum_kernel(kept, came, kept_out, sent_out):
+    half = kept_out.shape[0]
+    kept_out[...] = kept[:half] + came[:half]
+    sent_out[...] = kept[half:] + came[half:]
 
 
 VMEM_SPEC = pl.BlockSpec(memory_space=pltpu.VMEM)
 SMEM_SPEC = pl.BlockSpec(memory_space=pltpu.SMEM)
-HBM_SPEC = pl.BlockSpec(memory_space=pl.ANY)
+HBM_SPEC = pl.BlockSpec(memory_space=pltpu.HBM)
 
 
 def near(dims, dtype=F32):
@@ -327,7 +325,7 @@
 def call(kernel, args, outs, specs=None, scratch=(), flops=0):
     specs = specs or [VMEM_SPEC] * len(args)
     args = [
-        pltpu.with_memory_space_constraint(a, pltpu.VMEM) if s is VMEM_SPEC else a
+        a if s is SMEM_SPEC else pltpu.with_memory_space_constraint(a, s.memory_space)
         for a, s in zip(args, specs)
     ]
     moved = sum(a.size * a.dtype.itemsize for a in args)
@@ -364,10 +362,11 @@
         (sequence, state_weight, step_weight.T, step_bias, decay_rate, input_weight),
         [near((rows, width), BF16)] * 2 + [near(wide, BF16)] * 2 + [near(proj_dims, BF16)] * 2
         + [near(flat)] * 2 + [near((rows, 128))] + [near(half_state)] * 2,
-        specs=[HBM_SPEC, HBM_SPEC, VMEM_SPEC, SMEM_SPEC, SMEM_SPEC, HBM_SPEC],
+        specs=[HBM_SPEC] * 6,
         scratch=[
             pltpu.VMEM(state_weight.shape, BF16), pltpu.VMEM(input_weight.shape, BF16),
-            pltpu.VMEM((2 * heads, width), F32), pltpu.SemaphoreType.DMA((3,)),
+            pltpu.VMEM((heads, width), BF16), pltpu.SMEM((heads,), F32), pltpu.SMEM((heads,), F32),
+            pltpu.VMEM((2 * heads, width), F32), pltpu.SemaphoreType.DMA((9,)),
         ],
         flops=4 * rows * width * (inner + 2 * size),
     )
@@ -406,26 +405,36 @@
                        scratch=[pltpu.VMEM((size, inner), F32)])
     arrived = lax.ppermute(give, "core", swap)
 
-    parts = [near((4, r, width // 8)) for r in (176, 176, 160)]
-    *sent, gated = call(
-        sent_kernel,
-        (base_f, base_b, slope_f, slope_b, proj_f, proj_b, carry, arrived, plain, flipped),
-        parts + [near((2, rows, inner), BF16)],
-        flops=2 * rows * inner * width,
-    )
-    kept = call(kept_kernel, (gated, plain, flipped), parts, flops=2 * rows * inner * width)
+    whole, first_row, parts = [], 0, []
+    for group, counts in enumerate(((96, 96, 80), (80, 80, 80))):
+        outs = call(
+            lambda *refs, at=first_row: output_kernel(at, *refs),
+            (base_f, base_b, slope_f, slope_b, proj_f, proj_b, carry, arrived, plain, flipped),
+            [near((4, r, width // 8)) for r in counts] * 2,
+            flops=4 * sum(counts) * inner * width,
+        )
+        first_row += sum(counts)
+        parts.append([outs[:3], outs[3:]])
     for step in range(3):
-        came = []
-        for p in range(3):
-            axis, pairs = FLIPS[(p + step) % 3]
-            came.append(lax.ppermute(sent[p], axis, pairs))
-        if step == 2:
-            kept = [(a + b)[0] for a, b in zip(kept, came)]
-        else:
-            n = 2 - step
-            sent = [a[n:] + b[n:] for a, b in zip(kept, came)]
-            kept = [a[:n] + b[:n] for a, b in zip(kept, came)]
-    return jnp.concatenate(kept, axis=0).astype(BF16)
+        for group in range(2):
+            kept, sent = parts[group]
+            came = []
+            for p in range(3):
+                axis, pairs = FLIPS[(p + step) % 3]
+                came.append(lax.ppermute(sent[p], axis, pairs))
+            if step == 2:
+                whole += [(a + b)[0] for a, b in zip(kept, came)]
+            else:
+                n = 2 - step
+                sums = [
+                    call(
+                        sum_kernel, (kept[p], came[p]),
+                        [near((n, *came[p].shape[1:]))] * 2,
+                    )
+                    for p in range(3)
+                ]
+                parts[group] = [[a for a, _ in sums], [b for _, b in sums]]
+    return jnp.concatenate(whole, axis=0).astype(BF16)
 
 
 def solution(mesh):

time: 95.2 us -> 91.4 us (0.960)
  starting transfers between devices: 36.7 us -> 43.5 us
  waiting for transfers between devices: 31.9 us -> 25.6 us
  local copies, waits for them, and re-layouts: 6.49 us -> 0.7 us
    ppermute x9 -> x18, starting transfers between devices: 15.2 us -> 22.1 us  [on_device(): came.append(lax.ppermute(sent[p], axis, pairs))]
    ppermute x9 -> x18, waiting for transfers between devices: 21.4 us -> 15.1 us  [on_device(): came.append(lax.ppermute(sent[p], axis, pairs))]
    unnamed x18 -> x8, local copies, waits for them, and re-layouts: 6.49 us -> 0.7 us
    pallas_call x10 -> x22, Pallas kernels: 17.9 us -> 18.8 us  [call(): pl.pallas_call(kernel, out_shape=outs, in_specs=specs, out_specs=[VMEM_SP...]
  transfers between devices with their start and end apart: 20 -> 29, of which waited for: 13 -> 12; matrix products, arithmetic and copies ran while one was open for 0% -> 0% of each run, Pallas kernels for 10% -> 10%
where the time goes in v1:
time: 91.4 us; the launch traced here: 89.6 us
  starting transfers between devices  43.5 us (48%)
  waiting for transfers between devices  25.6 us (28%)
  Pallas kernels  18.8 us (21%)
    ppermute x18, starting transfers between devices, on_device(): came.append(lax.ppermute(sent[p], axis, pairs))  22.1 us
    ppermute x9, starting transfers between devices, shifted(): lax.ppermute(v, axis, [(j, (j + k) % 4) for j in range(4)])  21.1 us
    pallas_call x22, Pallas kernels, call(): pl.pallas_call(kernel, out_shape=outs, in_specs=specs, out_specs=[VMEM_SP...  18.8 us
    ppermute x18, waiting for transfers between devices, on_device(): came.append(lax.ppermute(sent[p], axis, pairs))  15.1 us
    ppermute x9, waiting for transfers between devices, shifted(): lax.ppermute(v, axis, [(j, (j + k) % 4) for j in range(4)])  8.86 us
  transfers between devices with their start and end apart: 29, of which 12 were waited for; matrix products, arithmetic and copies ran while one was open for 0% of the time, Pallas kernels for 10%

profile of v1, /device:TPU:8, one launch (start us, length us, event | category | flops | bytes accessed | tf_op | source)
XLA Modules:
  0.0 89.6 jit_solution(11281611055669360519)
XLA Ops:
  0.0 7.5 %shard_map.91 = (bf16[512,2048]{1,0:T(8,128)(2,1)S(1)}, bf16[512,2048]{1,0:T(8,128)(2,1)S(1)}, bf16[512,512]{1,0:T(8,128)(2,1)S(1)}, bf16[512,512]{1,0:T(8,128)(...) custom-call(bf16[512,2048]{1,0:T(8,128)(2,1)} %seq_hbm.1, ...), custom_call_target="tpu_custom_call" | custom-call | flops 3221225472 | bytes 5275712 | tf_op jit(solution)/shard_map/pallas_call | solution.py:332
  7.7 1.5 %collective-permute-done.got.other = f32[136,512]{1,0:T(8,128)S(1)} collective-permute-done((f32[136,512]{1,0:T(8,128)S(1)}, f32[136,512]{1,0:T(8,128)S(1)}, u32[]{:S(2)}, u32[]{:S(2)}) %collective-permute-start) | collective-permute-done | bytes 278560 | tf_op jit(solution)/shard_map/ppermute | solution.py:374
  9.3 1.7 %collective-permute-start.1 = (f32[136,128]{1,0:T(8,128)S(1)}, f32[136,128]{1,0:T(8,128)S(1)}, u32[]{:S(2)}, u32[]{:S(2)}) collective-permute-start(f32[136,128]{1,0:T(8,128)S(1)} %get-tuple-element.88), channel_id=1, source_target_pairs={{0,16},{16,32},{32,48},{48,0},{1,17},{17,33},{33,49},{49,1},{2,18}... | collective-permute-start | bytes 208904 | tf_op jit(solution)/shard_map/ppermute | solution.py:345
  10.9 2.6 %collective-permute-start.2 = (f32[136,128]{1,0:T(8,128)S(1)}, f32[136,128]{1,0:T(8,128)S(1)}, u32[]{:S(2)}, u32[]{:S(2)}) collective-permute-start(f32[136,128]{1,0:T(8,128)S(1)} %get-tuple-element.89), channel_id=1, source_target_pairs={{0,32},{16,48},{32,0},{48,16},{1,33},{17,49},{33,1},{49,17},{2,34}... | collective-permute-start | bytes 208904 | tf_op jit(solution)/shard_map/ppermute | solution.py:345
  13.6 0.7 collective-permute-start.3
  14.3 2.9 %collective-permute-done.2.got2 = f32[136,128]{1,0:T(8,128)S(1)} collective-permute-done((f32[136,128]{1,0:T(8,128)S(1)}, f32[136,128]{1,0:T(8,128)S(1)}, u32[]{:S(2)}, u32[]{:S(2)}) %collective-permute-start.2) | collective-permute-done | bytes 69664 | tf_op jit(solution)/shard_map/ppermute | solution.py:345
  17.2 0.8 collective-permute-done.3.got3
  18.1 2.6 %collective-permute-start.4 = (f32[72,128]{1,0:T(8,128)S(1)}, f32[72,128]{1,0:T(8,128)S(1)}, u32[]{:S(2)}, u32[]{:S(2)}) collective-permute-start(f32[72,128]{1,0:T(8,128)S(1)} %get-tuple-element.92), channel_id=1, source_target_pairs={{0,64},{64,128},{128,192},{192,0},{1,65},{65,129},{129,193},{193,1... | collective-permute-start | bytes 110600 | tf_op jit(solution)/shard_map/ppermute | solution.py:345
  20.6 5.4 %collective-permute-start.5 = (f32[72,128]{1,0:T(8,128)S(1)}, f32[72,128]{1,0:T(8,128)S(1)}, u32[]{:S(2)}, u32[]{:S(2)}) collective-permute-start(f32[72,128]{1,0:T(8,128)S(1)} %get-tuple-element.93), channel_id=1, source_target_pairs={{0,128},{64,192},{128,0},{192,64},{1,129},{65,193},{129,1},{193,65... | collective-permute-start | bytes 110600 | tf_op jit(solution)/shard_map/ppermute | solution.py:345
  26.0 2.7 %collective-permute-start.6 = (f32[72,128]{1,0:T(8,128)S(1)}, f32[72,128]{1,0:T(8,128)S(1)}, u32[]{:S(2)}, u32[]{:S(2)}) collective-permute-start(f32[72,128]{1,0:T(8,128)S(1)} %get-tuple-element.94), channel_id=1, source_target_pairs={{0,192},{64,0},{128,64},{192,128},{1,193},{65,1},{129,65},{193,129... | collective-permute-start | bytes 110600 | tf_op jit(solution)/shard_map/ppermute | solution.py:345
  28.7 2.2 %collective-permute-done.6.got3 = f32[72,128]{1,0:T(8,128)S(1)} collective-permute-done((f32[72,128]{1,0:T(8,128)S(1)}, f32[72,128]{1,0:T(8,128)S(1)}, u32[]{:S(2)}, u32[]{:S(2)}) %collective-permute-start.6) | collective-permute-done | bytes 36896 | tf_op jit(solution)/shard_map/ppermute | solution.py:345
  31.0 1.5 %collective-permute-start.7 = (f32[128,128]{1,0:T(8,128)S(1)}, f32[128,128]{1,0:T(8,128)S(1)}, u32[]{:S(2)}, u32[]{:S(2)}) collective-permute-start(f32[128,128]{1,0:T(8,128)S(1)} %get-tuple-element.96), channel_id=1, source_target_pairs={{0,16},{16,32},{32,48},{48,0},{1,17},{17,33},{33,49},{49,1},{2,18}... | collective-permute-start | bytes 196616 | tf_op jit(solution)/shard_map/ppermute | solution.py:345
  32.4 2.7 %collective-permute-start.8 = (f32[128,128]{1,0:T(8,128)S(1)}, f32[128,128]{1,0:T(8,128)S(1)}, u32[]{:S(2)}, u32[]{:S(2)}) collective-permute-start(f32[128,128]{1,0:T(8,128)S(1)} %get-tuple-element.97), channel_id=1, source_target_pairs={{0,32},{16,48},{32,0},{48,16},{1,33},{17,49},{33,1},{49,17},{2,34}... | collective-permute-start | bytes 196616 | tf_op jit(solution)/shard_map/ppermute | solution.py:345
  35.2 1.3 %collective-permute-start.9 = (f32[128,128]{1,0:T(8,128)S(1)}, f32[128,128]{1,0:T(8,128)S(1)}, u32[]{:S(2)}, u32[]{:S(2)}) collective-permute-start(f32[128,128]{1,0:T(8,128)S(1)} %get-tuple-element.98), channel_id=1, source_target_pairs={{0,48},{16,0},{32,16},{48,32},{1,49},{17,1},{33,17},{49,33},{2,50}... | collective-permute-start | bytes 196616 | tf_op jit(solution)/shard_map/ppermute | solution.py:345
  36.5 1.7 %collective-permute-done.8.got2 = f32[128,128]{1,0:T(8,128)S(1)} collective-permute-done((f32[128,128]{1,0:T(8,128)S(1)}, f32[128,128]{1,0:T(8,128)S(1)}, u32[]{:S(2)}, u32[]{:S(2)}) %collective-permute-start.8) | collective-permute-done | bytes 65568 | tf_op jit(solution)/shard_map/ppermute | solution.py:345
  38.2 1.2 %collective-permute-done.9.got3 = f32[128,128]{1,0:T(8,128)S(1)} collective-permute-done((f32[128,128]{1,0:T(8,128)S(1)}, f32[128,128]{1,0:T(8,128)S(1)}, u32[]{:S(2)}, u32[]{:S(2)}) %collective-permute-start.9) | collective-permute-done | bytes 65568 | tf_op jit(solution)/shard_map/ppermute | solution.py:345
  39.4 0.1 shard_map.97
  39.5 0.3 collective-permute-start.10
  39.9 3.3 %shard_map.92 = (bf16[512,512]{1,0:T(8,128)(2,1)S(1)}, bf16[512,512]{1,0:T(8,128)(2,1)S(1)}) custom-call(bf16[512,2048]{1,0:T(8,128)(2,1)S(1)} %get-tuple-element.72.refs_0_, bf16[2048,512]{1,0:T(8,128)(2,1)S(1)} %copy-done.1, bf16[512,512]{1,0:T(8,128)(2,1)S(1)} %get-tuple-element.73.refs_2_, bf16[512,256]{1,0:T(8,128)(2,1)S(1)} %get-tuple-element.74.refs_3_.refs_4_, ...), custom_call_target="tpu_custom_call" | custom-call | flops 2147483648 | bytes 5308448 | tf_op jit(solution)/shard_map/pallas_call | solution.py:332
  43.2 0.7 shard_map.98
  44.0 3.6 %shard_map.93 = (bf16[512,512]{1,0:T(8,128)(2,1)S(1)}, bf16[512,512]{1,0:T(8,128)(2,1)S(1)}) custom-call(bf16[512,2048]{1,0:T(8,128)(2,1)S(1)} %get-tuple-element.79.refs_0_, bf16[2048,512]{1,0:T(8,128)(2,1)S(1)} %copy-done.1, bf16[512,512]{1,0:T(8,128)(2,1)S(1)} %get-tuple-element.80.refs_2_, bf16[512,256]{1,0:T(8,128)(2,1)S(1)} %get-tuple-element.81.refs_3_.refs_5_, ...), custom_call_target="tpu_custom_call" | custom-call | flops 2147483648 | bytes 5308448 | tf_op jit(solution)/shard_map/pallas_call | solution.py:332
  47.5 1.6 %shard_map.99 = (f32[4,96,256]{2,1,0:T(8,128)S(1)}, f32[4,96,256]{2,1,0:T(8,128)S(1)}, f32[4,80,256]{2,1,0:T(8,128)S(1)}, f32[4,96,256]{2,1,0:T(8,128)S(1)}, f32...) custom-call(bf16[512,512]{1,0:T(8,128)(2,1)S(1)} %get-tuple-element.78.refs_0_, ...), custom_call_target="tpu_custom_call" | custom-call | flops 1140850688 | bytes 7340032 | tf_op jit(solution)/shard_map/pallas_call | solution.py:332
  49.1 1.7 %collective-permute-start.11 = (f32[4,96,256]{2,1,0:T(8,128)S(1)}, f32[4,96,256]{2,1,0:T(8,128)S(1)}, u32[]{:S(2)}, u32[]{:S(2)}) collective-permute-start(f32[4,96,256]{2,1,0:T(8,128)S(1)} %get-tuple-element.104), channel_id=1, source_target_pairs={{0,2},{2,0},{4,6},{6,4},{1,3},{3,1},{5,7},{7,5},{8,10},{10,8},{12,... | collective-permute-start | bytes 1179656 | tf_op jit(solution)/shard_map/ppermute | solution.py:424
  50.7 0.7 collective-permute-start.17
  51.4 2.1 %collective-permute-start.14 = (f32[4,96,256]{2,1,0:T(8,128)S(1)}, f32[4,96,256]{2,1,0:T(8,128)S(1)}, u32[]{:S(2)}, u32[]{:S(2)}) collective-permute-start(f32[4,96,256]{2,1,0:T(8,128)S(1)} %get-tuple-element.110), channel_id=1, source_target_pairs={{0,6},{6,0},{2,4},{4,2},{1,7},{7,1},{3,5},{5,3},{8,14},{14,8},{10,... | collective-permute-start | bytes 1179656 | tf_op jit(solution)/shard_map/ppermute | solution.py:424
  53.6 1.4 %shard_map.106 = (f32[4,80,256]{2,1,0:T(8,128)S(1)}, f32[4,80,256]{2,1,0:T(8,128)S(1)}, f32[4,80,256]{2,1,0:T(8,128)S(1)}, f32[4,80,256]{2,1,0:T(8,128)S(1)}, f3...) custom-call(bf16[512,512]{1,0:T(8,128)(2,1)S(1)} %get-tuple-element.78.refs_0_, ...), custom_call_target="tpu_custom_call" | custom-call | flops 1006632960 | bytes 7340032 | tf_op jit(solution)/shard_map/pallas_call | solution.py:332
  55.0 0.7 collective-permute-start.20
  55.6 0.6 collective-permute-start.23
  56.3 4.9 %collective-permute-done.11.came = f32[4,96,256]{2,1,0:T(8,128)S(1)} collective-permute-done((f32[4,96,256]{2,1,0:T(8,128)S(1)}, f32[4,96,256]{2,1,0:T(8,128)S(1)}, u32[]{:S(2)}, u32[]{:S(2)}) %collective-permute-start.11) | collective-permute-done | bytes 393248 | tf_op jit(solution)/shard_map/ppermute | solution.py:424
  61.2 0.8 collective-permute-start.26
  62.0 3.1 %collective-permute-start.12 = (f32[2,96,256]{2,1,0:T(8,128)S(1)}, f32[2,96,256]{2,1,0:T(8,128)S(1)}, u32[]{:S(2)}, u32[]{:S(2)}) collective-permute-start(f32[2,96,256]{2,1,0:T(8,128)S(1)} %get-tuple-element.106), channel_id=1, source_target_pairs={{0,6},{6,0},{2,4},{4,2},{1,7},{7,1},{3,5},{5,3},{8,14},{14,8},{10,... | collective-permute-start | bytes 589832 | tf_op jit(solution)/shard_map/ppermute | solution.py:424
  65.1 0.3 collective-permute-start.18
  65.5 2.7 %collective-permute-done.20.came = f32[4,80,256]{2,1,0:T(8,128)S(1)} collective-permute-done((f32[4,80,256]{2,1,0:T(8,128)S(1)}, f32[4,80,256]{2,1,0:T(8,128)S(1)}, u32[]{:S(2)}, u32[]{:S(2)}) %collective-permute-start.20) | collective-permute-done | bytes 327712 | tf_op jit(solution)/shard_map/ppermute | solution.py:424
  68.2 0.8 collective-permute-start.15
  69.0 2.6 %collective-permute-done.23.came = f32[4,80,256]{2,1,0:T(8,128)S(1)} collective-permute-done((f32[4,80,256]{2,1,0:T(8,128)S(1)}, f32[4,80,256]{2,1,0:T(8,128)S(1)}, u32[]{:S(2)}, u32[]{:S(2)}) %collective-permute-start.23) | collective-permute-done | bytes 327712 | tf_op jit(solution)/shard_map/ppermute | solution.py:424
  71.7 2.1 %collective-permute-start.21 = (f32[2,80,256]{2,1,0:T(8,128)S(1)}, f32[2,80,256]{2,1,0:T(8,128)S(1)}, u32[]{:S(2)}, u32[]{:S(2)}) collective-permute-start(f32[2,80,256]{2,1,0:T(8,128)S(1)} %get-tuple-element.124), channel_id=1, source_target_pairs={{0,6},{6,0},{2,4},{4,2},{1,7},{7,1},{3,5},{5,3},{8,14},{14,8},{10,... | collective-permute-start | bytes 491528 | tf_op jit(solution)/shard_map/ppermute | solution.py:424
  73.8 1.3 %collective-permute-start.24 = (f32[2,80,256]{2,1,0:T(8,128)S(1)}, f32[2,80,256]{2,1,0:T(8,128)S(1)}, u32[]{:S(2)}, u32[]{:S(2)}) collective-permute-start(f32[2,80,256]{2,1,0:T(8,128)S(1)} %get-tuple-element.130), channel_id=1, source_target_pairs={{0,1},{1,0},{2,3},{3,2},{4,5},{5,4},{6,7},{7,6},{8,9},{9,8},{10,11... | collective-permute-start | bytes 491528 | tf_op jit(solution)/shard_map/ppermute | solution.py:424
  75.2 0.7 collective-permute-done.12.came
  75.9 1.4 %collective-permute-start.13 = (f32[1,96,256]{2,1,0:T(8,128)S(1)}, f32[1,96,256]{2,1,0:T(8,128)S(1)}, u32[]{:S(2)}, u32[]{:S(2)}) collective-permute-start(f32[1,96,256]{2,1,0:T(8,128)S(1)} %get-tuple-element.108), channel_id=1, source_target_pairs={{0,1},{1,0},{2,3},{3,2},{4,5},{5,4},{6,7},{7,6},{8,9},{9,8},{10,11... | collective-permute-start | bytes 294920 | tf_op jit(solution)/shard_map/ppermute | solution.py:424
  77.3 1.0 %collective-permute-done.21.came = f32[2,80,256]{2,1,0:T(8,128)S(1)} collective-permute-done((f32[2,80,256]{2,1,0:T(8,128)S(1)}, f32[2,80,256]{2,1,0:T(8,128)S(1)}, u32[]{:S(2)}, u32[]{:S(2)}) %collective-permute-start.21) | collective-permute-done | bytes 163872 | tf_op jit(solution)/shard_map/ppermute | solution.py:424
  78.3 2.1 %collective-permute-start.19 = (f32[1,80,256]{2,1,0:T(8,128)S(1)}, f32[1,80,256]{2,1,0:T(8,128)S(1)}, u32[]{:S(2)}, u32[]{:S(2)}) collective-permute-start(f32[1,80,256]{2,1,0:T(8,128)S(1)} %get-tuple-element.120), channel_id=1, source_target_pairs={{0,6},{6,0},{2,4},{4,2},{1,7},{7,1},{3,5},{5,3},{8,14},{14,8},{10,... | collective-permute-start | bytes 245768 | tf_op jit(solution)/shard_map/ppermute | solution.py:424
  80.5 1.3 %collective-permute-start.22 = (f32[1,80,256]{2,1,0:T(8,128)S(1)}, f32[1,80,256]{2,1,0:T(8,128)S(1)}, u32[]{:S(2)}, u32[]{:S(2)}) collective-permute-start(f32[1,80,256]{2,1,0:T(8,128)S(1)} %get-tuple-element.126), channel_id=1, source_target_pairs={{0,1},{1,0},{2,3},{3,2},{4,5},{5,4},{6,7},{7,6},{8,9},{9,8},{10,11... | collective-permute-start | bytes 245768 | tf_op jit(solution)/shard_map/ppermute | solution.py:424
  81.8 0.1 collective-permute-start.25
  82.0 1.5 %collective-permute-start.28 = (f32[1,80,256]{2,1,0:T(8,128)S(1)}, f32[1,80,256]{2,1,0:T(8,128)S(1)}, u32[]{:S(2)}, u32[]{:S(2)}) collective-permute-start(f32[1,80,256]{2,1,0:T(8,128)S(1)} %get-tuple-element.138), channel_id=1, source_target_pairs={{0,6},{6,0},{2,4},{4,2},{1,7},{7,1},{3,5},{5,3},{8,14},{14,8},{10,... | collective-permute-start | bytes 245768 | tf_op jit(solution)/shard_map/ppermute | solution.py:424
  83.5 1.5 %collective-permute-start.16 = (f32[1,96,256]{2,1,0:T(8,128)S(1)}, f32[1,96,256]{2,1,0:T(8,128)S(1)}, u32[]{:S(2)}, u32[]{:S(2)}) collective-permute-start(f32[1,96,256]{2,1,0:T(8,128)S(1)} %get-tuple-element.114), channel_id=1, source_target_pairs={{0,2},{2,0},{4,6},{6,4},{1,3},{3,1},{5,7},{7,5},{8,10},{10,8},{12,... | collective-permute-start | bytes 294920 | tf_op jit(solution)/shard_map/ppermute | solution.py:424
  85.0 3.2 %collective-permute-done.16 = f32[1,96,256]{2,1,0:T(8,128)S(1)} collective-permute-done((f32[1,96,256]{2,1,0:T(8,128)S(1)}, f32[1,96,256]{2,1,0:T(8,128)S(1)}, u32[]{:S(2)}, u32[]{:S(2)}) %collective-permute-start.16) | collective-permute-done | bytes 98336 | tf_op jit(solution)/shard_map/ppermute | solution.py:424
  88.3 0.7 copy-done.3
  89.0 0.6 fusion.11
  (46 shorter events, 0.8 us)
Async XLA Ops:
  0.0 39.8 %copy-start.1 = (bf16[2048,512]{1,0:T(8,128)(2,1)S(1)}, bf16[2048,512]{1,0:T(8,128)(2,1)}, u32[]{:S(2)}) copy-start(bf16[2048,512]{1,0:T(8,128)(2,1)} %refs_1_.3) | copy-start | bytes 6291460
  0.0 39.8 %copy-start.2 = (f32[8]{0:T(128)S(1)}, f32[8]{0:T(128)}, u32[]{:S(2)}) copy-start(f32[8]{0:T(128)} %refs_7_.3) | copy-start | bytes 100
  7.6 1.6 %collective-permute-start = (f32[136,512]{1,0:T(8,128)S(1)}, f32[136,512]{1,0:T(8,128)S(1)}, u32[]{:S(2)}, u32[]{:S(2)}) collective-permute-start(f32[136,512]{1,0:T(8,128)S(1)} %get-tuple-element.86), channel_id=1, source_target_pairs={{0,8},{8,0},{1,9},{9,1},{2,10},{10,2},{3,11},{11,3},{4,12},{12,4},... | collective-permute-start | bytes 835592 | tf_op jit(solution)/shard_map/ppermute | solution.py:374
  9.3 5.0 %collective-permute-start.1 = (f32[136,128]{1,0:T(8,128)S(1)}, f32[136,128]{1,0:T(8,128)S(1)}, u32[]{:S(2)}, u32[]{:S(2)}) collective-permute-start(f32[136,128]{1,0:T(8,128)S(1)} %get-tuple-element.88), channel_id=1, source_target_pairs={{0,16},{16,32},{32,48},{48,0},{1,17},{17,33},{33,49},{49,1},{2,18}... | collective-permute-start | bytes 208904 | tf_op jit(solution)/shard_map/ppermute | solution.py:345
  10.9 6.3 %collective-permute-start.2 = (f32[136,128]{1,0:T(8,128)S(1)}, f32[136,128]{1,0:T(8,128)S(1)}, u32[]{:S(2)}, u32[]{:S(2)}) collective-permute-start(f32[136,128]{1,0:T(8,128)S(1)} %get-tuple-element.89), channel_id=1, source_target_pairs={{0,32},{16,48},{32,0},{48,16},{1,33},{17,49},{33,1},{49,17},{2,34}... | collective-permute-start | bytes 208904 | tf_op jit(solution)/shard_map/ppermute | solution.py:345
  13.6 4.4 %collective-permute-start.3 = (f32[136,128]{1,0:T(8,128)S(1)}, f32[136,128]{1,0:T(8,128)S(1)}, u32[]{:S(2)}, u32[]{:S(2)}) collective-permute-start(f32[136,128]{1,0:T(8,128)S(1)} %get-tuple-element.90), channel_id=1, source_target_pairs={{0,48},{16,0},{32,16},{48,32},{1,49},{17,1},{33,17},{49,33},{2,50}... | collective-permute-start | bytes 208904 | tf_op jit(solution)/shard_map/ppermute | solution.py:345
  18.1 10.6 %collective-permute-start.4 = (f32[72,128]{1,0:T(8,128)S(1)}, f32[72,128]{1,0:T(8,128)S(1)}, u32[]{:S(2)}, u32[]{:S(2)}) collective-permute-start(f32[72,128]{1,0:T(8,128)S(1)} %get-tuple-element.92), channel_id=1, source_target_pairs={{0,64},{64,128},{128,192},{192,0},{1,65},{65,129},{129,193},{193,1... | collective-permute-start | bytes 110600 | tf_op jit(solution)/shard_map/ppermute | solution.py:345
  20.6 8.0 %collective-permute-start.5 = (f32[72,128]{1,0:T(8,128)S(1)}, f32[72,128]{1,0:T(8,128)S(1)}, u32[]{:S(2)}, u32[]{:S(2)}) collective-permute-start(f32[72,128]{1,0:T(8,128)S(1)} %get-tuple-element.93), channel_id=1, source_target_pairs={{0,128},{64,192},{128,0},{192,64},{1,129},{65,193},{129,1},{193,65... | collective-permute-start | bytes 110600 | tf_op jit(solution)/shard_map/ppermute | solution.py:345
  26.0 4.9 %collective-permute-start.6 = (f32[72,128]{1,0:T(8,128)S(1)}, f32[72,128]{1,0:T(8,128)S(1)}, u32[]{:S(2)}, u32[]{:S(2)}) collective-permute-start(f32[72,128]{1,0:T(8,128)S(1)} %get-tuple-element.94), channel_id=1, source_target_pairs={{0,192},{64,0},{128,64},{192,128},{1,193},{65,1},{129,65},{193,129... | collective-permute-start | bytes 110600 | tf_op jit(solution)/shard_map/ppermute | solution.py:345
  31.0 5.5 %collective-permute-start.7 = (f32[128,128]{1,0:T(8,128)S(1)}, f32[128,128]{1,0:T(8,128)S(1)}, u32[]{:S(2)}, u32[]{:S(2)}) collective-permute-start(f32[128,128]{1,0:T(8,128)S(1)} %get-tuple-element.96), channel_id=1, source_target_pairs={{0,16},{16,32},{32,48},{48,0},{1,17},{17,33},{33,49},{49,1},{2,18}... | collective-permute-start | bytes 196616 | tf_op jit(solution)/shard_map/ppermute | solution.py:345
  32.4 5.8 %collective-permute-start.8 = (f32[128,128]{1,0:T(8,128)S(1)}, f32[128,128]{1,0:T(8,128)S(1)}, u32[]{:S(2)}, u32[]{:S(2)}) collective-permute-start(f32[128,128]{1,0:T(8,128)S(1)} %get-tuple-element.97), channel_id=1, source_target_pairs={{0,32},{16,48},{32,0},{48,16},{1,33},{17,49},{33,1},{49,17},{2,34}... | collective-permute-start | bytes 196616 | tf_op jit(solution)/shard_map/ppermute | solution.py:345
  35.2 4.3 %collective-permute-start.9 = (f32[128,128]{1,0:T(8,128)S(1)}, f32[128,128]{1,0:T(8,128)S(1)}, u32[]{:S(2)}, u32[]{:S(2)}) collective-permute-start(f32[128,128]{1,0:T(8,128)S(1)} %get-tuple-element.98), channel_id=1, source_target_pairs={{0,48},{16,0},{32,16},{48,32},{1,49},{17,1},{33,17},{49,33},{2,50}... | collective-permute-start | bytes 196616 | tf_op jit(solution)/shard_map/ppermute | solution.py:345
  39.5 8.0 %collective-permute-start.10 = (f32[128,512]{1,0:T(8,128)S(1)}, f32[128,512]{1,0:T(8,128)S(1)}, u32[]{:S(2)}, u32[]{:S(2)}) collective-permute-start(f32[128,512]{1,0:T(8,128)S(1)} %get-tuple-element.100), channel_id=1, source_target_pairs={{0,8},{8,0},{1,9},{9,1},{2,10},{10,2},{3,11},{11,3},{4,12},{12,4},... | collective-permute-start | bytes 786440 | tf_op jit(solution)/shard_map/ppermute | solution.py:406
  39.8 3.4 %copy-start = (bf16[512,2048]{1,0:T(8,128)(2,1)S(1)}, bf16[512,2048]{1,0:T(8,128)(2,1)}, u32[]{:S(2)}) copy-start(bf16[512,2048]{1,0:T(8,128)(2,1)} %out_w.1) | copy-start | bytes 6291460
  49.1 12.1 %collective-permute-start.11 = (f32[4,96,256]{2,1,0:T(8,128)S(1)}, f32[4,96,256]{2,1,0:T(8,128)S(1)}, u32[]{:S(2)}, u32[]{:S(2)}) collective-permute-start(f32[4,96,256]{2,1,0:T(8,128)S(1)} %get-tuple-element.104), channel_id=1, source_target_pairs={{0,2},{2,0},{4,6},{6,4},{1,3},{3,1},{5,7},{7,5},{8,10},{10,8},{12,... | collective-permute-start | bytes 1179656 | tf_op jit(solution)/shard_map/ppermute | solution.py:424
  50.7 11.3 %collective-permute-start.17 = (f32[4,80,256]{2,1,0:T(8,128)S(1)}, f32[4,80,256]{2,1,0:T(8,128)S(1)}, u32[]{:S(2)}, u32[]{:S(2)}) collective-permute-start(f32[4,80,256]{2,1,0:T(8,128)S(1)} %get-tuple-element.116), channel_id=1, source_target_pairs={{0,1},{1,0},{2,3},{3,2},{4,5},{5,4},{6,7},{7,6},{8,9},{9,8},{10,11... | collective-permute-start | bytes 983048 | tf_op jit(solution)/shard_map/ppermute | solution.py:424
  51.4 13.7 %collective-permute-start.14 = (f32[4,96,256]{2,1,0:T(8,128)S(1)}, f32[4,96,256]{2,1,0:T(8,128)S(1)}, u32[]{:S(2)}, u32[]{:S(2)}) collective-permute-start(f32[4,96,256]{2,1,0:T(8,128)S(1)} %get-tuple-element.110), channel_id=1, source_target_pairs={{0,6},{6,0},{2,4},{4,2},{1,7},{7,1},{3,5},{5,3},{8,14},{14,8},{10,... | collective-permute-start | bytes 1179656 | tf_op jit(solution)/shard_map/ppermute | solution.py:424
  55.0 13.2 %collective-permute-start.20 = (f32[4,80,256]{2,1,0:T(8,128)S(1)}, f32[4,80,256]{2,1,0:T(8,128)S(1)}, u32[]{:S(2)}, u32[]{:S(2)}) collective-permute-start(f32[4,80,256]{2,1,0:T(8,128)S(1)} %get-tuple-element.122), channel_id=1, source_target_pairs={{0,2},{2,0},{4,6},{6,4},{1,3},{3,1},{5,7},{7,5},{8,10},{10,8},{12,... | collective-permute-start | bytes 983048 | tf_op jit(solution)/shard_map/ppermute | solution.py:424
  55.6 16.0 %collective-permute-start.23 = (f32[4,80,256]{2,1,0:T(8,128)S(1)}, f32[4,80,256]{2,1,0:T(8,128)S(1)}, u32[]{:S(2)}, u32[]{:S(2)}) collective-permute-start(f32[4,80,256]{2,1,0:T(8,128)S(1)} %get-tuple-element.128), channel_id=1, source_target_pairs={{0,6},{6,0},{2,4},{4,2},{1,7},{7,1},{3,5},{5,3},{8,14},{14,8},{10,... | collective-permute-start | bytes 983048 | tf_op jit(solution)/shard_map/ppermute | solution.py:424
  61.2 12.6 %collective-permute-start.26 = (f32[4,80,256]{2,1,0:T(8,128)S(1)}, f32[4,80,256]{2,1,0:T(8,128)S(1)}, u32[]{:S(2)}, u32[]{:S(2)}) collective-permute-start(f32[4,80,256]{2,1,0:T(8,128)S(1)} %get-tuple-element.134), channel_id=1, source_target_pairs={{0,1},{1,0},{2,3},{3,2},{4,5},{5,4},{6,7},{7,6},{8,9},{9,8},{10,11... | collective-permute-start | bytes 983048 | tf_op jit(solution)/shard_map/ppermute | solution.py:424
  62.0 13.9 %collective-permute-start.12 = (f32[2,96,256]{2,1,0:T(8,128)S(1)}, f32[2,96,256]{2,1,0:T(8,128)S(1)}, u32[]{:S(2)}, u32[]{:S(2)}) collective-permute-start(f32[2,96,256]{2,1,0:T(8,128)S(1)} %get-tuple-element.106), channel_id=1, source_target_pairs={{0,6},{6,0},{2,4},{4,2},{1,7},{7,1},{3,5},{5,3},{8,14},{14,8},{10,... | collective-permute-start | bytes 589832 | tf_op jit(solution)/shard_map/ppermute | solution.py:424
  65.1 10.8 %collective-permute-start.18 = (f32[2,80,256]{2,1,0:T(8,128)S(1)}, f32[2,80,256]{2,1,0:T(8,128)S(1)}, u32[]{:S(2)}, u32[]{:S(2)}) collective-permute-start(f32[2,80,256]{2,1,0:T(8,128)S(1)} %get-tuple-element.118), channel_id=1, source_target_pairs={{0,2},{2,0},{4,6},{6,4},{1,3},{3,1},{5,7},{7,5},{8,10},{10,8},{12,... | collective-permute-start | bytes 491528 | tf_op jit(solution)/shard_map/ppermute | solution.py:424
  68.2 13.8 %collective-permute-start.15 = (f32[2,96,256]{2,1,0:T(8,128)S(1)}, f32[2,96,256]{2,1,0:T(8,128)S(1)}, u32[]{:S(2)}, u32[]{:S(2)}) collective-permute-start(f32[2,96,256]{2,1,0:T(8,128)S(1)} %get-tuple-element.112), channel_id=1, source_target_pairs={{0,1},{1,0},{2,3},{3,2},{4,5},{5,4},{6,7},{7,6},{8,9},{9,8},{10,11... | collective-permute-start | bytes 589832 | tf_op jit(solution)/shard_map/ppermute | solution.py:424
  71.7 6.7 %collective-permute-start.21 = (f32[2,80,256]{2,1,0:T(8,128)S(1)}, f32[2,80,256]{2,1,0:T(8,128)S(1)}, u32[]{:S(2)}, u32[]{:S(2)}) collective-permute-start(f32[2,80,256]{2,1,0:T(8,128)S(1)} %get-tuple-element.124), channel_id=1, source_target_pairs={{0,6},{6,0},{2,4},{4,2},{1,7},{7,1},{3,5},{5,3},{8,14},{14,8},{10,... | collective-permute-start | bytes 491528 | tf_op jit(solution)/shard_map/ppermute | solution.py:424
  73.8 6.6 %collective-permute-start.24 = (f32[2,80,256]{2,1,0:T(8,128)S(1)}, f32[2,80,256]{2,1,0:T(8,128)S(1)}, u32[]{:S(2)}, u32[]{:S(2)}) collective-permute-start(f32[2,80,256]{2,1,0:T(8,128)S(1)} %get-tuple-element.130), channel_id=1, source_target_pairs={{0,1},{1,0},{2,3},{3,2},{4,5},{5,4},{6,7},{7,6},{8,9},{9,8},{10,11... | collective-permute-start | bytes 491528 | tf_op jit(solution)/shard_map/ppermute | solution.py:424
  75.9 5.9 %collective-permute-start.27 = (f32[2,80,256]{2,1,0:T(8,128)S(1)}, f32[2,80,256]{2,1,0:T(8,128)S(1)}, u32[]{:S(2)}, u32[]{:S(2)}) collective-permute-start(f32[2,80,256]{2,1,0:T(8,128)S(1)} %get-tuple-element.136), channel_id=1, source_target_pairs={{0,2},{2,0},{4,6},{6,4},{1,3},{3,1},{5,7},{7,5},{8,10},{10,8},{12,... | collective-permute-start | bytes 491528 | tf_op jit(solution)/shard_map/ppermute | solution.py:424
  75.9 7.5 %collective-permute-start.13 = (f32[1,96,256]{2,1,0:T(8,128)S(1)}, f32[1,96,256]{2,1,0:T(8,128)S(1)}, u32[]{:S(2)}, u32[]{:S(2)}) collective-permute-start(f32[1,96,256]{2,1,0:T(8,128)S(1)} %get-tuple-element.108), channel_id=1, source_target_pairs={{0,1},{1,0},{2,3},{3,2},{4,5},{5,4},{6,7},{7,6},{8,9},{9,8},{10,11... | collective-permute-start | bytes 294920 | tf_op jit(solution)/shard_map/ppermute | solution.py:424
  78.3 9.8 %collective-permute-start.19 = (f32[1,80,256]{2,1,0:T(8,128)S(1)}, f32[1,80,256]{2,1,0:T(8,128)S(1)}, u32[]{:S(2)}, u32[]{:S(2)}) collective-permute-start(f32[1,80,256]{2,1,0:T(8,128)S(1)} %get-tuple-element.120), channel_id=1, source_target_pairs={{0,6},{6,0},{2,4},{4,2},{1,7},{7,1},{3,5},{5,3},{8,14},{14,8},{10,... | collective-permute-start | bytes 245768 | tf_op jit(solution)/shard_map/ppermute | solution.py:424
  80.5 7.7 %collective-permute-start.22 = (f32[1,80,256]{2,1,0:T(8,128)S(1)}, f32[1,80,256]{2,1,0:T(8,128)S(1)}, u32[]{:S(2)}, u32[]{:S(2)}) collective-permute-start(f32[1,80,256]{2,1,0:T(8,128)S(1)} %get-tuple-element.126), channel_id=1, source_target_pairs={{0,1},{1,0},{2,3},{3,2},{4,5},{5,4},{6,7},{7,6},{8,9},{9,8},{10,11... | collective-permute-start | bytes 245768 | tf_op jit(solution)/shard_map/ppermute | solution.py:424
  81.8 6.4 %collective-permute-start.25 = (f32[1,80,256]{2,1,0:T(8,128)S(1)}, f32[1,80,256]{2,1,0:T(8,128)S(1)}, u32[]{:S(2)}, u32[]{:S(2)}) collective-permute-start(f32[1,80,256]{2,1,0:T(8,128)S(1)} %get-tuple-element.132), channel_id=1, source_target_pairs={{0,2},{2,0},{4,6},{6,4},{1,3},{3,1},{5,7},{7,5},{8,10},{10,8},{12,... | collective-permute-start | bytes 245768 | tf_op jit(solution)/shard_map/ppermute | solution.py:424
  82.0 6.3 %collective-permute-start.28 = (f32[1,80,256]{2,1,0:T(8,128)S(1)}, f32[1,80,256]{2,1,0:T(8,128)S(1)}, u32[]{:S(2)}, u32[]{:S(2)}) collective-permute-start(f32[1,80,256]{2,1,0:T(8,128)S(1)} %get-tuple-element.138), channel_id=1, source_target_pairs={{0,6},{6,0},{2,4},{4,2},{1,7},{7,1},{3,5},{5,3},{8,14},{14,8},{10,... | collective-permute-start | bytes 245768 | tf_op jit(solution)/shard_map/ppermute | solution.py:424
  83.5 4.7 %collective-permute-start.16 = (f32[1,96,256]{2,1,0:T(8,128)S(1)}, f32[1,96,256]{2,1,0:T(8,128)S(1)}, u32[]{:S(2)}, u32[]{:S(2)}) collective-permute-start(f32[1,96,256]{2,1,0:T(8,128)S(1)} %get-tuple-element.114), channel_id=1, source_target_pairs={{0,2},{2,0},{4,6},{6,4},{1,3},{3,1},{5,7},{7,5},{8,10},{10,8},{12,... | collective-permute-start | bytes 294920 | tf_op jit(solution)/shard_map/ppermute | solution.py:424
  88.3 0.7 copy-start.3

commit v2 on v1

--- a/solution.py
+++ b/solution.py
@@ -313,6 +313,25 @@
     sent_out[...] = kept[half:] + came[half:]
 
 
+def join_kernel(kept_a, came_a, kept_b, came_b, kept, sent):
+    split = kept_a.shape[1]
+    for rows, mine, came in ((slice(0, split), kept_a, came_a), (slice(split, None), kept_b, came_b)):
+        kept[rows, :] = mine[0] + came[0]
+        sent[rows, :] = mine[1] + came[1]
+
+
+def finish_kernel(counts, *refs):
+    out = refs[-1]
+    start = 0
+    for group in range(2):
+        for p in range(3):
+            lo = counts[0][p] * group
+            rows = slice(lo, lo + counts[group][p])
+            value = refs[p][rows, :] + refs[3 + p][rows, :]
+            out[start : start + counts[group][p], :] = value.astype(BF16)
+            start += counts[group][p]
+
+
 VMEM_SPEC = pl.BlockSpec(memory_space=pltpu.VMEM)
 SMEM_SPEC = pl.BlockSpec(memory_space=pltpu.SMEM)
 HBM_SPEC = pl.BlockSpec(memory_space=pltpu.HBM)
@@ -405,36 +424,44 @@
                        scratch=[pltpu.VMEM((size, inner), F32)])
     arrived = lax.ppermute(give, "core", swap)
 
-    whole, first_row, parts = [], 0, []
-    for group, counts in enumerate(((96, 96, 80), (80, 80, 80))):
+    first_row, parts = 0, []
+    counts = ((112, 112, 96), (64, 64, 64))
+    for group in range(2):
         outs = call(
             lambda *refs, at=first_row: output_kernel(at, *refs),
             (base_f, base_b, slope_f, slope_b, proj_f, proj_b, carry, arrived, plain, flipped),
-            [near((4, r, width // 8)) for r in counts] * 2,
-            flops=4 * sum(counts) * inner * width,
+            [near((4, r, width // 8)) for r in counts[group]] * 2,
+            flops=4 * sum(counts[group]) * inner * width,
         )
-        first_row += sum(counts)
+        first_row += sum(counts[group])
         parts.append([outs[:3], outs[3:]])
-    for step in range(3):
-        for group in range(2):
-            kept, sent = parts[group]
-            came = []
-            for p in range(3):
-                axis, pairs = FLIPS[(p + step) % 3]
-                came.append(lax.ppermute(sent[p], axis, pairs))
-            if step == 2:
-                whole += [(a + b)[0] for a, b in zip(kept, came)]
-            else:
-                n = 2 - step
-                sums = [
-                    call(
-                        sum_kernel, (kept[p], came[p]),
-                        [near((n, *came[p].shape[1:]))] * 2,
-                    )
-                    for p in range(3)
-                ]
-                parts[group] = [[a for a, _ in sums], [b for _, b in sums]]
-    return jnp.concatenate(whole, axis=0).astype(BF16)
+
+    def travel(step, p, value):
+        axis, pairs = FLIPS[(p + step) % 3]
+        return lax.ppermute(value, axis, pairs)
+
+    for group in range(2):
+        kept, sent = parts[group]
+        came = [travel(0, p, sent[p]) for p in range(3)]
+        sums = [
+            call(
+                sum_kernel, (kept[p], came[p]),
+                [near((2, *came[p].shape[1:]))] * 2,
+            )
+            for p in range(3)
+        ]
+        parts[group] = [[a, travel(1, p, b)] for p, (a, b) in enumerate(sums)]
+    last = [
+        call(join_kernel, (*parts[0][p], *parts[1][p]),
+             [near((counts[0][p] + counts[1][p], width // 8))] * 2)
+        for p in range(3)
+    ]
+    came = [travel(2, p, last[p][1]) for p in range(3)]
+    (encoded,) = call(
+        lambda *refs: finish_kernel(counts, *refs), (*(a for a, _ in last), *came),
+        [jax.ShapeDtypeStruct((rows, width // 8), BF16)],
+    )
+    return encoded
 
 
 def solution(mesh):

time: 91.4 us -> 94.1 us (1.030); the launches traced: 89.6 us -> 94 us
  waiting for transfers between devices: 25.6 us -> 33.2 us
  starting transfers between devices: 43.5 us -> 40.9 us
    ppermute x18 -> x15, waiting for transfers between devices: 15.1 us -> 22.8 us  [travel(): return lax.ppermute(value, axis, pairs)]
    ppermute x18 -> x15, starting transfers between devices: 22.1 us -> 19.4 us  [travel(): return lax.ppermute(value, axis, pairs)]
    pallas_call x22 -> x20, Pallas kernels: 18.8 us -> 19.6 us  [call(): pl.pallas_call(kernel, out_shape=outs, in_specs=specs, out_specs=[VMEM_SP...]
  transfers between devices with their start and end apart: 29 -> 26, of which waited for: 12 -> 11; matrix products, arithmetic and copies ran while one was open for 0% -> 0% of each run, Pallas kernels for 10% -> 10%
where the time goes in v2:
time: 94.1 us; the launch traced here: 94 us
  starting transfers between devices  40.9 us (43%)
  waiting for transfers between devices  33.2 us (35%)
  Pallas kernels  19.6 us (21%)
    ppermute x15, waiting for transfers between devices, travel(): return lax.ppermute(value, axis, pairs)  22.8 us
    ppermute x9, starting transfers between devices, shifted(): lax.ppermute(v, axis, [(j, (j + k) % 4) for j in range(4)])  21.1 us
    pallas_call x20, Pallas kernels, call(): pl.pallas_call(kernel, out_shape=outs, in_specs=specs, out_specs=[VMEM_SP...  19.6 us
    ppermute x15, starting transfers between devices, travel(): return lax.ppermute(value, axis, pairs)  19.4 us
    ppermute x9, waiting for transfers between devices, shifted(): lax.ppermute(v, axis, [(j, (j + k) % 4) for j in range(4)])  8.86 us
  transfers between devices with their start and end apart: 26, of which 11 were waited for; matrix products, arithmetic and copies ran while one was open for 0% of the time, Pallas kernels for 10%

profile of v2, /device:TPU:8, one launch (start us, length us, event | category | flops | bytes accessed | tf_op | source)
XLA Modules:
  0.0 94.0 jit_solution(9128377182815482324)
XLA Ops:
  0.0 7.5 %shard_map.91 = (bf16[512,2048]{1,0:T(8,128)(2,1)S(1)}, bf16[512,2048]{1,0:T(8,128)(2,1)S(1)}, bf16[512,512]{1,0:T(8,128)(2,1)S(1)}, bf16[512,512]{1,0:T(8,128)(...) custom-call(bf16[512,2048]{1,0:T(8,128)(2,1)} %seq_hbm.1, ...), custom_call_target="tpu_custom_call" | custom-call | flops 3221225472 | bytes 5275712 | tf_op jit(solution)/shard_map/pallas_call | solution.py:351
  7.6 0.1 collective-permute-start
  7.7 1.5 %collective-permute-done.got.other = f32[136,512]{1,0:T(8,128)S(1)} collective-permute-done((f32[136,512]{1,0:T(8,128)S(1)}, f32[136,512]{1,0:T(8,128)S(1)}, u32[]{:S(2)}, u32[]{:S(2)}) %collective-permute-start) | collective-permute-done | bytes 278560 | tf_op jit(solution)/shard_map/ppermute | solution.py:393
  9.2 0.1 shard_map.94
  9.3 1.7 %collective-permute-start.1 = (f32[136,128]{1,0:T(8,128)S(1)}, f32[136,128]{1,0:T(8,128)S(1)}, u32[]{:S(2)}, u32[]{:S(2)}) collective-permute-start(f32[136,128]{1,0:T(8,128)S(1)} %get-tuple-element.82), channel_id=1, source_target_pairs={{0,16},{16,32},{32,48},{48,0},{1,17},{17,33},{33,49},{49,1},{2,18}... | collective-permute-start | bytes 208904 | tf_op jit(solution)/shard_map/ppermute | solution.py:364
  10.9 2.6 %collective-permute-start.2 = (f32[136,128]{1,0:T(8,128)S(1)}, f32[136,128]{1,0:T(8,128)S(1)}, u32[]{:S(2)}, u32[]{:S(2)}) collective-permute-start(f32[136,128]{1,0:T(8,128)S(1)} %get-tuple-element.83), channel_id=1, source_target_pairs={{0,32},{16,48},{32,0},{48,16},{1,33},{17,49},{33,1},{49,17},{2,34}... | collective-permute-start | bytes 208904 | tf_op jit(solution)/shard_map/ppermute | solution.py:364
  13.6 0.7 collective-permute-start.3
  14.3 2.9 %collective-permute-done.2.got2 = f32[136,128]{1,0:T(8,128)S(1)} collective-permute-done((f32[136,128]{1,0:T(8,128)S(1)}, f32[136,128]{1,0:T(8,128)S(1)}, u32[]{:S(2)}, u32[]{:S(2)}) %collective-permute-start.2) | collective-permute-done | bytes 69664 | tf_op jit(solution)/shard_map/ppermute | solution.py:364
  17.2 0.8 collective-permute-done.3.got3
  18.0 0.1 shard_map.95
  18.1 2.6 %collective-permute-start.4 = (f32[72,128]{1,0:T(8,128)S(1)}, f32[72,128]{1,0:T(8,128)S(1)}, u32[]{:S(2)}, u32[]{:S(2)}) collective-permute-start(f32[72,128]{1,0:T(8,128)S(1)} %get-tuple-element.86), channel_id=1, source_target_pairs={{0,64},{64,128},{128,192},{192,0},{1,65},{65,129},{129,193},{193,1... | collective-permute-start | bytes 110600 | tf_op jit(solution)/shard_map/ppermute | solution.py:364
  20.6 5.4 %collective-permute-start.5 = (f32[72,128]{1,0:T(8,128)S(1)}, f32[72,128]{1,0:T(8,128)S(1)}, u32[]{:S(2)}, u32[]{:S(2)}) collective-permute-start(f32[72,128]{1,0:T(8,128)S(1)} %get-tuple-element.87), channel_id=1, source_target_pairs={{0,128},{64,192},{128,0},{192,64},{1,129},{65,193},{129,1},{193,65... | collective-permute-start | bytes 110600 | tf_op jit(solution)/shard_map/ppermute | solution.py:364
  26.0 2.7 %collective-permute-start.6 = (f32[72,128]{1,0:T(8,128)S(1)}, f32[72,128]{1,0:T(8,128)S(1)}, u32[]{:S(2)}, u32[]{:S(2)}) collective-permute-start(f32[72,128]{1,0:T(8,128)S(1)} %get-tuple-element.88), channel_id=1, source_target_pairs={{0,192},{64,0},{128,64},{192,128},{1,193},{65,1},{129,65},{193,129... | collective-permute-start | bytes 110600 | tf_op jit(solution)/shard_map/ppermute | solution.py:364
  28.7 2.2 %collective-permute-done.6.got3 = f32[72,128]{1,0:T(8,128)S(1)} collective-permute-done((f32[72,128]{1,0:T(8,128)S(1)}, f32[72,128]{1,0:T(8,128)S(1)}, u32[]{:S(2)}, u32[]{:S(2)}) %collective-permute-start.6) | collective-permute-done | bytes 36896 | tf_op jit(solution)/shard_map/ppermute | solution.py:364
  30.9 0.1 shard_map.96
  31.0 1.5 %collective-permute-start.7 = (f32[128,128]{1,0:T(8,128)S(1)}, f32[128,128]{1,0:T(8,128)S(1)}, u32[]{:S(2)}, u32[]{:S(2)}) collective-permute-start(f32[128,128]{1,0:T(8,128)S(1)} %get-tuple-element.90), channel_id=1, source_target_pairs={{0,16},{16,32},{32,48},{48,0},{1,17},{17,33},{33,49},{49,1},{2,18}... | collective-permute-start | bytes 196616 | tf_op jit(solution)/shard_map/ppermute | solution.py:364
  32.4 2.7 %collective-permute-start.8 = (f32[128,128]{1,0:T(8,128)S(1)}, f32[128,128]{1,0:T(8,128)S(1)}, u32[]{:S(2)}, u32[]{:S(2)}) collective-permute-start(f32[128,128]{1,0:T(8,128)S(1)} %get-tuple-element.91), channel_id=1, source_target_pairs={{0,32},{16,48},{32,0},{48,16},{1,33},{17,49},{33,1},{49,17},{2,34}... | collective-permute-start | bytes 196616 | tf_op jit(solution)/shard_map/ppermute | solution.py:364
  35.2 1.3 %collective-permute-start.9 = (f32[128,128]{1,0:T(8,128)S(1)}, f32[128,128]{1,0:T(8,128)S(1)}, u32[]{:S(2)}, u32[]{:S(2)}) collective-permute-start(f32[128,128]{1,0:T(8,128)S(1)} %get-tuple-element.92), channel_id=1, source_target_pairs={{0,48},{16,0},{32,16},{48,32},{1,49},{17,1},{33,17},{49,33},{2,50}... | collective-permute-start | bytes 196616 | tf_op jit(solution)/shard_map/ppermute | solution.py:364
  36.5 1.7 %collective-permute-done.8.got2 = f32[128,128]{1,0:T(8,128)S(1)} collective-permute-done((f32[128,128]{1,0:T(8,128)S(1)}, f32[128,128]{1,0:T(8,128)S(1)}, u32[]{:S(2)}, u32[]{:S(2)}) %collective-permute-start.8) | collective-permute-done | bytes 65568 | tf_op jit(solution)/shard_map/ppermute | solution.py:364
  38.2 1.2 %collective-permute-done.9.got3 = f32[128,128]{1,0:T(8,128)S(1)} collective-permute-done((f32[128,128]{1,0:T(8,128)S(1)}, f32[128,128]{1,0:T(8,128)S(1)}, u32[]{:S(2)}, u32[]{:S(2)}) %collective-permute-start.9) | collective-permute-done | bytes 65568 | tf_op jit(solution)/shard_map/ppermute | solution.py:364
  39.4 0.1 shard_map.97
  39.5 0.3 collective-permute-start.10
  39.9 3.3 %shard_map.92 = (bf16[512,512]{1,0:T(8,128)(2,1)S(1)}, bf16[512,512]{1,0:T(8,128)(2,1)S(1)}) custom-call(bf16[512,2048]{1,0:T(8,128)(2,1)S(1)} %get-tuple-element.66.refs_0_, bf16[2048,512]{1,0:T(8,128)(2,1)S(1)} %copy-done.1, bf16[512,512]{1,0:T(8,128)(2,1)S(1)} %get-tuple-element.67.refs_2_, bf16[512,256]{1,0:T(8,128)(2,1)S(1)} %get-tuple-element.68.refs_3_.refs_4_, ...), custom_call_target="tpu_custom_call" | custom-call | flops 2147483648 | bytes 5308448 | tf_op jit(solution)/shard_map/pallas_call | solution.py:351
  43.2 0.7 shard_map.98
  44.0 3.6 %shard_map.93 = (bf16[512,512]{1,0:T(8,128)(2,1)S(1)}, bf16[512,512]{1,0:T(8,128)(2,1)S(1)}) custom-call(bf16[512,2048]{1,0:T(8,128)(2,1)S(1)} %get-tuple-element.73.refs_0_, bf16[2048,512]{1,0:T(8,128)(2,1)S(1)} %copy-done.1, bf16[512,512]{1,0:T(8,128)(2,1)S(1)} %get-tuple-element.74.refs_2_, bf16[512,256]{1,0:T(8,128)(2,1)S(1)} %get-tuple-element.75.refs_3_.refs_5_, ...), custom_call_target="tpu_custom_call" | custom-call | flops 2147483648 | bytes 5308448 | tf_op jit(solution)/shard_map/pallas_call | solution.py:351
  47.5 1.8 %shard_map.99 = (f32[4,112,256]{2,1,0:T(8,128)S(1)}, f32[4,112,256]{2,1,0:T(8,128)S(1)}, f32[4,96,256]{2,1,0:T(8,128)S(1)}, f32[4,112,256]{2,1,0:T(8,128)S(1)}, ...) custom-call(bf16[512,512]{1,0:T(8,128)(2,1)S(1)} %get-tuple-element.72.refs_0_, ...), custom_call_target="tpu_custom_call" | custom-call | flops 1342177280 | bytes 7340032 | tf_op jit(solution)/shard_map/pallas_call | solution.py:351
  49.3 1.7 %collective-permute-start.11 = (f32[4,112,256]{2,1,0:T(8,128)S(1)}, f32[4,112,256]{2,1,0:T(8,128)S(1)}, u32[]{:S(2)}, u32[]{:S(2)}) collective-permute-start(f32[4,112,256]{2,1,0:T(8,128)S(1)} %get-tuple-element.98), channel_id=1, source_target_pairs={{0,2},{2,0},{4,6},{6,4},{1,3},{3,1},{5,7},{7,5},{8,10},{10,8},{12,... | collective-permute-start | bytes 1376264 | tf_op jit(solution)/shard_map/ppermute | solution.py:441
  51.0 2.0 %collective-permute-start.15 = (f32[4,112,256]{2,1,0:T(8,128)S(1)}, f32[4,112,256]{2,1,0:T(8,128)S(1)}, u32[]{:S(2)}, u32[]{:S(2)}) collective-permute-start(f32[4,112,256]{2,1,0:T(8,128)S(1)} %get-tuple-element.107), channel_id=1, source_target_pairs={{0,6},{6,0},{2,4},{4,2},{1,7},{7,1},{3,5},{5,3},{8,14},{14,8},{10,... | collective-permute-start | bytes 1376264 | tf_op jit(solution)/shard_map/ppermute | solution.py:441
  53.0 1.2 %shard_map.101 = (f32[4,64,256]{2,1,0:T(8,128)S(1)}, f32[4,64,256]{2,1,0:T(8,128)S(1)}, f32[4,64,256]{2,1,0:T(8,128)S(1)}, f32[4,64,256]{2,1,0:T(8,128)S(1)}, f3...) custom-call(bf16[512,512]{1,0:T(8,128)(2,1)S(1)} %get-tuple-element.72.refs_0_, ...), custom_call_target="tpu_custom_call" | custom-call | flops 805306368 | bytes 7340032 | tf_op jit(solution)/shard_map/pallas_call | solution.py:351
  54.2 0.8 collective-permute-start.13
  54.9 0.7 collective-permute-start.19
  55.6 0.7 collective-permute-start.17
  56.3 11.6 %collective-permute-done.13.came = f32[4,64,256]{2,1,0:T(8,128)S(1)} collective-permute-done((f32[4,64,256]{2,1,0:T(8,128)S(1)}, f32[4,64,256]{2,1,0:T(8,128)S(1)}, u32[]{:S(2)}, u32[]{:S(2)}) %collective-permute-start.13) | collective-permute-done | bytes 262176 | tf_op jit(solution)/shard_map/ppermute | solution.py:441
  67.9 0.8 collective-permute-start.21
  68.7 3.1 %collective-permute-start.14 = (f32[2,64,256]{2,1,0:T(8,128)S(1)}, f32[2,64,256]{2,1,0:T(8,128)S(1)}, u32[]{:S(2)}, u32[]{:S(2)}) collective-permute-start(f32[2,64,256]{2,1,0:T(8,128)S(1)} %get-tuple-element.104), channel_id=1, source_target_pairs={{0,6},{6,0},{2,4},{4,2},{1,7},{7,1},{3,5},{5,3},{8,14},{14,8},{10,... | collective-permute-start | bytes 393224 | tf_op jit(solution)/shard_map/ppermute | solution.py:441
  71.9 0.6 collective-permute-start.12
  72.5 1.3 %collective-permute-start.16 = (f32[2,112,256]{2,1,0:T(8,128)S(1)}, f32[2,112,256]{2,1,0:T(8,128)S(1)}, u32[]{:S(2)}, u32[]{:S(2)}) collective-permute-start(f32[2,112,256]{2,1,0:T(8,128)S(1)} %get-tuple-element.109), channel_id=1, source_target_pairs={{0,1},{1,0},{2,3},{3,2},{4,5},{5,4},{6,7},{7,6},{8,9},{9,8},{10,11... | collective-permute-start | bytes 688136 | tf_op jit(solution)/shard_map/ppermute | solution.py:441
  73.9 0.5 collective-permute-start.20
  74.4 2.7 %collective-permute-done.21.came = f32[4,64,256]{2,1,0:T(8,128)S(1)} collective-permute-done((f32[4,64,256]{2,1,0:T(8,128)S(1)}, f32[4,64,256]{2,1,0:T(8,128)S(1)}, u32[]{:S(2)}, u32[]{:S(2)}) %collective-permute-start.21) | collective-permute-done | bytes 262176 | tf_op jit(solution)/shard_map/ppermute | solution.py:441
  77.1 0.8 collective-permute-start.18
  77.9 1.6 %collective-permute-start.22 = (f32[2,64,256]{2,1,0:T(8,128)S(1)}, f32[2,64,256]{2,1,0:T(8,128)S(1)}, u32[]{:S(2)}, u32[]{:S(2)}) collective-permute-start(f32[2,64,256]{2,1,0:T(8,128)S(1)} %get-tuple-element.122), channel_id=1, source_target_pairs={{0,2},{2,0},{4,6},{6,4},{1,3},{3,1},{5,7},{7,5},{8,10},{10,8},{12,... | collective-permute-start | bytes 393224 | tf_op jit(solution)/shard_map/ppermute | solution.py:441
  79.5 0.6 collective-permute-done.12.came_a
  80.2 1.3 %collective-permute-start.23 = (f32[176,256]{1,0:T(8,128)S(1)}, f32[176,256]{1,0:T(8,128)S(1)}, u32[]{:S(2)}, u32[]{:S(2)}) collective-permute-start(f32[176,256]{1,0:T(8,128)S(1)} %get-tuple-element.124), channel_id=1, source_target_pairs={{0,1},{1,0},{2,3},{3,2},{4,5},{5,4},{6,7},{7,6},{8,9},{9,8},{10,11... | collective-permute-start | bytes 540680 | tf_op jit(solution)/shard_map/ppermute | solution.py:441
  81.5 3.3 %collective-permute-done.18.came_b = f32[2,64,256]{2,1,0:T(8,128)S(1)} collective-permute-done((f32[2,64,256]{2,1,0:T(8,128)S(1)}, f32[2,64,256]{2,1,0:T(8,128)S(1)}, u32[]{:S(2)}, u32[]{:S(2)}) %collective-permute-start.18) | collective-permute-done | bytes 131104 | tf_op jit(solution)/shard_map/ppermute | solution.py:441
  84.9 1.7 %collective-permute-start.24 = (f32[176,256]{1,0:T(8,128)S(1)}, f32[176,256]{1,0:T(8,128)S(1)}, u32[]{:S(2)}, u32[]{:S(2)}) collective-permute-start(f32[176,256]{1,0:T(8,128)S(1)} %get-tuple-element.125), channel_id=1, source_target_pairs={{0,2},{2,0},{4,6},{6,4},{1,3},{3,1},{5,7},{7,5},{8,10},{10,8},{12,... | collective-permute-start | bytes 540680 | tf_op jit(solution)/shard_map/ppermute | solution.py:441
  86.6 2.1 %collective-permute-start.25 = (f32[160,256]{1,0:T(8,128)S(1)}, f32[160,256]{1,0:T(8,128)S(1)}, u32[]{:S(2)}, u32[]{:S(2)}) collective-permute-start(f32[160,256]{1,0:T(8,128)S(1)} %get-tuple-element.126), channel_id=1, source_target_pairs={{0,6},{6,0},{2,4},{4,2},{1,7},{7,1},{3,5},{5,3},{8,14},{14,8},{10,... | collective-permute-start | bytes 491528 | tf_op jit(solution)/shard_map/ppermute | solution.py:441
  88.7 4.5 %collective-permute-done.25.refs_5_ = f32[160,256]{1,0:T(8,128)S(1)} collective-permute-done((f32[160,256]{1,0:T(8,128)S(1)}, f32[160,256]{1,0:T(8,128)S(1)}, u32[]{:S(2)}, u32[]{:S(2)}) %collective-permute-start.25) | collective-permute-done | bytes 163872 | tf_op jit(solution)/shard_map/ppermute | solution.py:441
  93.2 0.8 shard_map.110
  (30 shorter events, 0.4 us)
Async XLA Ops:
  0.0 39.8 %copy-start.1 = (bf16[2048,512]{1,0:T(8,128)(2,1)S(1)}, bf16[2048,512]{1,0:T(8,128)(2,1)}, u32[]{:S(2)}) copy-start(bf16[2048,512]{1,0:T(8,128)(2,1)} %refs_1_.3) | copy-start | bytes 6291460
  0.0 39.8 %copy-start.2 = (f32[8]{0:T(128)S(1)}, f32[8]{0:T(128)}, u32[]{:S(2)}) copy-start(f32[8]{0:T(128)} %refs_7_.3) | copy-start | bytes 100
  7.6 1.6 %collective-permute-start = (f32[136,512]{1,0:T(8,128)S(1)}, f32[136,512]{1,0:T(8,128)S(1)}, u32[]{:S(2)}, u32[]{:S(2)}) collective-permute-start(f32[136,512]{1,0:T(8,128)S(1)} %get-tuple-element.80), channel_id=1, source_target_pairs={{0,8},{8,0},{1,9},{9,1},{2,10},{10,2},{3,11},{11,3},{4,12},{12,4},... | collective-permute-start | bytes 835592 | tf_op jit(solution)/shard_map/ppermute | solution.py:393
  9.3 5.0 %collective-permute-start.1 = (f32[136,128]{1,0:T(8,128)S(1)}, f32[136,128]{1,0:T(8,128)S(1)}, u32[]{:S(2)}, u32[]{:S(2)}) collective-permute-start(f32[136,128]{1,0:T(8,128)S(1)} %get-tuple-element.82), channel_id=1, source_target_pairs={{0,16},{16,32},{32,48},{48,0},{1,17},{17,33},{33,49},{49,1},{2,18}... | collective-permute-start | bytes 208904 | tf_op jit(solution)/shard_map/ppermute | solution.py:364
  10.9 6.3 %collective-permute-start.2 = (f32[136,128]{1,0:T(8,128)S(1)}, f32[136,128]{1,0:T(8,128)S(1)}, u32[]{:S(2)}, u32[]{:S(2)}) collective-permute-start(f32[136,128]{1,0:T(8,128)S(1)} %get-tuple-element.83), channel_id=1, source_target_pairs={{0,32},{16,48},{32,0},{48,16},{1,33},{17,49},{33,1},{49,17},{2,34}... | collective-permute-start | bytes 208904 | tf_op jit(solution)/shard_map/ppermute | solution.py:364
  13.6 4.4 %collective-permute-start.3 = (f32[136,128]{1,0:T(8,128)S(1)}, f32[136,128]{1,0:T(8,128)S(1)}, u32[]{:S(2)}, u32[]{:S(2)}) collective-permute-start(f32[136,128]{1,0:T(8,128)S(1)} %get-tuple-element.84), channel_id=1, source_target_pairs={{0,48},{16,0},{32,16},{48,32},{1,49},{17,1},{33,17},{49,33},{2,50}... | collective-permute-start | bytes 208904 | tf_op jit(solution)/shard_map/ppermute | solution.py:364
  18.1 10.6 %collective-permute-start.4 = (f32[72,128]{1,0:T(8,128)S(1)}, f32[72,128]{1,0:T(8,128)S(1)}, u32[]{:S(2)}, u32[]{:S(2)}) collective-permute-start(f32[72,128]{1,0:T(8,128)S(1)} %get-tuple-element.86), channel_id=1, source_target_pairs={{0,64},{64,128},{128,192},{192,0},{1,65},{65,129},{129,193},{193,1... | collective-permute-start | bytes 110600 | tf_op jit(solution)/shard_map/ppermute | solution.py:364
  20.6 8.0 %collective-permute-start.5 = (f32[72,128]{1,0:T(8,128)S(1)}, f32[72,128]{1,0:T(8,128)S(1)}, u32[]{:S(2)}, u32[]{:S(2)}) collective-permute-start(f32[72,128]{1,0:T(8,128)S(1)} %get-tuple-element.87), channel_id=1, source_target_pairs={{0,128},{64,192},{128,0},{192,64},{1,129},{65,193},{129,1},{193,65... | collective-permute-start | bytes 110600 | tf_op jit(solution)/shard_map/ppermute | solution.py:364
  26.0 4.9 %collective-permute-start.6 = (f32[72,128]{1,0:T(8,128)S(1)}, f32[72,128]{1,0:T(8,128)S(1)}, u32[]{:S(2)}, u32[]{:S(2)}) collective-permute-start(f32[72,128]{1,0:T(8,128)S(1)} %get-tuple-element.88), channel_id=1, source_target_pairs={{0,192},{64,0},{128,64},{192,128},{1,193},{65,1},{129,65},{193,129... | collective-permute-start | bytes 110600 | tf_op jit(solution)/shard_map/ppermute | solution.py:364
  31.0 5.5 %collective-permute-start.7 = (f32[128,128]{1,0:T(8,128)S(1)}, f32[128,128]{1,0:T(8,128)S(1)}, u32[]{:S(2)}, u32[]{:S(2)}) collective-permute-start(f32[128,128]{1,0:T(8,128)S(1)} %get-tuple-element.90), channel_id=1, source_target_pairs={{0,16},{16,32},{32,48},{48,0},{1,17},{17,33},{33,49},{49,1},{2,18}... | collective-permute-start | bytes 196616 | tf_op jit(solution)/shard_map/ppermute | solution.py:364
  32.4 5.8 %collective-permute-start.8 = (f32[128,128]{1,0:T(8,128)S(1)}, f32[128,128]{1,0:T(8,128)S(1)}, u32[]{:S(2)}, u32[]{:S(2)}) collective-permute-start(f32[128,128]{1,0:T(8,128)S(1)} %get-tuple-element.91), channel_id=1, source_target_pairs={{0,32},{16,48},{32,0},{48,16},{1,33},{17,49},{33,1},{49,17},{2,34}... | collective-permute-start | bytes 196616 | tf_op jit(solution)/shard_map/ppermute | solution.py:364
  35.2 4.3 %collective-permute-start.9 = (f32[128,128]{1,0:T(8,128)S(1)}, f32[128,128]{1,0:T(8,128)S(1)}, u32[]{:S(2)}, u32[]{:S(2)}) collective-permute-start(f32[128,128]{1,0:T(8,128)S(1)} %get-tuple-element.92), channel_id=1, source_target_pairs={{0,48},{16,0},{32,16},{48,32},{1,49},{17,1},{33,17},{49,33},{2,50}... | collective-permute-start | bytes 196616 | tf_op jit(solution)/shard_map/ppermute | solution.py:364
  39.5 8.0 %collective-permute-start.10 = (f32[128,512]{1,0:T(8,128)S(1)}, f32[128,512]{1,0:T(8,128)S(1)}, u32[]{:S(2)}, u32[]{:S(2)}) collective-permute-start(f32[128,512]{1,0:T(8,128)S(1)} %get-tuple-element.94), channel_id=1, source_target_pairs={{0,8},{8,0},{1,9},{9,1},{2,10},{10,2},{3,11},{11,3},{4,12},{12,4},... | collective-permute-start | bytes 786440 | tf_op jit(solution)/shard_map/ppermute | solution.py:425
  39.8 3.4 %copy-start = (bf16[512,2048]{1,0:T(8,128)(2,1)S(1)}, bf16[512,2048]{1,0:T(8,128)(2,1)}, u32[]{:S(2)}) copy-start(bf16[512,2048]{1,0:T(8,128)(2,1)} %out_w.1) | copy-start | bytes 6291460
  49.3 19.4 %collective-permute-start.11 = (f32[4,112,256]{2,1,0:T(8,128)S(1)}, f32[4,112,256]{2,1,0:T(8,128)S(1)}, u32[]{:S(2)}, u32[]{:S(2)}) collective-permute-start(f32[4,112,256]{2,1,0:T(8,128)S(1)} %get-tuple-element.98), channel_id=1, source_target_pairs={{0,2},{2,0},{4,6},{6,4},{1,3},{3,1},{5,7},{7,5},{8,10},{10,8},{12,... | collective-permute-start | bytes 1376264 | tf_op jit(solution)/shard_map/ppermute | solution.py:441
  51.0 20.9 %collective-permute-start.15 = (f32[4,112,256]{2,1,0:T(8,128)S(1)}, f32[4,112,256]{2,1,0:T(8,128)S(1)}, u32[]{:S(2)}, u32[]{:S(2)}) collective-permute-start(f32[4,112,256]{2,1,0:T(8,128)S(1)} %get-tuple-element.107), channel_id=1, source_target_pairs={{0,6},{6,0},{2,4},{4,2},{1,7},{7,1},{3,5},{5,3},{8,14},{14,8},{10,... | collective-permute-start | bytes 1376264 | tf_op jit(solution)/shard_map/ppermute | solution.py:441
  54.2 13.7 %collective-permute-start.13 = (f32[4,64,256]{2,1,0:T(8,128)S(1)}, f32[4,64,256]{2,1,0:T(8,128)S(1)}, u32[]{:S(2)}, u32[]{:S(2)}) collective-permute-start(f32[4,64,256]{2,1,0:T(8,128)S(1)} %get-tuple-element.102), channel_id=1, source_target_pairs={{0,2},{2,0},{4,6},{6,4},{1,3},{3,1},{5,7},{7,5},{8,10},{10,8},{12,... | collective-permute-start | bytes 786440 | tf_op jit(solution)/shard_map/ppermute | solution.py:441
  54.9 17.5 %collective-permute-start.19 = (f32[4,96,256]{2,1,0:T(8,128)S(1)}, f32[4,96,256]{2,1,0:T(8,128)S(1)}, u32[]{:S(2)}, u32[]{:S(2)}) collective-permute-start(f32[4,96,256]{2,1,0:T(8,128)S(1)} %get-tuple-element.116), channel_id=1, source_target_pairs={{0,1},{1,0},{2,3},{3,2},{4,5},{5,4},{6,7},{7,6},{8,9},{9,8},{10,11... | collective-permute-start | bytes 1179656 | tf_op jit(solution)/shard_map/ppermute | solution.py:441
  55.6 18.2 %collective-permute-start.17 = (f32[4,64,256]{2,1,0:T(8,128)S(1)}, f32[4,64,256]{2,1,0:T(8,128)S(1)}, u32[]{:S(2)}, u32[]{:S(2)}) collective-permute-start(f32[4,64,256]{2,1,0:T(8,128)S(1)} %get-tuple-element.111), channel_id=1, source_target_pairs={{0,6},{6,0},{2,4},{4,2},{1,7},{7,1},{3,5},{5,3},{8,14},{14,8},{10,... | collective-permute-start | bytes 786440 | tf_op jit(solution)/shard_map/ppermute | solution.py:441
  67.9 9.2 %collective-permute-start.21 = (f32[4,64,256]{2,1,0:T(8,128)S(1)}, f32[4,64,256]{2,1,0:T(8,128)S(1)}, u32[]{:S(2)}, u32[]{:S(2)}) collective-permute-start(f32[4,64,256]{2,1,0:T(8,128)S(1)} %get-tuple-element.120), channel_id=1, source_target_pairs={{0,1},{1,0},{2,3},{3,2},{4,5},{5,4},{6,7},{7,6},{8,9},{9,8},{10,11... | collective-permute-start | bytes 786440 | tf_op jit(solution)/shard_map/ppermute | solution.py:441
  68.7 9.2 %collective-permute-start.14 = (f32[2,64,256]{2,1,0:T(8,128)S(1)}, f32[2,64,256]{2,1,0:T(8,128)S(1)}, u32[]{:S(2)}, u32[]{:S(2)}) collective-permute-start(f32[2,64,256]{2,1,0:T(8,128)S(1)} %get-tuple-element.104), channel_id=1, source_target_pairs={{0,6},{6,0},{2,4},{4,2},{1,7},{7,1},{3,5},{5,3},{8,14},{14,8},{10,... | collective-permute-start | bytes 393224 | tf_op jit(solution)/shard_map/ppermute | solution.py:441
  71.9 8.3 %collective-permute-start.12 = (f32[2,112,256]{2,1,0:T(8,128)S(1)}, f32[2,112,256]{2,1,0:T(8,128)S(1)}, u32[]{:S(2)}, u32[]{:S(2)}) collective-permute-start(f32[2,112,256]{2,1,0:T(8,128)S(1)} %get-tuple-element.100), channel_id=1, source_target_pairs={{0,6},{6,0},{2,4},{4,2},{1,7},{7,1},{3,5},{5,3},{8,14},{14,8},{10,... | collective-permute-start | bytes 688136 | tf_op jit(solution)/shard_map/ppermute | solution.py:441
  72.5 12.3 %collective-permute-start.16 = (f32[2,112,256]{2,1,0:T(8,128)S(1)}, f32[2,112,256]{2,1,0:T(8,128)S(1)}, u32[]{:S(2)}, u32[]{:S(2)}) collective-permute-start(f32[2,112,256]{2,1,0:T(8,128)S(1)} %get-tuple-element.109), channel_id=1, source_target_pairs={{0,1},{1,0},{2,3},{3,2},{4,5},{5,4},{6,7},{7,6},{8,9},{9,8},{10,11... | collective-permute-start | bytes 688136 | tf_op jit(solution)/shard_map/ppermute | solution.py:441
  73.9 12.7 %collective-permute-start.20 = (f32[2,96,256]{2,1,0:T(8,128)S(1)}, f32[2,96,256]{2,1,0:T(8,128)S(1)}, u32[]{:S(2)}, u32[]{:S(2)}) collective-permute-start(f32[2,96,256]{2,1,0:T(8,128)S(1)} %get-tuple-element.118), channel_id=1, source_target_pairs={{0,2},{2,0},{4,6},{6,4},{1,3},{3,1},{5,7},{7,5},{8,10},{10,8},{12,... | collective-permute-start | bytes 589832 | tf_op jit(solution)/shard_map/ppermute | solution.py:441
  77.1 7.7 %collective-permute-start.18 = (f32[2,64,256]{2,1,0:T(8,128)S(1)}, f32[2,64,256]{2,1,0:T(8,128)S(1)}, u32[]{:S(2)}, u32[]{:S(2)}) collective-permute-start(f32[2,64,256]{2,1,0:T(8,128)S(1)} %get-tuple-element.113), channel_id=1, source_target_pairs={{0,1},{1,0},{2,3},{3,2},{4,5},{5,4},{6,7},{7,6},{8,9},{9,8},{10,11... | collective-permute-start | bytes 393224 | tf_op jit(solution)/shard_map/ppermute | solution.py:441
  77.9 8.6 %collective-permute-start.22 = (f32[2,64,256]{2,1,0:T(8,128)S(1)}, f32[2,64,256]{2,1,0:T(8,128)S(1)}, u32[]{:S(2)}, u32[]{:S(2)}) collective-permute-start(f32[2,64,256]{2,1,0:T(8,128)S(1)} %get-tuple-element.122), channel_id=1, source_target_pairs={{0,2},{2,0},{4,6},{6,4},{1,3},{3,1},{5,7},{7,5},{8,10},{10,8},{12,... | collective-permute-start | bytes 393224 | tf_op jit(solution)/shard_map/ppermute | solution.py:441
  80.2 13.0 %collective-permute-start.23 = (f32[176,256]{1,0:T(8,128)S(1)}, f32[176,256]{1,0:T(8,128)S(1)}, u32[]{:S(2)}, u32[]{:S(2)}) collective-permute-start(f32[176,256]{1,0:T(8,128)S(1)} %get-tuple-element.124), channel_id=1, source_target_pairs={{0,1},{1,0},{2,3},{3,2},{4,5},{5,4},{6,7},{7,6},{8,9},{9,8},{10,11... | collective-permute-start | bytes 540680 | tf_op jit(solution)/shard_map/ppermute | solution.py:441
  84.9 8.4 %collective-permute-start.24 = (f32[176,256]{1,0:T(8,128)S(1)}, f32[176,256]{1,0:T(8,128)S(1)}, u32[]{:S(2)}, u32[]{:S(2)}) collective-permute-start(f32[176,256]{1,0:T(8,128)S(1)} %get-tuple-element.125), channel_id=1, source_target_pairs={{0,2},{2,0},{4,6},{6,4},{1,3},{3,1},{5,7},{7,5},{8,10},{10,8},{12,... | collective-permute-start | bytes 540680 | tf_op jit(solution)/shard_map/ppermute | solution.py:441
  86.6 6.6 %collective-permute-start.25 = (f32[160,256]{1,0:T(8,128)S(1)}, f32[160,256]{1,0:T(8,128)S(1)}, u32[]{:S(2)}, u32[]{:S(2)}) collective-permute-start(f32[160,256]{1,0:T(8,128)S(1)} %get-tuple-element.126), channel_id=1, source_target_pairs={{0,6},{6,0},{2,4},{4,2},{1,7},{7,1},{3,5},{5,3},{8,14},{14,8},{10,... | collective-permute-start | bytes 491528 | tf_op jit(solution)/shard_map/ppermute | solution.py:441

commit v3 on v2

--- a/solution.py
+++ b/solution.py
@@ -54,7 +54,6 @@
     heads = rate.shape[0]
     inner = input_w.shape[1]
     size = state_w.shape[1] // 2
-    half = size // 2
     chunk = 512
     chunks = [slice(k * chunk, (k + 1) * chunk) for k in range(width // chunk)]
     moves = [(step_hbm, step_w), (bias_hbm, bias), (rate_hbm, rate)]
@@ -97,21 +96,27 @@
     decay = jnp.exp(total)
     d_fwd = jnp.sum(pick * decay[:heads], axis=0, keepdims=True)
     d_bwd = jnp.sum(pick * decay[heads:], axis=0, keepdims=True)
-    line = lax.broadcasted_iota(jnp.int32, (8, inner), 0)
-    decays = jnp.where(line == 0, d_fwd, jnp.where(line == 1, d_bwd, F32(0)))
-    keep[size:, :] = decays
-    send[size:, :] = decays
     copies[4 + len(chunks)].wait()
-    mine = lax.axis_index("core") == 0
-    for source, inputs, proj, b in ((seq, in_f, proj_f, 0), (flipped, in_b, proj_b, 1)):
+    core = lax.axis_index("core")
+    for source, inputs, proj, b, decay_row in (
+        (seq, in_f, proj_f, 0, d_fwd), (flipped, in_b, proj_b, 1, d_bwd)
+    ):
         weight = dot(to_end[b * heads : (b + 1) * heads], pick.astype(BF16), ((0,), (0,)))
         values = dot(source[...], input_w[...]).astype(BF16)
         inputs[...] = values
         weighted = (values.astype(F32) * weight).astype(BF16)
         state = dot(proj[:, :size], weighted, ((0,), (0,)))
-        at = slice(b * half, (b + 1) * half)
-        keep[at, :] = jnp.where(mine, state[:half], state[half:])
-        send[at, :] = jnp.where(mine, state[half:], state[:half])
+        decays = jnp.broadcast_to(decay_row, (8, inner))
+
+        @pl.when(core == b)
+        def _(state=state, decays=decays):
+            keep[:size, :] = state
+            keep[size:, :] = decays
+
+        @pl.when(core != b)
+        def _(state=state, decays=decays):
+            send[:size, :] = state
+            send[size:, :] = decays
 
 
 def inside_kernel(b, source, gate_w, inputs, proj, step, log, log_cols, gain, base, slope, pair):
@@ -169,106 +174,75 @@
 
 
 BLOCKS = 4
-ROWS = 16
+ROWS = 32
+
+
+def place(axis):
+    return in_order(lax.axis_index(axis))
+
+
+def in_order(index):
+    return jnp.where(lax.axis_index("core") == 0, index, 3 - index)
 
 
 def chip_kernel(keep, got, own, to1, to2, to3, total):
-    first = lax.axis_index("core") == 0
     y = lax.axis_index("y")
     size = 128
-    half = size // 2
+    total[...] = got[size : size + 1, :] * keep[:size, :] + got[:size, :]
     decays = keep[size:, :] * got[size:, :]
-    for b in range(2):
-        at = slice(b * half, (b + 1) * half)
-        mine, other = keep[at, :], got[at, :]
-        d_mine, d_other = keep[size + b : size + b + 1, :], got[size + b : size + b + 1, :]
-        last = first if b else jnp.logical_not(first)
-        total[at, :] = jnp.where(last, d_mine * other + mine, d_other * mine + other)
     for k, ref in enumerate((own, to1, to2, to3)):
-        to = lax.rem(y + k, 4)
-        for b in range(2):
-            start = pl.multiple_of(b * half + to * ROWS, ROWS)
-            piece = total[pl.ds(start, ROWS), :]
-            for j in range(BLOCKS):
-                cols = slice(j * 128, (j + 1) * 128)
-                row = (b * BLOCKS + j) * ROWS
-                ref[row : row + ROWS, :] = piece[:, cols]
-                row = 2 * BLOCKS * ROWS + b * BLOCKS + j
-                ref[row : row + 1, :] = decays[b : b + 1, cols]
-
-
-def state_at(ref, b, j):
-    row = (b * BLOCKS + j) * ROWS
-    return ref[row : row + ROWS, :]
-
-
-def decay_at(ref, b, j):
-    row = 2 * BLOCKS * ROWS + b * BLOCKS + j
-    return ref[row : row + 1, :]
-
-
-def group_kernel(own, got1, got2, got3, to1, to2, to3, ordered):
-    y, z = lax.axis_index("y"), lax.axis_index("z_hi")
+        start = pl.multiple_of(lax.rem(y + k, 4) * ROWS, ROWS)
+        piece = total[pl.ds(start, ROWS), :]
+        for j in range(BLOCKS):
+            cols = slice(j * 128, (j + 1) * 128)
+            ref[j * ROWS : (j + 1) * ROWS, :] = piece[:, cols]
+            ref[BLOCKS * ROWS + j : BLOCKS * ROWS + j + 1, :] = decays[:1, cols]
+
+
+def state_at(ref, j):
+    return ref[j * ROWS : (j + 1) * ROWS, :]
+
+
+def decay_at(ref, j):
+    return ref[BLOCKS * ROWS + j : BLOCKS * ROWS + j + 1, :]
+
+
+def group_kernel(own, got1, got2, got3, total, ordered):
+    y = lax.axis_index("y")
     for k, ref in enumerate((own, got1, got2, got3)):
-        ordered[lax.rem(y + 4 - k, 4)] = ref[...]
+        ordered[in_order(lax.rem(y + 4 - k, 4))] = ref[...]
     for j in range(BLOCKS):
-        sums = []
-        for b in range(2):
-            state, decay = jnp.zeros((ROWS, 128), F32), jnp.ones((1, 128), F32)
-            for k in (3, 2, 1, 0) if b else (0, 1, 2, 3):
-                piece = ordered.at[k]
-                state = decay_at(piece, b, j) * state + state_at(piece, b, j)
-                decay = decay * decay_at(piece, b, j)
-            sums.append((state, decay))
-        for k, ref in ((1, to1), (2, to2), (3, to3)):
-            up = z + k < 4
-            row = j * ROWS
-            ref[row : row + ROWS, :] = jnp.where(up, sums[0][0], sums[1][0])
-            row = BLOCKS * ROWS + j
-            ref[row : row + 1, :] = jnp.where(up, sums[0][1], sums[1][1])
+        state, decay = jnp.zeros((ROWS, 128), F32), jnp.ones((1, 128), F32)
+        for k in range(4):
+            piece = ordered.at[k]
+            state = decay_at(piece, j) * state + state_at(piece, j)
+            decay = decay * decay_at(piece, j)
+        total[j * ROWS : (j + 1) * ROWS, :] = state
+        total[BLOCKS * ROWS + j : BLOCKS * ROWS + j + 1, :] = decay
 
 
 def carry_kernel(ordered, got1, got2, got3, own, to1, to2, to3, carries):
-    y, z = lax.axis_index("y"), lax.axis_index("z_hi")
-    got = (None, got1, got2, got3)
+    y, z = lax.axis_index("y"), place("z_hi")
     for j in range(BLOCKS):
-        row = BLOCKS * ROWS + j
-        states = [None] + [g[j * ROWS : (j + 1) * ROWS, :] for g in got[1:]]
-        decays = [None] + [g[row : row + 1, :] for g in got[1:]]
-        fwd = bwd = jnp.zeros((ROWS, 128), F32)
-        for k in (3, 2, 1):
-            fwd = jnp.where(k <= z, decays[k] * fwd + states[k], fwd)
-        for k in (1, 2, 3):
-            bwd = jnp.where(k > z, decays[k] * bwd + states[k], bwd)
-        for b, carry in ((0, fwd), (1, bwd)):
-            at = slice((b * BLOCKS + j) * ROWS, (b * BLOCKS + j + 1) * ROWS)
-            for k in (3, 2, 1, 0) if b else (0, 1, 2, 3):
-                carries[k, at, :] = carry
-                piece = ordered.at[k]
-                carry = decay_at(piece, b, j) * carry + state_at(piece, b, j)
+        carry = jnp.zeros((ROWS, 128), F32)
+        for k, ref in ((3, got3), (2, got2), (1, got1)):
+            carry = jnp.where(k <= z, decay_at(ref, j) * carry + state_at(ref, j), carry)
+        for k in range(4):
+            carries[k, j * ROWS : (j + 1) * ROWS, :] = carry
+            piece = ordered.at[k]
+            carry = decay_at(piece, j) * carry + state_at(piece, j)
     for k, ref in enumerate((own, to1, to2, to3)):
-        ref[...] = carries[lax.rem(y + k, 4)]
-
-
-def core_kernel(own, got1, got2, got3, keep, other, mine_out, other_out, chip):
+        ref[...] = carries[in_order(lax.rem(y + k, 4))]
+
+
+def core_kernel(own, got1, got2, got3, keep, mine_out, other_out):
     y = lax.axis_index("y")
-    first = lax.axis_index("core") == 0
-    half = 64
+    size = 128
     for k, ref in enumerate((own, got1, got2, got3)):
-        source = lax.rem(y + 4 - k, 4)
-        for b in range(2):
-            start = pl.multiple_of(b * half + source * ROWS, ROWS)
-            for j in range(BLOCKS):
-                chip[pl.ds(start, ROWS), j * 128 : (j + 1) * 128] = state_at(ref, b, j)
-    for b in range(2):
-        at = slice(b * half, (b + 1) * half)
-        d = 2 * half + b
-        entering = chip[at, :]
-        from_mine = keep[d : d + 1, :] * entering + keep[at, :]
-        from_other = other[d : d + 1, :] * entering + other[at, :]
-        leads = jnp.logical_not(first) if b else first
-        mine_out[at, :] = jnp.where(leads, entering, from_other)
-        other_out[at, :] = jnp.where(leads, from_mine, entering)
+        start = pl.multiple_of(lax.rem(y + 4 - k, 4) * ROWS, ROWS)
+        for j in range(BLOCKS):
+            mine_out[pl.ds(start, ROWS), j * 128 : (j + 1) * 128] = state_at(ref, j)
+    other_out[...] = keep[size : size + 1, :] * mine_out[...] + keep[:size, :]
 
 
 def target_block(q):
@@ -284,14 +258,12 @@
     count = sum(out.shape[1] for out in outs[:3])
     at = slice(first_row, first_row + count)
     size = proj_f.shape[1] // 2
-    half = size // 2
     low_core = lax.axis_index("core") == 0
     gated = []
-    for b, base, slope, proj in ((0, base_f, slope_f, proj_f), (1, base_b, slope_b, proj_b)):
-        rows = slice(b * half, (b + 1) * half)
-        low = jnp.where(low_core, carry[rows, :], got[rows, :])
-        high = jnp.where(low_core, got[rows, :], carry[rows, :])
-        entering = jnp.concatenate([low, high], axis=0).astype(BF16)
+    for base, slope, proj, near_carry, far_carry in (
+        (base_f, slope_f, proj_f, carry, got), (base_b, slope_b, proj_b, got, carry)
+    ):
+        entering = jnp.where(low_core, near_carry[...], far_carry[...]).astype(BF16)
         carried = dot(proj[at, size:], entering)
         total = base[at, :].astype(F32) + slope[at, :].astype(F32) * carried
         gated.append(total.astype(BF16))
@@ -408,24 +380,28 @@
     plain, flipped = call(
         flip_kernel, (output_weight,), [near(blocks, BF16)] * 2, flops=inner * width * 512
     )
-    message = near((2 * BLOCKS * ROWS + 8, 128))
-    group = near((BLOCKS * ROWS + 8, 128))
-    back = near((2 * BLOCKS * ROWS, 128))
+    message = near((BLOCKS * ROWS + 8, 128))
+    back = near((BLOCKS * ROWS, 128))
     own, *pieces = call(chip_kernel, (keep, other), [message] * 4,
                         scratch=[pltpu.VMEM((size, inner), F32)])
     got = shifted(pieces, "y")
-    *pieces, ordered = call(group_kernel, (own, *got),
-                            [group] * 3 + [near((4, *message.shape))])
-    far = shifted(pieces, "z_hi")
+    total, ordered = call(group_kernel, (own, *got), [message, near((4, *message.shape))])
+    far = [
+        lax.ppermute(
+            total, ("z_hi", "core"),
+            [(2 * z, 2 * (z + k)) for z in range(4 - k)]
+            + [(2 * z + 1, 2 * (z - k) + 1) for z in range(k, 4)],
+        )
+        for k in (1, 2, 3)
+    ]
     own, *pieces = call(carry_kernel, (ordered, *far), [back] * 4,
                         scratch=[pltpu.VMEM((4, *back.shape), F32)])
     got = shifted(pieces, "y")
-    carry, give = call(core_kernel, (own, *got, keep, other), [near((size, inner))] * 2,
-                       scratch=[pltpu.VMEM((size, inner), F32)])
+    carry, give = call(core_kernel, (own, *got, keep), [near((size, inner))] * 2)
     arrived = lax.ppermute(give, "core", swap)
 
     first_row, parts = 0, []
-    counts = ((112, 112, 96), (64, 64, 64))
+    counts = ((128, 96, 96), (64, 64, 64))
     for group in range(2):
         outs = call(
             lambda *refs, at=first_row: output_kernel(at, *refs),

time: 94.1 us -> 98.3 us (1.045); the launches traced: 94 us -> 96.6 us
  waiting for transfers between devices: 33.2 us -> 36 us
    ppermute x0 -> x3, starting transfers between devices: none -> 13 us  [on_device(): lax.ppermute(total, ('z_hi', 'core'), [(2 * z, 2 * (z + k)) for z in rang...]
    ppermute x9 -> x6, starting transfers between devices: 21.1 us -> 10.5 us  [shifted(): lax.ppermute(v, axis, [(j, (j + k) % 4) for j in range(4)])]
    ppermute x15, waiting for transfers between devices: 22.8 us -> 25.8 us  [travel(): return lax.ppermute(value, axis, pairs)]
    ppermute x9 -> x6, waiting for transfers between devices: 8.86 us -> 6.01 us  [shifted(): lax.ppermute(v, axis, [(j, (j + k) % 4) for j in range(4)])]
    ppermute x0 -> x3, waiting for transfers between devices: none -> 2.58 us  [on_device(): lax.ppermute(total, ('z_hi', 'core'), [(2 * z, 2 * (z + k)) for z in rang...]
    ppermute x15, starting transfers between devices: 19.4 us -> 17 us  [travel(): return lax.ppermute(value, axis, pairs)]
  transfers between devices with their start and end apart: 26 -> 26, of which waited for: 11 -> 12; matrix products, arithmetic and copies ran while one was open for 0% -> 0% of each run, Pallas kernels for 10% -> 9%
where the time goes in v3:
time: 98.3 us; the launch traced here: 96.6 us
  starting transfers between devices  40.8 us (42%)
  waiting for transfers between devices  36 us (37%)
  Pallas kernels  19.6 us (20%)
    ppermute x15, waiting for transfers between devices, travel(): return lax.ppermute(value, axis, pairs)  25.8 us
    pallas_call x20, Pallas kernels, call(): pl.pallas_call(kernel, out_shape=outs, in_specs=specs, out_specs=[VMEM_SP...  19.6 us
    ppermute x15, starting transfers between devices, travel(): return lax.ppermute(value, axis, pairs)  17 us
    ppermute x3, starting transfers between devices, on_device(): lax.ppermute(total, ('z_hi', 'core'), [(2 * z, 2 * (z + k)) for z in rang...  13 us
    ppermute x6, starting transfers between devices, shifted(): lax.ppermute(v, axis, [(j, (j + k) % 4) for j in range(4)])  10.5 us
    ppermute x6, waiting for transfers between devices, shifted(): lax.ppermute(v, axis, [(j, (j + k) % 4) for j in range(4)])  6.01 us
    ppermute x3, waiting for transfers between devices, on_device(): lax.ppermute(total, ('z_hi', 'core'), [(2 * z, 2 * (z + k)) for z in rang...  2.58 us
  transfers between devices with their start and end apart: 26, of which 12 were waited for; matrix products, arithmetic and copies ran while one was open for 0% of the time, Pallas kernels for 9%

profile of v3, /device:TPU:8, one launch (start us, length us, event | category | flops | bytes accessed | tf_op | source)
XLA Modules:
  0.0 96.6 jit_solution(7300682282655668061)
XLA Ops:
  0.0 7.7 %shard_map.91 = (bf16[512,2048]{1,0:T(8,128)(2,1)S(1)}, bf16[512,2048]{1,0:T(8,128)(2,1)S(1)}, bf16[512,512]{1,0:T(8,128)(2,1)S(1)}, bf16[512,512]{1,0:T(8,128)(...) custom-call(bf16[512,2048]{1,0:T(8,128)(2,1)} %seq_hbm.1, ...), custom_call_target="tpu_custom_call" | custom-call | flops 3221225472 | bytes 5275712 | tf_op jit(solution)/shard_map/pallas_call | solution.py:323
  7.7 0.1 collective-permute-start
  7.8 1.5 %collective-permute-done.got = f32[136,512]{1,0:T(8,128)S(1)} collective-permute-done((f32[136,512]{1,0:T(8,128)S(1)}, f32[136,512]{1,0:T(8,128)S(1)}, u32[]{:S(2)}, u32[]{:S(2)}) %collective-permute-start) | collective-permute-done | bytes 278560 | tf_op jit(solution)/shard_map/ppermute | solution.py:365
  9.4 0.1 shard_map.94
  9.4 1.7 %collective-permute-start.1 = (f32[136,128]{1,0:T(8,128)S(1)}, f32[136,128]{1,0:T(8,128)S(1)}, u32[]{:S(2)}, u32[]{:S(2)}) collective-permute-start(f32[136,128]{1,0:T(8,128)S(1)} %get-tuple-element.80), channel_id=1, source_target_pairs={{0,16},{16,32},{32,48},{48,0},{1,17},{17,33},{33,49},{49,1},{2,18}... | collective-permute-start | bytes 208904 | tf_op jit(solution)/shard_map/ppermute | solution.py:336
  11.1 2.6 %collective-permute-start.2 = (f32[136,128]{1,0:T(8,128)S(1)}, f32[136,128]{1,0:T(8,128)S(1)}, u32[]{:S(2)}, u32[]{:S(2)}) collective-permute-start(f32[136,128]{1,0:T(8,128)S(1)} %get-tuple-element.81), channel_id=1, source_target_pairs={{0,32},{16,48},{32,0},{48,16},{1,33},{17,49},{33,1},{49,17},{2,34}... | collective-permute-start | bytes 208904 | tf_op jit(solution)/shard_map/ppermute | solution.py:336
  13.8 0.7 collective-permute-start.3
  14.5 2.9 %collective-permute-done.2.got2 = f32[136,128]{1,0:T(8,128)S(1)} collective-permute-done((f32[136,128]{1,0:T(8,128)S(1)}, f32[136,128]{1,0:T(8,128)S(1)}, u32[]{:S(2)}, u32[]{:S(2)}) %collective-permute-start.2) | collective-permute-done | bytes 69664 | tf_op jit(solution)/shard_map/ppermute | solution.py:336
  17.4 0.8 collective-permute-done.3.got3
  18.2 4.4 %collective-permute-start.4 = (f32[136,128]{1,0:T(8,128)S(1)}, f32[136,128]{1,0:T(8,128)S(1)}, u32[]{:S(2)}, u32[]{:S(2)}) collective-permute-start(f32[136,128]{1,0:T(8,128)S(1)} %get-tuple-element.84), channel_id=1, source_target_pairs={{0,64},{64,128},{128,192},{72,8},{136,72},{200,136},{1,65},{65,129... | collective-permute-start | bytes 208904 | tf_op jit(solution)/shard_map/ppermute | solution.py:390
  22.6 7.3 %collective-permute-start.5 = (f32[136,128]{1,0:T(8,128)S(1)}, f32[136,128]{1,0:T(8,128)S(1)}, u32[]{:S(2)}, u32[]{:S(2)}) collective-permute-start(f32[136,128]{1,0:T(8,128)S(1)} %get-tuple-element.84), channel_id=1, source_target_pairs={{0,128},{64,192},{136,8},{200,72},{1,129},{65,193},{137,9},{201,73... | collective-permute-start | bytes 208904 | tf_op jit(solution)/shard_map/ppermute | solution.py:390
  29.9 1.3 %collective-permute-start.6 = (f32[136,128]{1,0:T(8,128)S(1)}, f32[136,128]{1,0:T(8,128)S(1)}, u32[]{:S(2)}, u32[]{:S(2)}) collective-permute-start(f32[136,128]{1,0:T(8,128)S(1)} %get-tuple-element.84), channel_id=1, source_target_pairs={{0,192},{200,8},{1,193},{201,9},{2,194},{202,10},{3,195},{203,11},... | collective-permute-start | bytes 208904 | tf_op jit(solution)/shard_map/ppermute | solution.py:390
  31.2 0.6 collective-permute-done.5.got2
  31.8 2.0 %collective-permute-done.6.got3 = f32[136,128]{1,0:T(8,128)S(1)} collective-permute-done((f32[136,128]{1,0:T(8,128)S(1)}, f32[136,128]{1,0:T(8,128)S(1)}, u32[]{:S(2)}, u32[]{:S(2)}) %collective-permute-start.6) | collective-permute-done | bytes 69664 | tf_op jit(solution)/shard_map/ppermute | solution.py:390
  33.8 0.1 shard_map.96
  33.9 1.3 %collective-permute-start.7 = (f32[128,128]{1,0:T(8,128)S(1)}, f32[128,128]{1,0:T(8,128)S(1)}, u32[]{:S(2)}, u32[]{:S(2)}) collective-permute-start(f32[128,128]{1,0:T(8,128)S(1)} %get-tuple-element.86), channel_id=1, source_target_pairs={{0,16},{16,32},{32,48},{48,0},{1,17},{17,33},{33,49},{49,1},{2,18}... | collective-permute-start | bytes 196616 | tf_op jit(solution)/shard_map/ppermute | solution.py:336
  35.2 2.2 %collective-permute-start.8 = (f32[128,128]{1,0:T(8,128)S(1)}, f32[128,128]{1,0:T(8,128)S(1)}, u32[]{:S(2)}, u32[]{:S(2)}) collective-permute-start(f32[128,128]{1,0:T(8,128)S(1)} %get-tuple-element.87), channel_id=1, source_target_pairs={{0,32},{16,48},{32,0},{48,16},{1,33},{17,49},{33,1},{49,17},{2,34}... | collective-permute-start | bytes 196616 | tf_op jit(solution)/shard_map/ppermute | solution.py:336
  37.4 2.0 %collective-permute-start.9 = (f32[128,128]{1,0:T(8,128)S(1)}, f32[128,128]{1,0:T(8,128)S(1)}, u32[]{:S(2)}, u32[]{:S(2)}) collective-permute-start(f32[128,128]{1,0:T(8,128)S(1)} %get-tuple-element.88), channel_id=1, source_target_pairs={{0,48},{16,0},{32,16},{48,32},{1,49},{17,1},{33,17},{49,33},{2,50}... | collective-permute-start | bytes 196616 | tf_op jit(solution)/shard_map/ppermute | solution.py:336
  39.4 1.6 %collective-permute-done.8.got2 = f32[128,128]{1,0:T(8,128)S(1)} collective-permute-done((f32[128,128]{1,0:T(8,128)S(1)}, f32[128,128]{1,0:T(8,128)S(1)}, u32[]{:S(2)}, u32[]{:S(2)}) %collective-permute-start.8) | collective-permute-done | bytes 65568 | tf_op jit(solution)/shard_map/ppermute | solution.py:336
  41.0 0.7 collective-permute-done.9.got3
  41.7 0.1 shard_map.97
  41.7 0.3 collective-permute-start.10
  42.1 3.3 %shard_map.92 = (bf16[512,512]{1,0:T(8,128)(2,1)S(1)}, bf16[512,512]{1,0:T(8,128)(2,1)S(1)}) custom-call(bf16[512,2048]{1,0:T(8,128)(2,1)S(1)} %get-tuple-element.64.refs_0_, bf16[2048,512]{1,0:T(8,128)(2,1)S(1)} %copy-done.1, bf16[512,512]{1,0:T(8,128)(2,1)S(1)} %get-tuple-element.65.refs_2_, bf16[512,256]{1,0:T(8,128)(2,1)S(1)} %get-tuple-element.66.refs_3_.refs_4_, ...), custom_call_target="tpu_custom_call" | custom-call | flops 2147483648 | bytes 5308448 | tf_op jit(solution)/shard_map/pallas_call | solution.py:323
  45.4 0.7 shard_map.98
  46.1 3.5 %shard_map.93 = (bf16[512,512]{1,0:T(8,128)(2,1)S(1)}, bf16[512,512]{1,0:T(8,128)(2,1)S(1)}) custom-call(bf16[512,2048]{1,0:T(8,128)(2,1)S(1)} %get-tuple-element.71.refs_0_, bf16[2048,512]{1,0:T(8,128)(2,1)S(1)} %copy-done.1, bf16[512,512]{1,0:T(8,128)(2,1)S(1)} %get-tuple-element.72.refs_2_, bf16[512,256]{1,0:T(8,128)(2,1)S(1)} %get-tuple-element.73.refs_3_.refs_5_, ...), custom_call_target="tpu_custom_call" | custom-call | flops 2147483648 | bytes 5308448 | tf_op jit(solution)/shard_map/pallas_call | solution.py:323
  49.7 1.8 %shard_map.99 = (f32[4,128,256]{2,1,0:T(8,128)S(1)}, f32[4,96,256]{2,1,0:T(8,128)S(1)}, f32[4,96,256]{2,1,0:T(8,128)S(1)}, f32[4,128,256]{2,1,0:T(8,128)S(1)}, f...) custom-call(bf16[512,512]{1,0:T(8,128)(2,1)S(1)} %get-tuple-element.70.refs_0_, ...), custom_call_target="tpu_custom_call" | custom-call | flops 1342177280 | bytes 7340032 | tf_op jit(solution)/shard_map/pallas_call | solution.py:323
  51.5 1.6 %collective-permute-start.11 = (f32[4,128,256]{2,1,0:T(8,128)S(1)}, f32[4,128,256]{2,1,0:T(8,128)S(1)}, u32[]{:S(2)}, u32[]{:S(2)}) collective-permute-start(f32[4,128,256]{2,1,0:T(8,128)S(1)} %get-tuple-element.94), channel_id=1, source_target_pairs={{0,2},{2,0},{4,6},{6,4},{1,3},{3,1},{5,7},{7,5},{8,10},{10,8},{12,... | collective-permute-start | bytes 1572872 | tf_op jit(solution)/shard_map/ppermute | solution.py:417
  53.0 2.1 %collective-permute-start.15 = (f32[4,96,256]{2,1,0:T(8,128)S(1)}, f32[4,96,256]{2,1,0:T(8,128)S(1)}, u32[]{:S(2)}, u32[]{:S(2)}) collective-permute-start(f32[4,96,256]{2,1,0:T(8,128)S(1)} %get-tuple-element.103), channel_id=1, source_target_pairs={{0,6},{6,0},{2,4},{4,2},{1,7},{7,1},{3,5},{5,3},{8,14},{14,8},{10,... | collective-permute-start | bytes 1179656 | tf_op jit(solution)/shard_map/ppermute | solution.py:417
  55.1 0.4 collective-permute-start.19
  55.5 1.2 %shard_map.101 = (f32[4,64,256]{2,1,0:T(8,128)S(1)}, f32[4,64,256]{2,1,0:T(8,128)S(1)}, f32[4,64,256]{2,1,0:T(8,128)S(1)}, f32[4,64,256]{2,1,0:T(8,128)S(1)}, f3...) custom-call(bf16[512,512]{1,0:T(8,128)(2,1)S(1)} %get-tuple-element.70.refs_0_, ...), custom_call_target="tpu_custom_call" | custom-call | flops 805306368 | bytes 7340032 | tf_op jit(solution)/shard_map/pallas_call | solution.py:323
  56.7 0.7 collective-permute-start.13
  57.3 0.6 collective-permute-start.17
  58.0 8.3 %collective-permute-done.11.came = f32[4,128,256]{2,1,0:T(8,128)S(1)} collective-permute-done((f32[4,128,256]{2,1,0:T(8,128)S(1)}, f32[4,128,256]{2,1,0:T(8,128)S(1)}, u32[]{:S(2)}, u32[]{:S(2)}) %collective-permute-start.11) | collective-permute-done | bytes 524320 | tf_op jit(solution)/shard_map/ppermute | solution.py:417
  66.3 0.4 collective-permute-start.21
  66.8 4.7 %collective-permute-done.13.came = f32[4,64,256]{2,1,0:T(8,128)S(1)} collective-permute-done((f32[4,64,256]{2,1,0:T(8,128)S(1)}, f32[4,64,256]{2,1,0:T(8,128)S(1)}, u32[]{:S(2)}, u32[]{:S(2)}) %collective-permute-start.13) | collective-permute-done | bytes 262176 | tf_op jit(solution)/shard_map/ppermute | solution.py:417
  71.5 2.8 %collective-permute-start.12 = (f32[2,128,256]{2,1,0:T(8,128)S(1)}, f32[2,128,256]{2,1,0:T(8,128)S(1)}, u32[]{:S(2)}, u32[]{:S(2)}) collective-permute-start(f32[2,128,256]{2,1,0:T(8,128)S(1)} %get-tuple-element.96), channel_id=1, source_target_pairs={{0,6},{6,0},{2,4},{4,2},{1,7},{7,1},{3,5},{5,3},{8,14},{14,8},{10,... | collective-permute-start | bytes 786440 | tf_op jit(solution)/shard_map/ppermute | solution.py:417
  74.3 0.6 collective-permute-start.14
  74.9 0.4 collective-permute-start.16
  75.4 0.4 collective-permute-start.20
  75.8 1.8 %collective-permute-start.18 = (f32[2,64,256]{2,1,0:T(8,128)S(1)}, f32[2,64,256]{2,1,0:T(8,128)S(1)}, u32[]{:S(2)}, u32[]{:S(2)}) collective-permute-start(f32[2,64,256]{2,1,0:T(8,128)S(1)} %get-tuple-element.109), channel_id=1, source_target_pairs={{0,1},{1,0},{2,3},{3,2},{4,5},{5,4},{6,7},{7,6},{8,9},{9,8},{10,11... | collective-permute-start | bytes 393224 | tf_op jit(solution)/shard_map/ppermute | solution.py:417
  77.6 5.7 %collective-permute-done.14.came_b = f32[2,64,256]{2,1,0:T(8,128)S(1)} collective-permute-done((f32[2,64,256]{2,1,0:T(8,128)S(1)}, f32[2,64,256]{2,1,0:T(8,128)S(1)}, u32[]{:S(2)}, u32[]{:S(2)}) %collective-permute-start.14) | collective-permute-done | bytes 131104 | tf_op jit(solution)/shard_map/ppermute | solution.py:417
  83.3 0.3 collective-permute-start.22
  83.6 0.4 collective-permute-start.23
  84.1 1.8 %collective-permute-start.24 = (f32[160,256]{1,0:T(8,128)S(1)}, f32[160,256]{1,0:T(8,128)S(1)}, u32[]{:S(2)}, u32[]{:S(2)}) collective-permute-start(f32[160,256]{1,0:T(8,128)S(1)} %get-tuple-element.121), channel_id=1, source_target_pairs={{0,2},{2,0},{4,6},{6,4},{1,3},{3,1},{5,7},{7,5},{8,10},{10,8},{12,... | collective-permute-start | bytes 491528 | tf_op jit(solution)/shard_map/ppermute | solution.py:417
  85.9 3.3 %collective-permute-done.22.came_b = f32[2,64,256]{2,1,0:T(8,128)S(1)} collective-permute-done((f32[2,64,256]{2,1,0:T(8,128)S(1)}, f32[2,64,256]{2,1,0:T(8,128)S(1)}, u32[]{:S(2)}, u32[]{:S(2)}) %collective-permute-start.22) | collective-permute-done | bytes 131104 | tf_op jit(solution)/shard_map/ppermute | solution.py:417
  89.3 2.8 %collective-permute-start.25 = (f32[160,256]{1,0:T(8,128)S(1)}, f32[160,256]{1,0:T(8,128)S(1)}, u32[]{:S(2)}, u32[]{:S(2)}) collective-permute-start(f32[160,256]{1,0:T(8,128)S(1)} %get-tuple-element.122), channel_id=1, source_target_pairs={{0,6},{6,0},{2,4},{4,2},{1,7},{7,1},{3,5},{5,3},{8,14},{14,8},{10,... | collective-permute-start | bytes 491528 | tf_op jit(solution)/shard_map/ppermute | solution.py:417
  92.1 3.8 %collective-permute-done.25.refs_5_ = f32[160,256]{1,0:T(8,128)S(1)} collective-permute-done((f32[160,256]{1,0:T(8,128)S(1)}, f32[160,256]{1,0:T(8,128)S(1)}, u32[]{:S(2)}, u32[]{:S(2)}) %collective-permute-start.25) | collective-permute-done | bytes 163872 | tf_op jit(solution)/shard_map/ppermute | solution.py:417
  95.9 0.8 shard_map.110
  (30 shorter events, 0.5 us)
Async XLA Ops:
  0.0 42.0 %copy-start.1 = (bf16[2048,512]{1,0:T(8,128)(2,1)S(1)}, bf16[2048,512]{1,0:T(8,128)(2,1)}, u32[]{:S(2)}) copy-start(bf16[2048,512]{1,0:T(8,128)(2,1)} %refs_1_.3) | copy-start | bytes 6291460
  0.0 42.0 %copy-start.2 = (f32[8]{0:T(128)S(1)}, f32[8]{0:T(128)}, u32[]{:S(2)}) copy-start(f32[8]{0:T(128)} %refs_7_.3) | copy-start | bytes 100
  7.7 1.6 %collective-permute-start = (f32[136,512]{1,0:T(8,128)S(1)}, f32[136,512]{1,0:T(8,128)S(1)}, u32[]{:S(2)}, u32[]{:S(2)}) collective-permute-start(f32[136,512]{1,0:T(8,128)S(1)} %get-tuple-element.78), channel_id=1, source_target_pairs={{0,8},{8,0},{1,9},{9,1},{2,10},{10,2},{3,11},{11,3},{4,12},{12,4},... | collective-permute-start | bytes 835592 | tf_op jit(solution)/shard_map/ppermute | solution.py:365
  9.4 5.0 %collective-permute-start.1 = (f32[136,128]{1,0:T(8,128)S(1)}, f32[136,128]{1,0:T(8,128)S(1)}, u32[]{:S(2)}, u32[]{:S(2)}) collective-permute-start(f32[136,128]{1,0:T(8,128)S(1)} %get-tuple-element.80), channel_id=1, source_target_pairs={{0,16},{16,32},{32,48},{48,0},{1,17},{17,33},{33,49},{49,1},{2,18}... | collective-permute-start | bytes 208904 | tf_op jit(solution)/shard_map/ppermute | solution.py:336
  11.1 6.3 %collective-permute-start.2 = (f32[136,128]{1,0:T(8,128)S(1)}, f32[136,128]{1,0:T(8,128)S(1)}, u32[]{:S(2)}, u32[]{:S(2)}) collective-permute-start(f32[136,128]{1,0:T(8,128)S(1)} %get-tuple-element.81), channel_id=1, source_target_pairs={{0,32},{16,48},{32,0},{48,16},{1,33},{17,49},{33,1},{49,17},{2,34}... | collective-permute-start | bytes 208904 | tf_op jit(solution)/shard_map/ppermute | solution.py:336
  13.8 4.4 %collective-permute-start.3 = (f32[136,128]{1,0:T(8,128)S(1)}, f32[136,128]{1,0:T(8,128)S(1)}, u32[]{:S(2)}, u32[]{:S(2)}) collective-permute-start(f32[136,128]{1,0:T(8,128)S(1)} %get-tuple-element.82), channel_id=1, source_target_pairs={{0,48},{16,0},{32,16},{48,32},{1,49},{17,1},{33,17},{49,33},{2,50}... | collective-permute-start | bytes 208904 | tf_op jit(solution)/shard_map/ppermute | solution.py:336
  18.2 13.0 %collective-permute-start.4 = (f32[136,128]{1,0:T(8,128)S(1)}, f32[136,128]{1,0:T(8,128)S(1)}, u32[]{:S(2)}, u32[]{:S(2)}) collective-permute-start(f32[136,128]{1,0:T(8,128)S(1)} %get-tuple-element.84), channel_id=1, source_target_pairs={{0,64},{64,128},{128,192},{72,8},{136,72},{200,136},{1,65},{65,129... | collective-permute-start | bytes 208904 | tf_op jit(solution)/shard_map/ppermute | solution.py:390
  22.6 9.2 %collective-permute-start.5 = (f32[136,128]{1,0:T(8,128)S(1)}, f32[136,128]{1,0:T(8,128)S(1)}, u32[]{:S(2)}, u32[]{:S(2)}) collective-permute-start(f32[136,128]{1,0:T(8,128)S(1)} %get-tuple-element.84), channel_id=1, source_target_pairs={{0,128},{64,192},{136,8},{200,72},{1,129},{65,193},{137,9},{201,73... | collective-permute-start | bytes 208904 | tf_op jit(solution)/shard_map/ppermute | solution.py:390
  29.9 3.9 %collective-permute-start.6 = (f32[136,128]{1,0:T(8,128)S(1)}, f32[136,128]{1,0:T(8,128)S(1)}, u32[]{:S(2)}, u32[]{:S(2)}) collective-permute-start(f32[136,128]{1,0:T(8,128)S(1)} %get-tuple-element.84), channel_id=1, source_target_pairs={{0,192},{200,8},{1,193},{201,9},{2,194},{202,10},{3,195},{203,11},... | collective-permute-start | bytes 208904 | tf_op jit(solution)/shard_map/ppermute | solution.py:390
  33.9 5.5 %collective-permute-start.7 = (f32[128,128]{1,0:T(8,128)S(1)}, f32[128,128]{1,0:T(8,128)S(1)}, u32[]{:S(2)}, u32[]{:S(2)}) collective-permute-start(f32[128,128]{1,0:T(8,128)S(1)} %get-tuple-element.86), channel_id=1, source_target_pairs={{0,16},{16,32},{32,48},{48,0},{1,17},{17,33},{33,49},{49,1},{2,18}... | collective-permute-start | bytes 196616 | tf_op jit(solution)/shard_map/ppermute | solution.py:336
  35.2 5.8 %collective-permute-start.8 = (f32[128,128]{1,0:T(8,128)S(1)}, f32[128,128]{1,0:T(8,128)S(1)}, u32[]{:S(2)}, u32[]{:S(2)}) collective-permute-start(f32[128,128]{1,0:T(8,128)S(1)} %get-tuple-element.87), channel_id=1, source_target_pairs={{0,32},{16,48},{32,0},{48,16},{1,33},{17,49},{33,1},{49,17},{2,34}... | collective-permute-start | bytes 196616 | tf_op jit(solution)/shard_map/ppermute | solution.py:336
  37.4 4.3 %collective-permute-start.9 = (f32[128,128]{1,0:T(8,128)S(1)}, f32[128,128]{1,0:T(8,128)S(1)}, u32[]{:S(2)}, u32[]{:S(2)}) collective-permute-start(f32[128,128]{1,0:T(8,128)S(1)} %get-tuple-element.88), channel_id=1, source_target_pairs={{0,48},{16,0},{32,16},{48,32},{1,49},{17,1},{33,17},{49,33},{2,50}... | collective-permute-start | bytes 196616 | tf_op jit(solution)/shard_map/ppermute | solution.py:336
  41.7 7.9 %collective-permute-start.10 = (f32[128,512]{1,0:T(8,128)S(1)}, f32[128,512]{1,0:T(8,128)S(1)}, u32[]{:S(2)}, u32[]{:S(2)}) collective-permute-start(f32[128,512]{1,0:T(8,128)S(1)} %get-tuple-element.90), channel_id=1, source_target_pairs={{0,8},{8,0},{1,9},{9,1},{2,10},{10,2},{3,11},{11,3},{4,12},{12,4},... | collective-permute-start | bytes 786440 | tf_op jit(solution)/shard_map/ppermute | solution.py:401
  42.0 3.3 %copy-start = (bf16[512,2048]{1,0:T(8,128)(2,1)S(1)}, bf16[512,2048]{1,0:T(8,128)(2,1)}, u32[]{:S(2)}) copy-start(bf16[512,2048]{1,0:T(8,128)(2,1)} %out_w.1) | copy-start | bytes 6291460
  51.5 14.9 %collective-permute-start.11 = (f32[4,128,256]{2,1,0:T(8,128)S(1)}, f32[4,128,256]{2,1,0:T(8,128)S(1)}, u32[]{:S(2)}, u32[]{:S(2)}) collective-permute-start(f32[4,128,256]{2,1,0:T(8,128)S(1)} %get-tuple-element.94), channel_id=1, source_target_pairs={{0,2},{2,0},{4,6},{6,4},{1,3},{3,1},{5,7},{7,5},{8,10},{10,8},{12,... | collective-permute-start | bytes 1572872 | tf_op jit(solution)/shard_map/ppermute | solution.py:417
  53.0 21.2 %collective-permute-start.15 = (f32[4,96,256]{2,1,0:T(8,128)S(1)}, f32[4,96,256]{2,1,0:T(8,128)S(1)}, u32[]{:S(2)}, u32[]{:S(2)}) collective-permute-start(f32[4,96,256]{2,1,0:T(8,128)S(1)} %get-tuple-element.103), channel_id=1, source_target_pairs={{0,6},{6,0},{2,4},{4,2},{1,7},{7,1},{3,5},{5,3},{8,14},{14,8},{10,... | collective-permute-start | bytes 1179656 | tf_op jit(solution)/shard_map/ppermute | solution.py:417
  55.1 19.7 %collective-permute-start.19 = (f32[4,96,256]{2,1,0:T(8,128)S(1)}, f32[4,96,256]{2,1,0:T(8,128)S(1)}, u32[]{:S(2)}, u32[]{:S(2)}) collective-permute-start(f32[4,96,256]{2,1,0:T(8,128)S(1)} %get-tuple-element.112), channel_id=1, source_target_pairs={{0,1},{1,0},{2,3},{3,2},{4,5},{5,4},{6,7},{7,6},{8,9},{9,8},{10,11... | collective-permute-start | bytes 1179656 | tf_op jit(solution)/shard_map/ppermute | solution.py:417
  56.7 14.8 %collective-permute-start.13 = (f32[4,64,256]{2,1,0:T(8,128)S(1)}, f32[4,64,256]{2,1,0:T(8,128)S(1)}, u32[]{:S(2)}, u32[]{:S(2)}) collective-permute-start(f32[4,64,256]{2,1,0:T(8,128)S(1)} %get-tuple-element.98), channel_id=1, source_target_pairs={{0,2},{2,0},{4,6},{6,4},{1,3},{3,1},{5,7},{7,5},{8,10},{10,8},{12,... | collective-permute-start | bytes 786440 | tf_op jit(solution)/shard_map/ppermute | solution.py:417
  57.3 18.0 %collective-permute-start.17 = (f32[4,64,256]{2,1,0:T(8,128)S(1)}, f32[4,64,256]{2,1,0:T(8,128)S(1)}, u32[]{:S(2)}, u32[]{:S(2)}) collective-permute-start(f32[4,64,256]{2,1,0:T(8,128)S(1)} %get-tuple-element.107), channel_id=1, source_target_pairs={{0,6},{6,0},{2,4},{4,2},{1,7},{7,1},{3,5},{5,3},{8,14},{14,8},{10,... | collective-permute-start | bytes 786440 | tf_op jit(solution)/shard_map/ppermute | solution.py:417
  66.3 9.4 %collective-permute-start.21 = (f32[4,64,256]{2,1,0:T(8,128)S(1)}, f32[4,64,256]{2,1,0:T(8,128)S(1)}, u32[]{:S(2)}, u32[]{:S(2)}) collective-permute-start(f32[4,64,256]{2,1,0:T(8,128)S(1)} %get-tuple-element.116), channel_id=1, source_target_pairs={{0,1},{1,0},{2,3},{3,2},{4,5},{5,4},{6,7},{7,6},{8,9},{9,8},{10,11... | collective-permute-start | bytes 786440 | tf_op jit(solution)/shard_map/ppermute | solution.py:417
  71.5 12.1 %collective-permute-start.12 = (f32[2,128,256]{2,1,0:T(8,128)S(1)}, f32[2,128,256]{2,1,0:T(8,128)S(1)}, u32[]{:S(2)}, u32[]{:S(2)}) collective-permute-start(f32[2,128,256]{2,1,0:T(8,128)S(1)} %get-tuple-element.96), channel_id=1, source_target_pairs={{0,6},{6,0},{2,4},{4,2},{1,7},{7,1},{3,5},{5,3},{8,14},{14,8},{10,... | collective-permute-start | bytes 786440 | tf_op jit(solution)/shard_map/ppermute | solution.py:417
  74.3 9.0 %collective-permute-start.14 = (f32[2,64,256]{2,1,0:T(8,128)S(1)}, f32[2,64,256]{2,1,0:T(8,128)S(1)}, u32[]{:S(2)}, u32[]{:S(2)}) collective-permute-start(f32[2,64,256]{2,1,0:T(8,128)S(1)} %get-tuple-element.100), channel_id=1, source_target_pairs={{0,6},{6,0},{2,4},{4,2},{1,7},{7,1},{3,5},{5,3},{8,14},{14,8},{10,... | collective-permute-start | bytes 393224 | tf_op jit(solution)/shard_map/ppermute | solution.py:417
  74.9 9.2 %collective-permute-start.16 = (f32[2,96,256]{2,1,0:T(8,128)S(1)}, f32[2,96,256]{2,1,0:T(8,128)S(1)}, u32[]{:S(2)}, u32[]{:S(2)}) collective-permute-start(f32[2,96,256]{2,1,0:T(8,128)S(1)} %get-tuple-element.105), channel_id=1, source_target_pairs={{0,1},{1,0},{2,3},{3,2},{4,5},{5,4},{6,7},{7,6},{8,9},{9,8},{10,11... | collective-permute-start | bytes 589832 | tf_op jit(solution)/shard_map/ppermute | solution.py:417
  75.4 13.8 %collective-permute-start.20 = (f32[2,96,256]{2,1,0:T(8,128)S(1)}, f32[2,96,256]{2,1,0:T(8,128)S(1)}, u32[]{:S(2)}, u32[]{:S(2)}) collective-permute-start(f32[2,96,256]{2,1,0:T(8,128)S(1)} %get-tuple-element.114), channel_id=1, source_target_pairs={{0,2},{2,0},{4,6},{6,4},{1,3},{3,1},{5,7},{7,5},{8,10},{10,8},{12,... | collective-permute-start | bytes 589832 | tf_op jit(solution)/shard_map/ppermute | solution.py:417
  75.8 8.3 %collective-permute-start.18 = (f32[2,64,256]{2,1,0:T(8,128)S(1)}, f32[2,64,256]{2,1,0:T(8,128)S(1)}, u32[]{:S(2)}, u32[]{:S(2)}) collective-permute-start(f32[2,64,256]{2,1,0:T(8,128)S(1)} %get-tuple-element.109), channel_id=1, source_target_pairs={{0,1},{1,0},{2,3},{3,2},{4,5},{5,4},{6,7},{7,6},{8,9},{9,8},{10,11... | collective-permute-start | bytes 393224 | tf_op jit(solution)/shard_map/ppermute | solution.py:417
  83.3 5.9 %collective-permute-start.22 = (f32[2,64,256]{2,1,0:T(8,128)S(1)}, f32[2,64,256]{2,1,0:T(8,128)S(1)}, u32[]{:S(2)}, u32[]{:S(2)}) collective-permute-start(f32[2,64,256]{2,1,0:T(8,128)S(1)} %get-tuple-element.118), channel_id=1, source_target_pairs={{0,2},{2,0},{4,6},{6,4},{1,3},{3,1},{5,7},{7,5},{8,10},{10,8},{12,... | collective-permute-start | bytes 393224 | tf_op jit(solution)/shard_map/ppermute | solution.py:417
  83.6 12.2 %collective-permute-start.23 = (f32[192,256]{1,0:T(8,128)S(1)}, f32[192,256]{1,0:T(8,128)S(1)}, u32[]{:S(2)}, u32[]{:S(2)}) collective-permute-start(f32[192,256]{1,0:T(8,128)S(1)} %get-tuple-element.120), channel_id=1, source_target_pairs={{0,1},{1,0},{2,3},{3,2},{4,5},{5,4},{6,7},{7,6},{8,9},{9,8},{10,11... | collective-permute-start | bytes 589832 | tf_op jit(solution)/shard_map/ppermute | solution.py:417
  84.1 8.0 %collective-permute-start.24 = (f32[160,256]{1,0:T(8,128)S(1)}, f32[160,256]{1,0:T(8,128)S(1)}, u32[]{:S(2)}, u32[]{:S(2)}) collective-permute-start(f32[160,256]{1,0:T(8,128)S(1)} %get-tuple-element.121), channel_id=1, source_target_pairs={{0,2},{2,0},{4,6},{6,4},{1,3},{3,1},{5,7},{7,5},{8,10},{10,8},{12,... | collective-permute-start | bytes 491528 | tf_op jit(solution)/shard_map/ppermute | solution.py:417
  89.3 6.6 %collective-permute-start.25 = (f32[160,256]{1,0:T(8,128)S(1)}, f32[160,256]{1,0:T(8,128)S(1)}, u32[]{:S(2)}, u32[]{:S(2)}) collective-permute-start(f32[160,256]{1,0:T(8,128)S(1)} %get-tuple-element.122), channel_id=1, source_target_pairs={{0,6},{6,0},{2,4},{4,2},{1,7},{7,1},{3,5},{5,3},{8,14},{14,8},{10,... | collective-permute-start | bytes 491528 | tf_op jit(solution)/shard_map/ppermute | solution.py:417

commit v4 on v2

--- a/solution.py
+++ b/solution.py
@@ -114,7 +114,10 @@
         send[at, :] = jnp.where(mine, state[half:], state[:half])
 
 
-def inside_kernel(b, source, gate_w, inputs, proj, step, log, log_cols, gain, base, slope, pair):
+def inside_kernel(
+    b, halves, source, gate_w, inputs, proj, step, log, log_cols, gain, *rest
+):
+    outs, pair = rest[:-1], rest[-1]
     rows = source.shape[0]
     heads = gain.shape[0]
     width = gate_w.shape[1] // heads
@@ -127,36 +130,41 @@
     lane = lax.broadcasted_iota(jnp.int32, (block, 128), 1)
     r = lax.broadcasted_iota(jnp.int32, (block, block), 0)
     c = lax.broadcasted_iota(jnp.int32, (block, block), 1)
-    pick = head_pick(heads, width, F32)
-    gain_row = jnp.sum(pick * head_column(gain, heads), axis=0, keepdims=True)
-    pick = pick.astype(BF16)
-    gates = dot(source[...], gate_w[...]).astype(BF16).astype(F32)
-    gates = gates / (1.0 + jnp.exp(-gates))
-    values = inputs[...].astype(F32)
-    steps = dot(step[mine, :].astype(BF16), pick, ((0,), (0,)))
-    scaled = (values * steps).astype(BF16)
-    ahead = dot(jnp.exp(log[mine, :]).astype(BF16), pick, ((0,), (0,)))
-    slope[...] = (ahead * gates).astype(BF16)
-    for k in range(count):
-        at = slice(k * block, (k + 1) * block)
-        lo, hi = (k * block, rows) if later else (0, (k + 1) * block)
-        for p in range(heads // 2):
-            cols = slice(p * 128, (p + 1) * 128)
-            found = []
-            for h in (2 * p, 2 * p + 1):
-                row = b * heads + h
-                mixed = []
-                for s in range(lo // block, hi // block):
-                    span = slice(s * block, (s + 1) * block)
-                    spread = log_cols[at, row : row + 1] - log[row : row + 1, span]
-                    if s == k:
-                        spread = jnp.where((c >= r) if later else (c <= r), spread, F32(-1e30))
-                    mixed.append((pair[at, span] * jnp.exp(spread)).astype(BF16))
-                mixed = jnp.concatenate(mixed, axis=1) if len(mixed) > 1 else mixed[0]
-                found.append(dot(mixed, scaled[lo:hi, cols]))
-            inside = jnp.where(lane < width, found[0], found[1])
-            total = inside + gain_row[:, cols] * values[at, cols]
-            base[at, cols] = (total * gates[at, cols]).astype(BF16)
+    every_pick = head_pick(heads, width, F32)
+    for n, half in enumerate(halves):
+        base, slope = outs[2 * n], outs[2 * n + 1]
+        half_cols = slice(half * heads // 2 * width, (half + 1) * heads // 2 * width)
+        pick = every_pick[:, half_cols]
+        gain_row = jnp.sum(pick * head_column(gain, heads), axis=0, keepdims=True)
+        pick = pick.astype(BF16)
+        gates = dot(source[...], gate_w[:, half_cols]).astype(BF16).astype(F32)
+        gates = gates / (1.0 + jnp.exp(-gates))
+        values = inputs[:, half_cols].astype(F32)
+        steps = dot(step[mine, :].astype(BF16), pick, ((0,), (0,)))
+        scaled = (values * steps).astype(BF16)
+        ahead = dot(jnp.exp(log[mine, :]).astype(BF16), pick, ((0,), (0,)))
+        slope[...] = (ahead * gates).astype(BF16)
+        for k in range(count):
+            at = slice(k * block, (k + 1) * block)
+            lo, hi = (k * block, rows) if later else (0, (k + 1) * block)
+            for p in range(heads // 4):
+                cols = slice(p * 128, (p + 1) * 128)
+                found = []
+                for h in (2 * p, 2 * p + 1):
+                    row = b * heads + half * heads // 2 + h
+                    mixed = []
+                    for s in range(lo // block, hi // block):
+                        span = slice(s * block, (s + 1) * block)
+                        spread = log_cols[at, row : row + 1] - log[row : row + 1, span]
+                        if s == k:
+                            seen = (c >= r) if later else (c <= r)
+                            spread = jnp.where(seen, spread, F32(-1e30))
+                        mixed.append((pair[at, span] * jnp.exp(spread)).astype(BF16))
+                    mixed = jnp.concatenate(mixed, axis=1) if len(mixed) > 1 else mixed[0]
+                    found.append(dot(mixed, scaled[lo:hi, cols]))
+                inside = jnp.where(lane < width, found[0], found[1])
+                total = inside + gain_row[:, cols] * values[at, cols]
+                base[at, cols] = (total * gates[at, cols]).astype(BF16)
 
 
 def flip_kernel(out_w, plain, flipped):
@@ -279,7 +287,8 @@
 
 
 def output_kernel(
-    first_row, base_f, base_b, slope_f, slope_b, proj_f, proj_b, carry, got, plain, flipped, *outs
+    first_row, base_f0, slope_f0, base_f1, slope_f1, base_b0, slope_b0, base_b1, slope_b1,
+    proj_f, proj_b, carry, got, plain, flipped, *outs
 ):
     count = sum(out.shape[1] for out in outs[:3])
     at = slice(first_row, first_row + count)
@@ -287,14 +296,18 @@
     half = size // 2
     low_core = lax.axis_index("core") == 0
     gated = []
-    for b, base, slope, proj in ((0, base_f, slope_f, proj_f), (1, base_b, slope_b, proj_b)):
+    for b, halves, proj in (
+        (0, ((base_f0, slope_f0), (base_f1, slope_f1)), proj_f),
+        (1, ((base_b0, slope_b0), (base_b1, slope_b1)), proj_b),
+    ):
         rows = slice(b * half, (b + 1) * half)
         low = jnp.where(low_core, carry[rows, :], got[rows, :])
         high = jnp.where(low_core, got[rows, :], carry[rows, :])
         entering = jnp.concatenate([low, high], axis=0).astype(BF16)
         carried = dot(proj[at, size:], entering)
-        total = base[at, :].astype(F32) + slope[at, :].astype(F32) * carried
-        gated.append(total.astype(BF16))
+        base = jnp.concatenate([a[at, :] for a, _ in halves], axis=1).astype(F32)
+        slope = jnp.concatenate([a[at, :] for _, a in halves], axis=1).astype(F32)
+        gated.append((base + slope * carried).astype(BF16))
     for q in (7, 6, 5, 3, 4, 2, 1, 0):
         bits = [(q >> n) & 1 for n in range(3)]
         j = target_block(q)
@@ -392,18 +405,21 @@
     swap = [(0, 1), (1, 0)]
     other = lax.ppermute(send, "core", swap)
 
-    def inside(b, source, inputs, proj):
+    def inside(b, halves, source, inputs, proj):
         return call(
-            lambda *refs: inside_kernel(b, *refs),
+            lambda *refs: inside_kernel(b, halves, *refs),
             (source, gate_weight, inputs, proj, step, log, log_cols, skip_gain),
-            [near(wide, BF16)] * 2,
+            [near((rows, inner // 2), BF16)] * (2 * len(halves)),
             specs=[VMEM_SPEC] * 7 + [SMEM_SPEC],
             scratch=[pltpu.VMEM((rows, rows), F32)],
-            flops=4 * rows * width * inner,
+            flops=2 * rows * width * inner * len(halves),
         )
 
-    base_f, slope_f = inside(0, seq, in_f, proj_f)
-    base_b, slope_b = inside(1, rev, in_b, proj_b)
+    inner_parts = [
+        *inside(0, (0, 1), seq, in_f, proj_f),
+        *inside(1, (0,), rev, in_b, proj_b),
+        *inside(1, (1,), rev, in_b, proj_b),
+    ]
     blocks = (8, inner, width // 8)
     plain, flipped = call(
         flip_kernel, (output_weight,), [near(blocks, BF16)] * 2, flops=inner * width * 512
@@ -425,11 +441,11 @@
     arrived = lax.ppermute(give, "core", swap)
 
     first_row, parts = 0, []
-    counts = ((112, 112, 96), (64, 64, 64))
+    counts = ((128, 96, 96), (64, 64, 64))
     for group in range(2):
         outs = call(
             lambda *refs, at=first_row: output_kernel(at, *refs),
-            (base_f, base_b, slope_f, slope_b, proj_f, proj_b, carry, arrived, plain, flipped),
+            (*inner_parts, proj_f, proj_b, carry, arrived, plain, flipped),
             [near((4, r, width // 8)) for r in counts[group]] * 2,
             flops=4 * sum(counts[group]) * inner * width,
         )

time: 94.1 us -> 94.2 us (level)
  starting transfers between devices: 40.9 us -> 39.6 us
  Pallas kernels: 19.6 us -> 20.7 us
    ppermute x9, waiting for transfers between devices: 8.86 us -> 6.75 us  [shifted(): lax.ppermute(v, axis, [(j, (j + k) % 4) for j in range(4)])]
    ppermute x15, waiting for transfers between devices: 22.8 us -> 24.6 us  [travel(): return lax.ppermute(value, axis, pairs)]
    ppermute x15, starting transfers between devices: 19.4 us -> 18.3 us  [travel(): return lax.ppermute(value, axis, pairs)]
    pallas_call x20 -> x21, Pallas kernels: 19.6 us -> 20.7 us  [call(): pl.pallas_call(kernel, out_shape=outs, in_specs=specs, out_specs=[VMEM_SP...]
  transfers between devices with their start and end apart: 26 -> 26, of which waited for: 11 -> 10; matrix products, arithmetic and copies ran while one was open for 0% -> 0% of each run, Pallas kernels for 10% -> 11%
where the time goes in v4:
time: 94.2 us; the launch traced here: 93.4 us
  starting transfers between devices  39.6 us (42%)
  waiting for transfers between devices  32.9 us (35%)
  Pallas kernels  20.7 us (22%)
    ppermute x15, waiting for transfers between devices, travel(): return lax.ppermute(value, axis, pairs)  24.6 us
    ppermute x9, starting transfers between devices, shifted(): lax.ppermute(v, axis, [(j, (j + k) % 4) for j in range(4)])  21.1 us
    pallas_call x21, Pallas kernels, call(): pl.pallas_call(kernel, out_shape=outs, in_specs=specs, out_specs=[VMEM_SP...  20.7 us
    ppermute x15, starting transfers between devices, travel(): return lax.ppermute(value, axis, pairs)  18.3 us
    ppermute x9, waiting for transfers between devices, shifted(): lax.ppermute(v, axis, [(j, (j + k) % 4) for j in range(4)])  6.75 us
  transfers between devices with their start and end apart: 26, of which 10 were waited for; matrix products, arithmetic and copies ran while one was open for 0% of the time, Pallas kernels for 11%

profile of v4, /device:TPU:8, one launch (start us, length us, event | category | flops | bytes accessed | tf_op | source)
XLA Modules:
  0.0 93.4 jit_solution(11098528188695590627)
XLA Ops:
  0.0 7.5 %shard_map.91 = (bf16[512,2048]{1,0:T(8,128)(2,1)S(1)}, bf16[512,2048]{1,0:T(8,128)(2,1)S(1)}, bf16[512,512]{1,0:T(8,128)(2,1)S(1)}, bf16[512,512]{1,0:T(8,128)(...) custom-call(bf16[512,2048]{1,0:T(8,128)(2,1)} %seq_hbm.1, ...), custom_call_target="tpu_custom_call" | custom-call | flops 3221225472 | bytes 5275712 | tf_op jit(solution)/shard_map/pallas_call | solution.py:364
  7.5 0.1 collective-permute-start
  7.6 1.5 %collective-permute-done.got.other = f32[136,512]{1,0:T(8,128)S(1)} collective-permute-done((f32[136,512]{1,0:T(8,128)S(1)}, f32[136,512]{1,0:T(8,128)S(1)}, u32[]{:S(2)}, u32[]{:S(2)}) %collective-permute-start) | collective-permute-done | bytes 278560 | tf_op jit(solution)/shard_map/ppermute | solution.py:406
  9.2 0.1 shard_map.95
  9.3 1.7 %collective-permute-start.1 = (f32[136,128]{1,0:T(8,128)S(1)}, f32[136,128]{1,0:T(8,128)S(1)}, u32[]{:S(2)}, u32[]{:S(2)}) collective-permute-start(f32[136,128]{1,0:T(8,128)S(1)} %get-tuple-element.90), channel_id=1, source_target_pairs={{0,16},{16,32},{32,48},{48,0},{1,17},{17,33},{33,49},{49,1},{2,18}... | collective-permute-start | bytes 208904 | tf_op jit(solution)/shard_map/ppermute | solution.py:377
  10.9 2.6 %collective-permute-start.2 = (f32[136,128]{1,0:T(8,128)S(1)}, f32[136,128]{1,0:T(8,128)S(1)}, u32[]{:S(2)}, u32[]{:S(2)}) collective-permute-start(f32[136,128]{1,0:T(8,128)S(1)} %get-tuple-element.91), channel_id=1, source_target_pairs={{0,32},{16,48},{32,0},{48,16},{1,33},{17,49},{33,1},{49,17},{2,34}... | collective-permute-start | bytes 208904 | tf_op jit(solution)/shard_map/ppermute | solution.py:377
  13.6 0.7 collective-permute-start.3
  14.3 2.9 %collective-permute-done.2.got2 = f32[136,128]{1,0:T(8,128)S(1)} collective-permute-done((f32[136,128]{1,0:T(8,128)S(1)}, f32[136,128]{1,0:T(8,128)S(1)}, u32[]{:S(2)}, u32[]{:S(2)}) %collective-permute-start.2) | collective-permute-done | bytes 69664 | tf_op jit(solution)/shard_map/ppermute | solution.py:377
  17.2 0.8 collective-permute-done.3.got3
  18.1 2.5 %collective-permute-start.4 = (f32[72,128]{1,0:T(8,128)S(1)}, f32[72,128]{1,0:T(8,128)S(1)}, u32[]{:S(2)}, u32[]{:S(2)}) collective-permute-start(f32[72,128]{1,0:T(8,128)S(1)} %get-tuple-element.94), channel_id=1, source_target_pairs={{0,64},{64,128},{128,192},{192,0},{1,65},{65,129},{129,193},{193,1... | collective-permute-start | bytes 110600 | tf_op jit(solution)/shard_map/ppermute | solution.py:377
  20.6 5.4 %collective-permute-start.5 = (f32[72,128]{1,0:T(8,128)S(1)}, f32[72,128]{1,0:T(8,128)S(1)}, u32[]{:S(2)}, u32[]{:S(2)}) collective-permute-start(f32[72,128]{1,0:T(8,128)S(1)} %get-tuple-element.95), channel_id=1, source_target_pairs={{0,128},{64,192},{128,0},{192,64},{1,129},{65,193},{129,1},{193,65... | collective-permute-start | bytes 110600 | tf_op jit(solution)/shard_map/ppermute | solution.py:377
  26.0 2.7 %collective-permute-start.6 = (f32[72,128]{1,0:T(8,128)S(1)}, f32[72,128]{1,0:T(8,128)S(1)}, u32[]{:S(2)}, u32[]{:S(2)}) collective-permute-start(f32[72,128]{1,0:T(8,128)S(1)} %get-tuple-element.96), channel_id=1, source_target_pairs={{0,192},{64,0},{128,64},{192,128},{1,193},{65,1},{129,65},{193,129... | collective-permute-start | bytes 110600 | tf_op jit(solution)/shard_map/ppermute | solution.py:377
  28.7 2.2 %collective-permute-done.6.got3 = f32[72,128]{1,0:T(8,128)S(1)} collective-permute-done((f32[72,128]{1,0:T(8,128)S(1)}, f32[72,128]{1,0:T(8,128)S(1)}, u32[]{:S(2)}, u32[]{:S(2)}) %collective-permute-start.6) | collective-permute-done | bytes 36896 | tf_op jit(solution)/shard_map/ppermute | solution.py:377
  30.9 0.1 shard_map.97
  30.9 1.5 %collective-permute-start.7 = (f32[128,128]{1,0:T(8,128)S(1)}, f32[128,128]{1,0:T(8,128)S(1)}, u32[]{:S(2)}, u32[]{:S(2)}) collective-permute-start(f32[128,128]{1,0:T(8,128)S(1)} %get-tuple-element.98), channel_id=1, source_target_pairs={{0,16},{16,32},{32,48},{48,0},{1,17},{17,33},{33,49},{49,1},{2,18}... | collective-permute-start | bytes 196616 | tf_op jit(solution)/shard_map/ppermute | solution.py:377
  32.4 2.8 %collective-permute-start.8 = (f32[128,128]{1,0:T(8,128)S(1)}, f32[128,128]{1,0:T(8,128)S(1)}, u32[]{:S(2)}, u32[]{:S(2)}) collective-permute-start(f32[128,128]{1,0:T(8,128)S(1)} %get-tuple-element.99), channel_id=1, source_target_pairs={{0,32},{16,48},{32,0},{48,16},{1,33},{17,49},{33,1},{49,17},{2,34}... | collective-permute-start | bytes 196616 | tf_op jit(solution)/shard_map/ppermute | solution.py:377
  35.2 1.2 %collective-permute-start.9 = (f32[128,128]{1,0:T(8,128)S(1)}, f32[128,128]{1,0:T(8,128)S(1)}, u32[]{:S(2)}, u32[]{:S(2)}) collective-permute-start(f32[128,128]{1,0:T(8,128)S(1)} %get-tuple-element.100), channel_id=1, source_target_pairs={{0,48},{16,0},{32,16},{48,32},{1,49},{17,1},{33,17},{49,33},{2,50}... | collective-permute-start | bytes 196616 | tf_op jit(solution)/shard_map/ppermute | solution.py:377
  36.4 2.2 %shard_map.93 = (bf16[512,256]{1,0:T(8,128)(2,1)S(1)}, bf16[512,256]{1,0:T(8,128)(2,1)S(1)}) custom-call(bf16[512,2048]{1,0:T(8,128)(2,1)S(1)} %get-tuple-element.80.refs_0_, bf16[2048,512]{1,0:T(8,128)(2,1)S(1)} %copy-done, bf16[512,512]{1,0:T(8,128)(2,1)S(1)} %get-tuple-element.81.refs_2_, bf16[512,256]{1,0:T(8,128)(2,1)S(1)} %get-tuple-element.82.refs_3_.refs_9_, ...), custom_call_target="tpu_custom_call" | custom-call | flops 1073741824 | bytes 5308448 | tf_op jit(solution)/shard_map/pallas_call | solution.py:364
  38.6 0.9 collective-permute-done.9.got3
  39.5 0.1 shard_map.98
  39.6 0.1 collective-permute-start.10
  39.7 2.2 %shard_map.94 = (bf16[512,256]{1,0:T(8,128)(2,1)S(1)}, bf16[512,256]{1,0:T(8,128)(2,1)S(1)}) custom-call(bf16[512,2048]{1,0:T(8,128)(2,1)S(1)} %get-tuple-element.80.refs_0_, bf16[2048,512]{1,0:T(8,128)(2,1)S(1)} %copy-done, bf16[512,512]{1,0:T(8,128)(2,1)S(1)} %get-tuple-element.81.refs_2_, bf16[512,256]{1,0:T(8,128)(2,1)S(1)} %get-tuple-element.82.refs_3_.refs_9_, ...), custom_call_target="tpu_custom_call" | custom-call | flops 1073741824 | bytes 5308448 | tf_op jit(solution)/shard_map/pallas_call | solution.py:364
  41.9 0.7 shard_map.99
  42.6 3.7 %shard_map.92 = (bf16[512,256]{1,0:T(8,128)(2,1)S(1)}, bf16[512,256]{1,0:T(8,128)(2,1)S(1)}, bf16[512,256]{1,0:T(8,128)(2,1)S(1)}, bf16[512,256]{1,0:T(8,128)(2,1)S(1)}) custom-call(bf16[512,2048]{1,0:T(8,128)(2,1)S(1)} %get-tuple-element.70.refs_0_, bf16[2048,512]{1,0:T(8,128)(2,1)S(1)} %copy-done, bf16[512,512]{1,0:T(8,128)(2,1)S(1)} %get-tuple-element.71.refs_2_, ...), custom_call_target="tpu_custom_call" | custom-call | flops 2147483648 | bytes 5308448 | tf_op jit(solution)/shard_map/pallas_call | solution.py:364
  46.3 1.8 %shard_map.100 = (f32[4,128,256]{2,1,0:T(8,128)S(1)}, f32[4,96,256]{2,1,0:T(8,128)S(1)}, f32[4,96,256]{2,1,0:T(8,128)S(1)}, f32[4,128,256]{2,1,0:T(8,128)S(1)}, ...) custom-call(bf16[512,256]{1,0:T(8,128)(2,1)S(1)} %get-tuple-element.76.refs_0_, ...), custom_call_target="tpu_custom_call" | custom-call | flops 1342177280 | bytes 7340032 | tf_op jit(solution)/shard_map/pallas_call | solution.py:364
  48.1 1.6 %collective-permute-start.11 = (f32[4,128,256]{2,1,0:T(8,128)S(1)}, f32[4,128,256]{2,1,0:T(8,128)S(1)}, u32[]{:S(2)}, u32[]{:S(2)}) collective-permute-start(f32[4,128,256]{2,1,0:T(8,128)S(1)} %get-tuple-element.106), channel_id=1, source_target_pairs={{0,2},{2,0},{4,6},{6,4},{1,3},{3,1},{5,7},{7,5},{8,10},{10,8},{12,... | collective-permute-start | bytes 1572872 | tf_op jit(solution)/shard_map/ppermute | solution.py:457
  49.7 2.1 %collective-permute-start.15 = (f32[4,96,256]{2,1,0:T(8,128)S(1)}, f32[4,96,256]{2,1,0:T(8,128)S(1)}, u32[]{:S(2)}, u32[]{:S(2)}) collective-permute-start(f32[4,96,256]{2,1,0:T(8,128)S(1)} %get-tuple-element.115), channel_id=1, source_target_pairs={{0,6},{6,0},{2,4},{4,2},{1,7},{7,1},{3,5},{5,3},{8,14},{14,8},{10,... | collective-permute-start | bytes 1179656 | tf_op jit(solution)/shard_map/ppermute | solution.py:457
  51.8 0.7 collective-permute-start.19
  52.5 1.2 %shard_map.102 = (f32[4,64,256]{2,1,0:T(8,128)S(1)}, f32[4,64,256]{2,1,0:T(8,128)S(1)}, f32[4,64,256]{2,1,0:T(8,128)S(1)}, f32[4,64,256]{2,1,0:T(8,128)S(1)}, f3...) custom-call(bf16[512,256]{1,0:T(8,128)(2,1)S(1)} %get-tuple-element.76.refs_0_, ...), custom_call_target="tpu_custom_call" | custom-call | flops 805306368 | bytes 7340032 | tf_op jit(solution)/shard_map/pallas_call | solution.py:364
  53.7 0.7 collective-permute-start.13
  54.4 0.9 collective-permute-start.17
  55.2 7.8 %collective-permute-done.11.came = f32[4,128,256]{2,1,0:T(8,128)S(1)} collective-permute-done((f32[4,128,256]{2,1,0:T(8,128)S(1)}, f32[4,128,256]{2,1,0:T(8,128)S(1)}, u32[]{:S(2)}, u32[]{:S(2)}) %collective-permute-start.11) | collective-permute-done | bytes 524320 | tf_op jit(solution)/shard_map/ppermute | solution.py:457
  63.0 0.7 collective-permute-start.21
  63.7 0.1 shard_map.101
  63.8 4.4 %collective-permute-done.13.came = f32[4,64,256]{2,1,0:T(8,128)S(1)} collective-permute-done((f32[4,64,256]{2,1,0:T(8,128)S(1)}, f32[4,64,256]{2,1,0:T(8,128)S(1)}, u32[]{:S(2)}, u32[]{:S(2)}) %collective-permute-start.13) | collective-permute-done | bytes 262176 | tf_op jit(solution)/shard_map/ppermute | solution.py:457
  68.2 2.8 %collective-permute-start.12 = (f32[2,128,256]{2,1,0:T(8,128)S(1)}, f32[2,128,256]{2,1,0:T(8,128)S(1)}, u32[]{:S(2)}, u32[]{:S(2)}) collective-permute-start(f32[2,128,256]{2,1,0:T(8,128)S(1)} %get-tuple-element.108), channel_id=1, source_target_pairs={{0,6},{6,0},{2,4},{4,2},{1,7},{7,1},{3,5},{5,3},{8,14},{14,8},{10,... | collective-permute-start | bytes 786440 | tf_op jit(solution)/shard_map/ppermute | solution.py:457
  71.0 0.6 collective-permute-start.14
  71.6 0.8 collective-permute-start.16
  72.4 0.4 collective-permute-start.20
  72.8 1.4 %collective-permute-start.18 = (f32[2,64,256]{2,1,0:T(8,128)S(1)}, f32[2,64,256]{2,1,0:T(8,128)S(1)}, u32[]{:S(2)}, u32[]{:S(2)}) collective-permute-start(f32[2,64,256]{2,1,0:T(8,128)S(1)} %get-tuple-element.121), channel_id=1, source_target_pairs={{0,1},{1,0},{2,3},{3,2},{4,5},{5,4},{6,7},{7,6},{8,9},{9,8},{10,11... | collective-permute-start | bytes 393224 | tf_op jit(solution)/shard_map/ppermute | solution.py:457
  74.3 5.7 %collective-permute-done.14.came_b = f32[2,64,256]{2,1,0:T(8,128)S(1)} collective-permute-done((f32[2,64,256]{2,1,0:T(8,128)S(1)}, f32[2,64,256]{2,1,0:T(8,128)S(1)}, u32[]{:S(2)}, u32[]{:S(2)}) %collective-permute-start.14) | collective-permute-done | bytes 131104 | tf_op jit(solution)/shard_map/ppermute | solution.py:457
  80.0 0.3 collective-permute-start.22
  80.4 0.8 collective-permute-start.23
  81.2 1.8 %collective-permute-start.24 = (f32[160,256]{1,0:T(8,128)S(1)}, f32[160,256]{1,0:T(8,128)S(1)}, u32[]{:S(2)}, u32[]{:S(2)}) collective-permute-start(f32[160,256]{1,0:T(8,128)S(1)} %get-tuple-element.133), channel_id=1, source_target_pairs={{0,2},{2,0},{4,6},{6,4},{1,3},{3,1},{5,7},{7,5},{8,10},{10,8},{12,... | collective-permute-start | bytes 491528 | tf_op jit(solution)/shard_map/ppermute | solution.py:457
  83.0 2.9 %collective-permute-done.22.came_b = f32[2,64,256]{2,1,0:T(8,128)S(1)} collective-permute-done((f32[2,64,256]{2,1,0:T(8,128)S(1)}, f32[2,64,256]{2,1,0:T(8,128)S(1)}, u32[]{:S(2)}, u32[]{:S(2)}) %collective-permute-start.22) | collective-permute-done | bytes 131104 | tf_op jit(solution)/shard_map/ppermute | solution.py:457
  86.0 2.8 %collective-permute-start.25 = (f32[160,256]{1,0:T(8,128)S(1)}, f32[160,256]{1,0:T(8,128)S(1)}, u32[]{:S(2)}, u32[]{:S(2)}) collective-permute-start(f32[160,256]{1,0:T(8,128)S(1)} %get-tuple-element.134), channel_id=1, source_target_pairs={{0,6},{6,0},{2,4},{4,2},{1,7},{7,1},{3,5},{5,3},{8,14},{14,8},{10,... | collective-permute-start | bytes 491528 | tf_op jit(solution)/shard_map/ppermute | solution.py:457
  88.9 3.8 %collective-permute-done.25.refs_5_ = f32[160,256]{1,0:T(8,128)S(1)} collective-permute-done((f32[160,256]{1,0:T(8,128)S(1)}, f32[160,256]{1,0:T(8,128)S(1)}, u32[]{:S(2)}, u32[]{:S(2)}) %collective-permute-start.25) | collective-permute-done | bytes 163872 | tf_op jit(solution)/shard_map/ppermute | solution.py:457
  92.6 0.8 shard_map.111
  (31 shorter events, 0.4 us)
Async XLA Ops:
  0.0 36.4 %copy-start = (bf16[2048,512]{1,0:T(8,128)(2,1)S(1)}, bf16[2048,512]{1,0:T(8,128)(2,1)}, u32[]{:S(2)}) copy-start(bf16[2048,512]{1,0:T(8,128)(2,1)} %refs_1_.5) | copy-start | bytes 6291460
  0.0 36.4 %copy-start.2 = (f32[8]{0:T(128)S(1)}, f32[8]{0:T(128)}, u32[]{:S(2)}) copy-start(f32[8]{0:T(128)} %refs_7_.5) | copy-start | bytes 100
  7.5 1.6 %collective-permute-start = (f32[136,512]{1,0:T(8,128)S(1)}, f32[136,512]{1,0:T(8,128)S(1)}, u32[]{:S(2)}, u32[]{:S(2)}) collective-permute-start(f32[136,512]{1,0:T(8,128)S(1)} %get-tuple-element.88), channel_id=1, source_target_pairs={{0,8},{8,0},{1,9},{9,1},{2,10},{10,2},{3,11},{11,3},{4,12},{12,4},... | collective-permute-start | bytes 835592 | tf_op jit(solution)/shard_map/ppermute | solution.py:406
  9.3 5.0 %collective-permute-start.1 = (f32[136,128]{1,0:T(8,128)S(1)}, f32[136,128]{1,0:T(8,128)S(1)}, u32[]{:S(2)}, u32[]{:S(2)}) collective-permute-start(f32[136,128]{1,0:T(8,128)S(1)} %get-tuple-element.90), channel_id=1, source_target_pairs={{0,16},{16,32},{32,48},{48,0},{1,17},{17,33},{33,49},{49,1},{2,18}... | collective-permute-start | bytes 208904 | tf_op jit(solution)/shard_map/ppermute | solution.py:377
  10.9 6.3 %collective-permute-start.2 = (f32[136,128]{1,0:T(8,128)S(1)}, f32[136,128]{1,0:T(8,128)S(1)}, u32[]{:S(2)}, u32[]{:S(2)}) collective-permute-start(f32[136,128]{1,0:T(8,128)S(1)} %get-tuple-element.91), channel_id=1, source_target_pairs={{0,32},{16,48},{32,0},{48,16},{1,33},{17,49},{33,1},{49,17},{2,34}... | collective-permute-start | bytes 208904 | tf_op jit(solution)/shard_map/ppermute | solution.py:377
  13.6 4.4 %collective-permute-start.3 = (f32[136,128]{1,0:T(8,128)S(1)}, f32[136,128]{1,0:T(8,128)S(1)}, u32[]{:S(2)}, u32[]{:S(2)}) collective-permute-start(f32[136,128]{1,0:T(8,128)S(1)} %get-tuple-element.92), channel_id=1, source_target_pairs={{0,48},{16,0},{32,16},{48,32},{1,49},{17,1},{33,17},{49,33},{2,50}... | collective-permute-start | bytes 208904 | tf_op jit(solution)/shard_map/ppermute | solution.py:377
  18.1 10.6 %collective-permute-start.4 = (f32[72,128]{1,0:T(8,128)S(1)}, f32[72,128]{1,0:T(8,128)S(1)}, u32[]{:S(2)}, u32[]{:S(2)}) collective-permute-start(f32[72,128]{1,0:T(8,128)S(1)} %get-tuple-element.94), channel_id=1, source_target_pairs={{0,64},{64,128},{128,192},{192,0},{1,65},{65,129},{129,193},{193,1... | collective-permute-start | bytes 110600 | tf_op jit(solution)/shard_map/ppermute | solution.py:377
  20.6 8.1 %collective-permute-start.5 = (f32[72,128]{1,0:T(8,128)S(1)}, f32[72,128]{1,0:T(8,128)S(1)}, u32[]{:S(2)}, u32[]{:S(2)}) collective-permute-start(f32[72,128]{1,0:T(8,128)S(1)} %get-tuple-element.95), channel_id=1, source_target_pairs={{0,128},{64,192},{128,0},{192,64},{1,129},{65,193},{129,1},{193,65... | collective-permute-start | bytes 110600 | tf_op jit(solution)/shard_map/ppermute | solution.py:377
  26.0 4.9 %collective-permute-start.6 = (f32[72,128]{1,0:T(8,128)S(1)}, f32[72,128]{1,0:T(8,128)S(1)}, u32[]{:S(2)}, u32[]{:S(2)}) collective-permute-start(f32[72,128]{1,0:T(8,128)S(1)} %get-tuple-element.96), channel_id=1, source_target_pairs={{0,192},{64,0},{128,64},{192,128},{1,193},{65,1},{129,65},{193,129... | collective-permute-start | bytes 110600 | tf_op jit(solution)/shard_map/ppermute | solution.py:377
  30.9 7.7 %collective-permute-start.7 = (f32[128,128]{1,0:T(8,128)S(1)}, f32[128,128]{1,0:T(8,128)S(1)}, u32[]{:S(2)}, u32[]{:S(2)}) collective-permute-start(f32[128,128]{1,0:T(8,128)S(1)} %get-tuple-element.98), channel_id=1, source_target_pairs={{0,16},{16,32},{32,48},{48,0},{1,17},{17,33},{33,49},{49,1},{2,18}... | collective-permute-start | bytes 196616 | tf_op jit(solution)/shard_map/ppermute | solution.py:377
  32.4 6.2 %collective-permute-start.8 = (f32[128,128]{1,0:T(8,128)S(1)}, f32[128,128]{1,0:T(8,128)S(1)}, u32[]{:S(2)}, u32[]{:S(2)}) collective-permute-start(f32[128,128]{1,0:T(8,128)S(1)} %get-tuple-element.99), channel_id=1, source_target_pairs={{0,32},{16,48},{32,0},{48,16},{1,33},{17,49},{33,1},{49,17},{2,34}... | collective-permute-start | bytes 196616 | tf_op jit(solution)/shard_map/ppermute | solution.py:377
  35.2 4.3 %collective-permute-start.9 = (f32[128,128]{1,0:T(8,128)S(1)}, f32[128,128]{1,0:T(8,128)S(1)}, u32[]{:S(2)}, u32[]{:S(2)}) collective-permute-start(f32[128,128]{1,0:T(8,128)S(1)} %get-tuple-element.100), channel_id=1, source_target_pairs={{0,48},{16,0},{32,16},{48,32},{1,49},{17,1},{33,17},{49,33},{2,50}... | collective-permute-start | bytes 196616 | tf_op jit(solution)/shard_map/ppermute | solution.py:377
  39.6 2.3 %copy-start.1 = (bf16[512,2048]{1,0:T(8,128)(2,1)S(1)}, bf16[512,2048]{1,0:T(8,128)(2,1)}, u32[]{:S(2)}) copy-start(bf16[512,2048]{1,0:T(8,128)(2,1)} %out_w.1) | copy-start | bytes 6291460
  39.6 6.7 %collective-permute-start.10 = (f32[128,512]{1,0:T(8,128)S(1)}, f32[128,512]{1,0:T(8,128)S(1)}, u32[]{:S(2)}, u32[]{:S(2)}) collective-permute-start(f32[128,512]{1,0:T(8,128)S(1)} %get-tuple-element.102), channel_id=1, source_target_pairs={{0,8},{8,0},{1,9},{9,1},{2,10},{10,2},{3,11},{11,3},{4,12},{12,4},... | collective-permute-start | bytes 786440 | tf_op jit(solution)/shard_map/ppermute | solution.py:441
  48.1 14.9 %collective-permute-start.11 = (f32[4,128,256]{2,1,0:T(8,128)S(1)}, f32[4,128,256]{2,1,0:T(8,128)S(1)}, u32[]{:S(2)}, u32[]{:S(2)}) collective-permute-start(f32[4,128,256]{2,1,0:T(8,128)S(1)} %get-tuple-element.106), channel_id=1, source_target_pairs={{0,2},{2,0},{4,6},{6,4},{1,3},{3,1},{5,7},{7,5},{8,10},{10,8},{12,... | collective-permute-start | bytes 1572872 | tf_op jit(solution)/shard_map/ppermute | solution.py:457
  49.7 21.2 %collective-permute-start.15 = (f32[4,96,256]{2,1,0:T(8,128)S(1)}, f32[4,96,256]{2,1,0:T(8,128)S(1)}, u32[]{:S(2)}, u32[]{:S(2)}) collective-permute-start(f32[4,96,256]{2,1,0:T(8,128)S(1)} %get-tuple-element.115), channel_id=1, source_target_pairs={{0,6},{6,0},{2,4},{4,2},{1,7},{7,1},{3,5},{5,3},{8,14},{14,8},{10,... | collective-permute-start | bytes 1179656 | tf_op jit(solution)/shard_map/ppermute | solution.py:457
  51.8 19.8 %collective-permute-start.19 = (f32[4,96,256]{2,1,0:T(8,128)S(1)}, f32[4,96,256]{2,1,0:T(8,128)S(1)}, u32[]{:S(2)}, u32[]{:S(2)}) collective-permute-start(f32[4,96,256]{2,1,0:T(8,128)S(1)} %get-tuple-element.124), channel_id=1, source_target_pairs={{0,1},{1,0},{2,3},{3,2},{4,5},{5,4},{6,7},{7,6},{8,9},{9,8},{10,11... | collective-permute-start | bytes 1179656 | tf_op jit(solution)/shard_map/ppermute | solution.py:457
  53.7 14.5 %collective-permute-start.13 = (f32[4,64,256]{2,1,0:T(8,128)S(1)}, f32[4,64,256]{2,1,0:T(8,128)S(1)}, u32[]{:S(2)}, u32[]{:S(2)}) collective-permute-start(f32[4,64,256]{2,1,0:T(8,128)S(1)} %get-tuple-element.110), channel_id=1, source_target_pairs={{0,2},{2,0},{4,6},{6,4},{1,3},{3,1},{5,7},{7,5},{8,10},{10,8},{12,... | collective-permute-start | bytes 786440 | tf_op jit(solution)/shard_map/ppermute | solution.py:457
  54.4 18.0 %collective-permute-start.17 = (f32[4,64,256]{2,1,0:T(8,128)S(1)}, f32[4,64,256]{2,1,0:T(8,128)S(1)}, u32[]{:S(2)}, u32[]{:S(2)}) collective-permute-start(f32[4,64,256]{2,1,0:T(8,128)S(1)} %get-tuple-element.119), channel_id=1, source_target_pairs={{0,6},{6,0},{2,4},{4,2},{1,7},{7,1},{3,5},{5,3},{8,14},{14,8},{10,... | collective-permute-start | bytes 786440 | tf_op jit(solution)/shard_map/ppermute | solution.py:457
  63.0 9.8 %collective-permute-start.21 = (f32[4,64,256]{2,1,0:T(8,128)S(1)}, f32[4,64,256]{2,1,0:T(8,128)S(1)}, u32[]{:S(2)}, u32[]{:S(2)}) collective-permute-start(f32[4,64,256]{2,1,0:T(8,128)S(1)} %get-tuple-element.128), channel_id=1, source_target_pairs={{0,1},{1,0},{2,3},{3,2},{4,5},{5,4},{6,7},{7,6},{8,9},{9,8},{10,11... | collective-permute-start | bytes 786440 | tf_op jit(solution)/shard_map/ppermute | solution.py:457
  68.2 12.2 %collective-permute-start.12 = (f32[2,128,256]{2,1,0:T(8,128)S(1)}, f32[2,128,256]{2,1,0:T(8,128)S(1)}, u32[]{:S(2)}, u32[]{:S(2)}) collective-permute-start(f32[2,128,256]{2,1,0:T(8,128)S(1)} %get-tuple-element.108), channel_id=1, source_target_pairs={{0,6},{6,0},{2,4},{4,2},{1,7},{7,1},{3,5},{5,3},{8,14},{14,8},{10,... | collective-permute-start | bytes 786440 | tf_op jit(solution)/shard_map/ppermute | solution.py:457
  71.0 9.1 %collective-permute-start.14 = (f32[2,64,256]{2,1,0:T(8,128)S(1)}, f32[2,64,256]{2,1,0:T(8,128)S(1)}, u32[]{:S(2)}, u32[]{:S(2)}) collective-permute-start(f32[2,64,256]{2,1,0:T(8,128)S(1)} %get-tuple-element.112), channel_id=1, source_target_pairs={{0,6},{6,0},{2,4},{4,2},{1,7},{7,1},{3,5},{5,3},{8,14},{14,8},{10,... | collective-permute-start | bytes 393224 | tf_op jit(solution)/shard_map/ppermute | solution.py:457
  71.6 9.6 %collective-permute-start.16 = (f32[2,96,256]{2,1,0:T(8,128)S(1)}, f32[2,96,256]{2,1,0:T(8,128)S(1)}, u32[]{:S(2)}, u32[]{:S(2)}) collective-permute-start(f32[2,96,256]{2,1,0:T(8,128)S(1)} %get-tuple-element.117), channel_id=1, source_target_pairs={{0,1},{1,0},{2,3},{3,2},{4,5},{5,4},{6,7},{7,6},{8,9},{9,8},{10,11... | collective-permute-start | bytes 589832 | tf_op jit(solution)/shard_map/ppermute | solution.py:457
  72.4 13.5 %collective-permute-start.20 = (f32[2,96,256]{2,1,0:T(8,128)S(1)}, f32[2,96,256]{2,1,0:T(8,128)S(1)}, u32[]{:S(2)}, u32[]{:S(2)}) collective-permute-start(f32[2,96,256]{2,1,0:T(8,128)S(1)} %get-tuple-element.126), channel_id=1, source_target_pairs={{0,2},{2,0},{4,6},{6,4},{1,3},{3,1},{5,7},{7,5},{8,10},{10,8},{12,... | collective-permute-start | bytes 589832 | tf_op jit(solution)/shard_map/ppermute | solution.py:457
  72.8 8.3 %collective-permute-start.18 = (f32[2,64,256]{2,1,0:T(8,128)S(1)}, f32[2,64,256]{2,1,0:T(8,128)S(1)}, u32[]{:S(2)}, u32[]{:S(2)}) collective-permute-start(f32[2,64,256]{2,1,0:T(8,128)S(1)} %get-tuple-element.121), channel_id=1, source_target_pairs={{0,1},{1,0},{2,3},{3,2},{4,5},{5,4},{6,7},{7,6},{8,9},{9,8},{10,11... | collective-permute-start | bytes 393224 | tf_op jit(solution)/shard_map/ppermute | solution.py:457
  80.0 5.9 %collective-permute-start.22 = (f32[2,64,256]{2,1,0:T(8,128)S(1)}, f32[2,64,256]{2,1,0:T(8,128)S(1)}, u32[]{:S(2)}, u32[]{:S(2)}) collective-permute-start(f32[2,64,256]{2,1,0:T(8,128)S(1)} %get-tuple-element.130), channel_id=1, source_target_pairs={{0,2},{2,0},{4,6},{6,4},{1,3},{3,1},{5,7},{7,5},{8,10},{10,8},{12,... | collective-permute-start | bytes 393224 | tf_op jit(solution)/shard_map/ppermute | solution.py:457
  80.4 12.3 %collective-permute-start.23 = (f32[192,256]{1,0:T(8,128)S(1)}, f32[192,256]{1,0:T(8,128)S(1)}, u32[]{:S(2)}, u32[]{:S(2)}) collective-permute-start(f32[192,256]{1,0:T(8,128)S(1)} %get-tuple-element.132), channel_id=1, source_target_pairs={{0,1},{1,0},{2,3},{3,2},{4,5},{5,4},{6,7},{7,6},{8,9},{9,8},{10,11... | collective-permute-start | bytes 589832 | tf_op jit(solution)/shard_map/ppermute | solution.py:457
  81.2 7.7 %collective-permute-start.24 = (f32[160,256]{1,0:T(8,128)S(1)}, f32[160,256]{1,0:T(8,128)S(1)}, u32[]{:S(2)}, u32[]{:S(2)}) collective-permute-start(f32[160,256]{1,0:T(8,128)S(1)} %get-tuple-element.133), channel_id=1, source_target_pairs={{0,2},{2,0},{4,6},{6,4},{1,3},{3,1},{5,7},{7,5},{8,10},{10,8},{12,... | collective-permute-start | bytes 491528 | tf_op jit(solution)/shard_map/ppermute | solution.py:457
  86.0 6.6 %collective-permute-start.25 = (f32[160,256]{1,0:T(8,128)S(1)}, f32[160,256]{1,0:T(8,128)S(1)}, u32[]{:S(2)}, u32[]{:S(2)}) collective-permute-start(f32[160,256]{1,0:T(8,128)S(1)} %get-tuple-element.134), channel_id=1, source_target_pairs={{0,6},{6,0},{2,4},{4,2},{1,7},{7,1},{3,5},{5,3},{8,14},{14,8},{10,... | collective-permute-start | bytes 491528 | tf_op jit(solution)/shard_map/ppermute | solution.py:457

commit v5 on v4

--- a/solution.py
+++ b/solution.py
@@ -114,19 +114,30 @@
         send[at, :] = jnp.where(mine, state[half:], state[:half])
 
 
+def affinities(proj):
+    size = proj.shape[1] // 2
+    return dot(proj[:, size:], proj[:, :size], ((1,), (1,)))
+
+
+def early_kernel(source, gate_w, proj, pair, gates):
+    pair[...] = affinities(proj)
+    gates[...] = dot(source[...], gate_w[:, : gates.shape[1]]).astype(BF16)
+
+
 def inside_kernel(
-    b, halves, source, gate_w, inputs, proj, step, log, log_cols, gain, *rest
+    b, halves, ready, source, gate_w, inputs, proj, step, log, log_cols, gain, *rest
 ):
-    outs, pair = rest[:-1], rest[-1]
+    early, outs = rest[:ready], rest[ready:]
     rows = source.shape[0]
     heads = gain.shape[0]
     width = gate_w.shape[1] // heads
-    size = proj.shape[1] // 2
     block = 128
     count = rows // block
     later = b == 1
     mine = slice(b * heads, (b + 1) * heads)
-    pair[...] = dot(proj[:, size:], proj[:, :size], ((1,), (1,)))
+    pair = early[0] if early else outs[-1]
+    if not early:
+        pair[...] = affinities(proj)
     lane = lax.broadcasted_iota(jnp.int32, (block, 128), 1)
     r = lax.broadcasted_iota(jnp.int32, (block, block), 0)
     c = lax.broadcasted_iota(jnp.int32, (block, block), 1)
@@ -137,7 +148,10 @@
         pick = every_pick[:, half_cols]
         gain_row = jnp.sum(pick * head_column(gain, heads), axis=0, keepdims=True)
         pick = pick.astype(BF16)
-        gates = dot(source[...], gate_w[:, half_cols]).astype(BF16).astype(F32)
+        if ready == 2 and half == 0:
+            gates = early[1][...].astype(F32)
+        else:
+            gates = dot(source[...], gate_w[:, half_cols]).astype(BF16).astype(F32)
         gates = gates / (1.0 + jnp.exp(-gates))
         values = inputs[:, half_cols].astype(F32)
         steps = dot(step[mine, :].astype(BF16), pick, ((0,), (0,)))
@@ -405,20 +419,26 @@
     swap = [(0, 1), (1, 0)]
     other = lax.ppermute(send, "core", swap)
 
-    def inside(b, halves, source, inputs, proj):
+    half_wide, square = near((rows, inner // 2), BF16), near((rows, rows))
+    early = call(
+        early_kernel, (seq, gate_weight, proj_f), [square, half_wide],
+        flops=rows * width * inner,
+    )
+
+    def inside(b, halves, ready, source, inputs, proj):
         return call(
-            lambda *refs: inside_kernel(b, halves, *refs),
-            (source, gate_weight, inputs, proj, step, log, log_cols, skip_gain),
-            [near((rows, inner // 2), BF16)] * (2 * len(halves)),
-            specs=[VMEM_SPEC] * 7 + [SMEM_SPEC],
-            scratch=[pltpu.VMEM((rows, rows), F32)],
+            lambda *refs: inside_kernel(b, halves, len(ready), *refs),
+            (source, gate_weight, inputs, proj, step, log, log_cols, skip_gain, *ready),
+            [half_wide] * (2 * len(halves)) + [square] * (not ready),
+            specs=[VMEM_SPEC] * 7 + [SMEM_SPEC] + [VMEM_SPEC] * len(ready),
             flops=2 * rows * width * inner * len(halves),
         )
 
+    *first_half, pair_b = inside(1, (0,), (), rev, in_b, proj_b)
     inner_parts = [
-        *inside(0, (0, 1), seq, in_f, proj_f),
-        *inside(1, (0,), rev, in_b, proj_b),
-        *inside(1, (1,), rev, in_b, proj_b),
+        *inside(0, (0, 1), early, seq, in_f, proj_f),
+        *first_half,
+        *inside(1, (1,), (pair_b,), rev, in_b, proj_b),
     ]
     blocks = (8, inner, width // 8)
     plain, flipped = call(
@@ -441,7 +461,7 @@
     arrived = lax.ppermute(give, "core", swap)
 
     first_row, parts = 0, []
-    counts = ((128, 96, 96), (64, 64, 64))
+    counts = ((112, 96, 96), (80, 64, 64))
     for group in range(2):
         outs = call(
             lambda *refs, at=first_row: output_kernel(at, *refs),

time: 94.2 us -> 91.5 us (0.971)
  waiting for transfers between devices: 32.9 us -> 28.4 us
  starting transfers between devices: 39.6 us -> 41.9 us
    ppermute x15, waiting for transfers between devices: 24.6 us -> 22.2 us  [travel(): return lax.ppermute(value, axis, pairs)]
    ppermute x15, starting transfers between devices: 18.3 us -> 20.6 us  [travel(): return lax.ppermute(value, axis, pairs)]
    ppermute x9, waiting for transfers between devices: 6.75 us -> 4.67 us  [shifted(): lax.ppermute(v, axis, [(j, (j + k) % 4) for j in range(4)])]
    pallas_call x21 -> x22, Pallas kernels: 20.7 us -> 20.6 us  [call(): pl.pallas_call(kernel, out_shape=outs, in_specs=specs, out_specs=[VMEM_SP...]
where the time goes in v5:
time: 91.5 us; the launch traced here: 91.2 us
  starting transfers between devices  41.9 us (46%)
  waiting for transfers between devices  28.4 us (31%)
  Pallas kernels  20.6 us (23%)
    ppermute x15, waiting for transfers between devices, travel(): return lax.ppermute(value, axis, pairs)  22.2 us
    ppermute x9, starting transfers between devices, shifted(): lax.ppermute(v, axis, [(j, (j + k) % 4) for j in range(4)])  21.1 us
    pallas_call x22, Pallas kernels, call(): pl.pallas_call(kernel, out_shape=outs, in_specs=specs, out_specs=[VMEM_SP...  20.6 us
    ppermute x15, starting transfers between devices, travel(): return lax.ppermute(value, axis, pairs)  20.6 us
    ppermute x9, waiting for transfers between devices, shifted(): lax.ppermute(v, axis, [(j, (j + k) % 4) for j in range(4)])  4.67 us
  transfers between devices with their start and end apart: 26, of which 10 were waited for; matrix products, arithmetic and copies ran while one was open for 0% of the time, Pallas kernels for 11%

profile of v5, /device:TPU:8, one launch (start us, length us, event | category | flops | bytes accessed | tf_op | source)
XLA Modules:
  0.0 91.2 jit_solution(17320027558605441445)
XLA Ops:
  0.0 7.5 %shard_map.91 = (bf16[512,2048]{1,0:T(8,128)(2,1)S(1)}, bf16[512,2048]{1,0:T(8,128)(2,1)S(1)}, bf16[512,512]{1,0:T(8,128)(2,1)S(1)}, bf16[512,512]{1,0:T(8,128)(...) custom-call(bf16[512,2048]{1,0:T(8,128)(2,1)} %seq_hbm.1, ...), custom_call_target="tpu_custom_call" | custom-call | flops 3221225472 | bytes 5275712 | tf_op jit(solution)/shard_map/pallas_call | solution.py:378
  7.6 0.1 collective-permute-start
  7.7 1.5 %collective-permute-done.got.other = f32[136,512]{1,0:T(8,128)S(1)} collective-permute-done((f32[136,512]{1,0:T(8,128)S(1)}, f32[136,512]{1,0:T(8,128)S(1)}, u32[]{:S(2)}, u32[]{:S(2)}) %collective-permute-start) | collective-permute-done | bytes 278560 | tf_op jit(solution)/shard_map/ppermute | solution.py:420
  9.2 0.1 shard_map.96
  9.3 1.7 %collective-permute-start.1 = (f32[136,128]{1,0:T(8,128)S(1)}, f32[136,128]{1,0:T(8,128)S(1)}, u32[]{:S(2)}, u32[]{:S(2)}) collective-permute-start(f32[136,128]{1,0:T(8,128)S(1)} %get-tuple-element.96), channel_id=1, source_target_pairs={{0,16},{16,32},{32,48},{48,0},{1,17},{17,33},{33,49},{49,1},{2,18}... | collective-permute-start | bytes 208904 | tf_op jit(solution)/shard_map/ppermute | solution.py:391
  10.9 2.6 %collective-permute-start.2 = (f32[136,128]{1,0:T(8,128)S(1)}, f32[136,128]{1,0:T(8,128)S(1)}, u32[]{:S(2)}, u32[]{:S(2)}) collective-permute-start(f32[136,128]{1,0:T(8,128)S(1)} %get-tuple-element.97), channel_id=1, source_target_pairs={{0,32},{16,48},{32,0},{48,16},{1,33},{17,49},{33,1},{49,17},{2,34}... | collective-permute-start | bytes 208904 | tf_op jit(solution)/shard_map/ppermute | solution.py:391
  13.6 0.7 collective-permute-start.3
  14.3 2.9 %collective-permute-done.2.got2 = f32[136,128]{1,0:T(8,128)S(1)} collective-permute-done((f32[136,128]{1,0:T(8,128)S(1)}, f32[136,128]{1,0:T(8,128)S(1)}, u32[]{:S(2)}, u32[]{:S(2)}) %collective-permute-start.2) | collective-permute-done | bytes 69664 | tf_op jit(solution)/shard_map/ppermute | solution.py:391
  17.2 0.8 collective-permute-done.3.got3
  18.1 2.5 %collective-permute-start.4 = (f32[72,128]{1,0:T(8,128)S(1)}, f32[72,128]{1,0:T(8,128)S(1)}, u32[]{:S(2)}, u32[]{:S(2)}) collective-permute-start(f32[72,128]{1,0:T(8,128)S(1)} %get-tuple-element.100), channel_id=1, source_target_pairs={{0,64},{64,128},{128,192},{192,0},{1,65},{65,129},{129,193},{193,1... | collective-permute-start | bytes 110600 | tf_op jit(solution)/shard_map/ppermute | solution.py:391
  20.6 5.4 %collective-permute-start.5 = (f32[72,128]{1,0:T(8,128)S(1)}, f32[72,128]{1,0:T(8,128)S(1)}, u32[]{:S(2)}, u32[]{:S(2)}) collective-permute-start(f32[72,128]{1,0:T(8,128)S(1)} %get-tuple-element.101), channel_id=1, source_target_pairs={{0,128},{64,192},{128,0},{192,64},{1,129},{65,193},{129,1},{193,65... | collective-permute-start | bytes 110600 | tf_op jit(solution)/shard_map/ppermute | solution.py:391
  26.0 2.7 %collective-permute-start.6 = (f32[72,128]{1,0:T(8,128)S(1)}, f32[72,128]{1,0:T(8,128)S(1)}, u32[]{:S(2)}, u32[]{:S(2)}) collective-permute-start(f32[72,128]{1,0:T(8,128)S(1)} %get-tuple-element.102), channel_id=1, source_target_pairs={{0,192},{64,0},{128,64},{192,128},{1,193},{65,1},{129,65},{193,129... | collective-permute-start | bytes 110600 | tf_op jit(solution)/shard_map/ppermute | solution.py:391
  28.7 2.3 %shard_map.94 = (bf16[512,256]{1,0:T(8,128)(2,1)S(1)}, bf16[512,256]{1,0:T(8,128)(2,1)S(1)}, f32[512,512]{1,0:T(8,128)S(1)}) custom-call(bf16[512,2048]{1,0:T(8,128)(2,1)S(1)} %get-tuple-element.85.refs_0_, bf16[2048,512]{1,0:T(8,128)(2,1)S(1)} %copy-done, bf16[512,512]{1,0:T(8,128)(2,1)S(1)} %get-tuple-element.86.refs_2_, ...), custom_call_target="tpu_custom_call" | custom-call | flops 1073741824 | bytes 5308448 | tf_op jit(solution)/shard_map/pallas_call | solution.py:378
  31.0 0.1 shard_map.98
  31.1 1.4 %collective-permute-start.7 = (f32[128,128]{1,0:T(8,128)S(1)}, f32[128,128]{1,0:T(8,128)S(1)}, u32[]{:S(2)}, u32[]{:S(2)}) collective-permute-start(f32[128,128]{1,0:T(8,128)S(1)} %get-tuple-element.104), channel_id=1, source_target_pairs={{0,16},{16,32},{32,48},{48,0},{1,17},{17,33},{33,49},{49,1},{2,18}... | collective-permute-start | bytes 196616 | tf_op jit(solution)/shard_map/ppermute | solution.py:391
  32.4 2.8 %collective-permute-start.8 = (f32[128,128]{1,0:T(8,128)S(1)}, f32[128,128]{1,0:T(8,128)S(1)}, u32[]{:S(2)}, u32[]{:S(2)}) collective-permute-start(f32[128,128]{1,0:T(8,128)S(1)} %get-tuple-element.105), channel_id=1, source_target_pairs={{0,32},{16,48},{32,0},{48,16},{1,33},{17,49},{33,1},{49,17},{2,34}... | collective-permute-start | bytes 196616 | tf_op jit(solution)/shard_map/ppermute | solution.py:391
  35.2 1.3 %collective-permute-start.9 = (f32[128,128]{1,0:T(8,128)S(1)}, f32[128,128]{1,0:T(8,128)S(1)}, u32[]{:S(2)}, u32[]{:S(2)}) collective-permute-start(f32[128,128]{1,0:T(8,128)S(1)} %get-tuple-element.106), channel_id=1, source_target_pairs={{0,48},{16,0},{32,16},{48,32},{1,49},{17,1},{33,17},{49,33},{2,50}... | collective-permute-start | bytes 196616 | tf_op jit(solution)/shard_map/ppermute | solution.py:391
  36.6 2.0 %shard_map.95 = (bf16[512,256]{1,0:T(8,128)(2,1)S(1)}, bf16[512,256]{1,0:T(8,128)(2,1)S(1)}) custom-call(bf16[512,2048]{1,0:T(8,128)(2,1)S(1)} %get-tuple-element.85.refs_0_, bf16[2048,512]{1,0:T(8,128)(2,1)S(1)} %copy-done, bf16[512,512]{1,0:T(8,128)(2,1)S(1)} %get-tuple-element.86.refs_2_, bf16[512,256]{1,0:T(8,128)(2,1)S(1)} %get-tuple-element.87.refs_3_.refs_9_, ...), custom_call_target="tpu_custom_call" | custom-call | flops 1073741824 | bytes 6357024 | tf_op jit(solution)/shard_map/pallas_call | solution.py:378
  38.6 1.0 %collective-permute-done.9.got3 = f32[128,128]{1,0:T(8,128)S(1)} collective-permute-done((f32[128,128]{1,0:T(8,128)S(1)}, f32[128,128]{1,0:T(8,128)S(1)}, u32[]{:S(2)}, u32[]{:S(2)}) %collective-permute-start.9) | collective-permute-done | bytes 65568 | tf_op jit(solution)/shard_map/ppermute | solution.py:391
  39.5 0.1 shard_map.99
  39.6 0.1 collective-permute-start.10
  39.7 0.7 shard_map.100
  40.5 0.9 shard_map.92
  41.3 2.9 %shard_map.93 = (bf16[512,256]{1,0:T(8,128)(2,1)S(1)}, bf16[512,256]{1,0:T(8,128)(2,1)S(1)}, bf16[512,256]{1,0:T(8,128)(2,1)S(1)}, bf16[512,256]{1,0:T(8,128)(2,1)S(1)}) custom-call(bf16[512,2048]{1,0:T(8,128)(2,1)S(1)} %get-tuple-element.73.source.refs_0_, bf16[2048,512]{1,0:T(8,128)(2,1)S(1)} %copy-done, bf16[512,512]{1,0:T(8,128)(2,1)S(1)} %get-tuple-element.74.refs_2_, ...), custom_call_target="tpu_custom_call" | custom-call | flops 2147483648 | bytes 6619168 | tf_op jit(solution)/shard_map/pallas_call | solution.py:378
  44.3 1.7 %shard_map.101 = (f32[4,112,256]{2,1,0:T(8,128)S(1)}, f32[4,96,256]{2,1,0:T(8,128)S(1)}, f32[4,96,256]{2,1,0:T(8,128)S(1)}, f32[4,112,256]{2,1,0:T(8,128)S(1)}, ...) custom-call(bf16[512,256]{1,0:T(8,128)(2,1)S(1)} %get-tuple-element.81.refs_0_, ...), custom_call_target="tpu_custom_call" | custom-call | flops 1275068416 | bytes 7340032 | tf_op jit(solution)/shard_map/pallas_call | solution.py:378
  46.0 1.6 %collective-permute-start.11 = (f32[4,112,256]{2,1,0:T(8,128)S(1)}, f32[4,112,256]{2,1,0:T(8,128)S(1)}, u32[]{:S(2)}, u32[]{:S(2)}) collective-permute-start(f32[4,112,256]{2,1,0:T(8,128)S(1)} %get-tuple-element.112), channel_id=1, source_target_pairs={{0,2},{2,0},{4,6},{6,4},{1,3},{3,1},{5,7},{7,5},{8,10},{10,8},{12,... | collective-permute-start | bytes 1376264 | tf_op jit(solution)/shard_map/ppermute | solution.py:477
  47.6 1.2 %shard_map.103 = (f32[4,80,256]{2,1,0:T(8,128)S(1)}, f32[4,64,256]{2,1,0:T(8,128)S(1)}, f32[4,64,256]{2,1,0:T(8,128)S(1)}, f32[4,80,256]{2,1,0:T(8,128)S(1)}, f3...) custom-call(bf16[512,256]{1,0:T(8,128)(2,1)S(1)} %get-tuple-element.81.refs_0_, ...), custom_call_target="tpu_custom_call" | custom-call | flops 872415232 | bytes 7340032 | tf_op jit(solution)/shard_map/pallas_call | solution.py:378
  48.8 0.6 collective-permute-start.13
  49.4 2.8 %collective-permute-start.15 = (f32[4,96,256]{2,1,0:T(8,128)S(1)}, f32[4,96,256]{2,1,0:T(8,128)S(1)}, u32[]{:S(2)}, u32[]{:S(2)}) collective-permute-start(f32[4,96,256]{2,1,0:T(8,128)S(1)} %get-tuple-element.121), channel_id=1, source_target_pairs={{0,6},{6,0},{2,4},{4,2},{1,7},{7,1},{3,5},{5,3},{8,14},{14,8},{10,... | collective-permute-start | bytes 1179656 | tf_op jit(solution)/shard_map/ppermute | solution.py:477
  52.2 0.7 collective-permute-start.19
  52.9 0.5 collective-permute-start.17
  53.4 12.6 %collective-permute-done.13.came = f32[4,80,256]{2,1,0:T(8,128)S(1)} collective-permute-done((f32[4,80,256]{2,1,0:T(8,128)S(1)}, f32[4,80,256]{2,1,0:T(8,128)S(1)}, u32[]{:S(2)}, u32[]{:S(2)}) %collective-permute-start.13) | collective-permute-done | bytes 327712 | tf_op jit(solution)/shard_map/ppermute | solution.py:477
  66.0 0.7 collective-permute-start.21
  66.8 3.1 %collective-permute-start.14 = (f32[2,80,256]{2,1,0:T(8,128)S(1)}, f32[2,80,256]{2,1,0:T(8,128)S(1)}, u32[]{:S(2)}, u32[]{:S(2)}) collective-permute-start(f32[2,80,256]{2,1,0:T(8,128)S(1)} %get-tuple-element.118), channel_id=1, source_target_pairs={{0,6},{6,0},{2,4},{4,2},{1,7},{7,1},{3,5},{5,3},{8,14},{14,8},{10,... | collective-permute-start | bytes 491528 | tf_op jit(solution)/shard_map/ppermute | solution.py:477
  69.9 0.6 collective-permute-start.12
  70.5 1.4 %collective-permute-start.16 = (f32[2,96,256]{2,1,0:T(8,128)S(1)}, f32[2,96,256]{2,1,0:T(8,128)S(1)}, u32[]{:S(2)}, u32[]{:S(2)}) collective-permute-start(f32[2,96,256]{2,1,0:T(8,128)S(1)} %get-tuple-element.123), channel_id=1, source_target_pairs={{0,1},{1,0},{2,3},{3,2},{4,5},{5,4},{6,7},{7,6},{8,9},{9,8},{10,11... | collective-permute-start | bytes 589832 | tf_op jit(solution)/shard_map/ppermute | solution.py:477
  72.0 0.4 collective-permute-start.20
  72.4 2.8 %collective-permute-done.21.came = f32[4,64,256]{2,1,0:T(8,128)S(1)} collective-permute-done((f32[4,64,256]{2,1,0:T(8,128)S(1)}, f32[4,64,256]{2,1,0:T(8,128)S(1)}, u32[]{:S(2)}, u32[]{:S(2)}) %collective-permute-start.21) | collective-permute-done | bytes 262176 | tf_op jit(solution)/shard_map/ppermute | solution.py:477
  75.2 0.6 collective-permute-start.18
  75.8 1.7 %collective-permute-start.22 = (f32[2,64,256]{2,1,0:T(8,128)S(1)}, f32[2,64,256]{2,1,0:T(8,128)S(1)}, u32[]{:S(2)}, u32[]{:S(2)}) collective-permute-start(f32[2,64,256]{2,1,0:T(8,128)S(1)} %get-tuple-element.136), channel_id=1, source_target_pairs={{0,2},{2,0},{4,6},{6,4},{1,3},{3,1},{5,7},{7,5},{8,10},{10,8},{12,... | collective-permute-start | bytes 393224 | tf_op jit(solution)/shard_map/ppermute | solution.py:477
  77.5 1.1 %collective-permute-done.12.came_a = f32[2,112,256]{2,1,0:T(8,128)S(1)} collective-permute-done((f32[2,112,256]{2,1,0:T(8,128)S(1)}, f32[2,112,256]{2,1,0:T(8,128)S(1)}, u32[]{:S(2)}, u32[]{:S(2)}) %collective-permute-start.12) | collective-permute-done | bytes 229408 | tf_op jit(solution)/shard_map/ppermute | solution.py:477
  78.7 1.4 %collective-permute-start.23 = (f32[192,256]{1,0:T(8,128)S(1)}, f32[192,256]{1,0:T(8,128)S(1)}, u32[]{:S(2)}, u32[]{:S(2)}) collective-permute-start(f32[192,256]{1,0:T(8,128)S(1)} %get-tuple-element.138), channel_id=1, source_target_pairs={{0,1},{1,0},{2,3},{3,2},{4,5},{5,4},{6,7},{7,6},{8,9},{9,8},{10,11... | collective-permute-start | bytes 589832 | tf_op jit(solution)/shard_map/ppermute | solution.py:477
  80.1 1.1 %collective-permute-done.18.came_b = f32[2,64,256]{2,1,0:T(8,128)S(1)} collective-permute-done((f32[2,64,256]{2,1,0:T(8,128)S(1)}, f32[2,64,256]{2,1,0:T(8,128)S(1)}, u32[]{:S(2)}, u32[]{:S(2)}) %collective-permute-start.18) | collective-permute-done | bytes 131104 | tf_op jit(solution)/shard_map/ppermute | solution.py:477
  81.3 2.5 %collective-permute-start.24 = (f32[160,256]{1,0:T(8,128)S(1)}, f32[160,256]{1,0:T(8,128)S(1)}, u32[]{:S(2)}, u32[]{:S(2)}) collective-permute-start(f32[160,256]{1,0:T(8,128)S(1)} %get-tuple-element.139), channel_id=1, source_target_pairs={{0,2},{2,0},{4,6},{6,4},{1,3},{3,1},{5,7},{7,5},{8,10},{10,8},{12,... | collective-permute-start | bytes 491528 | tf_op jit(solution)/shard_map/ppermute | solution.py:477
  83.9 2.2 %collective-permute-start.25 = (f32[160,256]{1,0:T(8,128)S(1)}, f32[160,256]{1,0:T(8,128)S(1)}, u32[]{:S(2)}, u32[]{:S(2)}) collective-permute-start(f32[160,256]{1,0:T(8,128)S(1)} %get-tuple-element.140), channel_id=1, source_target_pairs={{0,6},{6,0},{2,4},{4,2},{1,7},{7,1},{3,5},{5,3},{8,14},{14,8},{10,... | collective-permute-start | bytes 491528 | tf_op jit(solution)/shard_map/ppermute | solution.py:477
  86.1 1.1 %collective-permute-done.24.refs_4_ = f32[160,256]{1,0:T(8,128)S(1)} collective-permute-done((f32[160,256]{1,0:T(8,128)S(1)}, f32[160,256]{1,0:T(8,128)S(1)}, u32[]{:S(2)}, u32[]{:S(2)}) %collective-permute-start.24) | collective-permute-done | bytes 163872 | tf_op jit(solution)/shard_map/ppermute | solution.py:477
  87.1 3.4 %collective-permute-done.25.refs_5_ = f32[160,256]{1,0:T(8,128)S(1)} collective-permute-done((f32[160,256]{1,0:T(8,128)S(1)}, f32[160,256]{1,0:T(8,128)S(1)}, u32[]{:S(2)}, u32[]{:S(2)}) %collective-permute-start.25) | collective-permute-done | bytes 163872 | tf_op jit(solution)/shard_map/ppermute | solution.py:477
  90.5 0.8 shard_map.112
  (32 shorter events, 0.5 us)
Async XLA Ops:
  0.0 28.7 %copy-start = (bf16[2048,512]{1,0:T(8,128)(2,1)S(1)}, bf16[2048,512]{1,0:T(8,128)(2,1)}, u32[]{:S(2)}) copy-start(bf16[2048,512]{1,0:T(8,128)(2,1)} %refs_1_.5) | copy-start | bytes 6291460
  0.0 28.7 %copy-start.2 = (f32[8]{0:T(128)S(1)}, f32[8]{0:T(128)}, u32[]{:S(2)}) copy-start(f32[8]{0:T(128)} %refs_7_.5) | copy-start | bytes 100
  7.6 1.6 %collective-permute-start = (f32[136,512]{1,0:T(8,128)S(1)}, f32[136,512]{1,0:T(8,128)S(1)}, u32[]{:S(2)}, u32[]{:S(2)}) collective-permute-start(f32[136,512]{1,0:T(8,128)S(1)} %get-tuple-element.94), channel_id=1, source_target_pairs={{0,8},{8,0},{1,9},{9,1},{2,10},{10,2},{3,11},{11,3},{4,12},{12,4},... | collective-permute-start | bytes 835592 | tf_op jit(solution)/shard_map/ppermute | solution.py:420
  9.3 5.0 %collective-permute-start.1 = (f32[136,128]{1,0:T(8,128)S(1)}, f32[136,128]{1,0:T(8,128)S(1)}, u32[]{:S(2)}, u32[]{:S(2)}) collective-permute-start(f32[136,128]{1,0:T(8,128)S(1)} %get-tuple-element.96), channel_id=1, source_target_pairs={{0,16},{16,32},{32,48},{48,0},{1,17},{17,33},{33,49},{49,1},{2,18}... | collective-permute-start | bytes 208904 | tf_op jit(solution)/shard_map/ppermute | solution.py:391
  10.9 6.3 %collective-permute-start.2 = (f32[136,128]{1,0:T(8,128)S(1)}, f32[136,128]{1,0:T(8,128)S(1)}, u32[]{:S(2)}, u32[]{:S(2)}) collective-permute-start(f32[136,128]{1,0:T(8,128)S(1)} %get-tuple-element.97), channel_id=1, source_target_pairs={{0,32},{16,48},{32,0},{48,16},{1,33},{17,49},{33,1},{49,17},{2,34}... | collective-permute-start | bytes 208904 | tf_op jit(solution)/shard_map/ppermute | solution.py:391
  13.6 4.4 %collective-permute-start.3 = (f32[136,128]{1,0:T(8,128)S(1)}, f32[136,128]{1,0:T(8,128)S(1)}, u32[]{:S(2)}, u32[]{:S(2)}) collective-permute-start(f32[136,128]{1,0:T(8,128)S(1)} %get-tuple-element.98), channel_id=1, source_target_pairs={{0,48},{16,0},{32,16},{48,32},{1,49},{17,1},{33,17},{49,33},{2,50}... | collective-permute-start | bytes 208904 | tf_op jit(solution)/shard_map/ppermute | solution.py:391
  18.1 12.9 %collective-permute-start.4 = (f32[72,128]{1,0:T(8,128)S(1)}, f32[72,128]{1,0:T(8,128)S(1)}, u32[]{:S(2)}, u32[]{:S(2)}) collective-permute-start(f32[72,128]{1,0:T(8,128)S(1)} %get-tuple-element.100), channel_id=1, source_target_pairs={{0,64},{64,128},{128,192},{192,0},{1,65},{65,129},{129,193},{193,1... | collective-permute-start | bytes 110600 | tf_op jit(solution)/shard_map/ppermute | solution.py:391
  20.6 10.3 %collective-permute-start.5 = (f32[72,128]{1,0:T(8,128)S(1)}, f32[72,128]{1,0:T(8,128)S(1)}, u32[]{:S(2)}, u32[]{:S(2)}) collective-permute-start(f32[72,128]{1,0:T(8,128)S(1)} %get-tuple-element.101), channel_id=1, source_target_pairs={{0,128},{64,192},{128,0},{192,64},{1,129},{65,193},{129,1},{193,65... | collective-permute-start | bytes 110600 | tf_op jit(solution)/shard_map/ppermute | solution.py:391
  26.0 5.0 %collective-permute-start.6 = (f32[72,128]{1,0:T(8,128)S(1)}, f32[72,128]{1,0:T(8,128)S(1)}, u32[]{:S(2)}, u32[]{:S(2)}) collective-permute-start(f32[72,128]{1,0:T(8,128)S(1)} %get-tuple-element.102), channel_id=1, source_target_pairs={{0,192},{64,0},{128,64},{192,128},{1,193},{65,1},{129,65},{193,129... | collective-permute-start | bytes 110600 | tf_op jit(solution)/shard_map/ppermute | solution.py:391
  31.1 7.5 %collective-permute-start.7 = (f32[128,128]{1,0:T(8,128)S(1)}, f32[128,128]{1,0:T(8,128)S(1)}, u32[]{:S(2)}, u32[]{:S(2)}) collective-permute-start(f32[128,128]{1,0:T(8,128)S(1)} %get-tuple-element.104), channel_id=1, source_target_pairs={{0,16},{16,32},{32,48},{48,0},{1,17},{17,33},{33,49},{49,1},{2,18}... | collective-permute-start | bytes 196616 | tf_op jit(solution)/shard_map/ppermute | solution.py:391
  32.4 6.1 %collective-permute-start.8 = (f32[128,128]{1,0:T(8,128)S(1)}, f32[128,128]{1,0:T(8,128)S(1)}, u32[]{:S(2)}, u32[]{:S(2)}) collective-permute-start(f32[128,128]{1,0:T(8,128)S(1)} %get-tuple-element.105), channel_id=1, source_target_pairs={{0,32},{16,48},{32,0},{48,16},{1,33},{17,49},{33,1},{49,17},{2,34}... | collective-permute-start | bytes 196616 | tf_op jit(solution)/shard_map/ppermute | solution.py:391
  35.2 4.3 %collective-permute-start.9 = (f32[128,128]{1,0:T(8,128)S(1)}, f32[128,128]{1,0:T(8,128)S(1)}, u32[]{:S(2)}, u32[]{:S(2)}) collective-permute-start(f32[128,128]{1,0:T(8,128)S(1)} %get-tuple-element.106), channel_id=1, source_target_pairs={{0,48},{16,0},{32,16},{48,32},{1,49},{17,1},{33,17},{49,33},{2,50}... | collective-permute-start | bytes 196616 | tf_op jit(solution)/shard_map/ppermute | solution.py:391
  36.6 3.2 %copy-start.1 = (bf16[512,2048]{1,0:T(8,128)(2,1)S(1)}, bf16[512,2048]{1,0:T(8,128)(2,1)}, u32[]{:S(2)}) copy-start(bf16[512,2048]{1,0:T(8,128)(2,1)} %out_w.1) | copy-start | bytes 6291460
  39.6 4.6 %collective-permute-start.10 = (f32[128,512]{1,0:T(8,128)S(1)}, f32[128,512]{1,0:T(8,128)S(1)}, u32[]{:S(2)}, u32[]{:S(2)}) collective-permute-start(f32[128,512]{1,0:T(8,128)S(1)} %get-tuple-element.108), channel_id=1, source_target_pairs={{0,8},{8,0},{1,9},{9,1},{2,10},{10,2},{3,11},{11,3},{4,12},{12,4},... | collective-permute-start | bytes 786440 | tf_op jit(solution)/shard_map/ppermute | solution.py:461
  46.0 20.8 %collective-permute-start.11 = (f32[4,112,256]{2,1,0:T(8,128)S(1)}, f32[4,112,256]{2,1,0:T(8,128)S(1)}, u32[]{:S(2)}, u32[]{:S(2)}) collective-permute-start(f32[4,112,256]{2,1,0:T(8,128)S(1)} %get-tuple-element.112), channel_id=1, source_target_pairs={{0,2},{2,0},{4,6},{6,4},{1,3},{3,1},{5,7},{7,5},{8,10},{10,8},{12,... | collective-permute-start | bytes 1376264 | tf_op jit(solution)/shard_map/ppermute | solution.py:477
  48.8 17.2 %collective-permute-start.13 = (f32[4,80,256]{2,1,0:T(8,128)S(1)}, f32[4,80,256]{2,1,0:T(8,128)S(1)}, u32[]{:S(2)}, u32[]{:S(2)}) collective-permute-start(f32[4,80,256]{2,1,0:T(8,128)S(1)} %get-tuple-element.116), channel_id=1, source_target_pairs={{0,2},{2,0},{4,6},{6,4},{1,3},{3,1},{5,7},{7,5},{8,10},{10,8},{12,... | collective-permute-start | bytes 983048 | tf_op jit(solution)/shard_map/ppermute | solution.py:477
  49.4 20.4 %collective-permute-start.15 = (f32[4,96,256]{2,1,0:T(8,128)S(1)}, f32[4,96,256]{2,1,0:T(8,128)S(1)}, u32[]{:S(2)}, u32[]{:S(2)}) collective-permute-start(f32[4,96,256]{2,1,0:T(8,128)S(1)} %get-tuple-element.121), channel_id=1, source_target_pairs={{0,6},{6,0},{2,4},{4,2},{1,7},{7,1},{3,5},{5,3},{8,14},{14,8},{10,... | collective-permute-start | bytes 1179656 | tf_op jit(solution)/shard_map/ppermute | solution.py:477
  52.2 18.3 %collective-permute-start.19 = (f32[4,96,256]{2,1,0:T(8,128)S(1)}, f32[4,96,256]{2,1,0:T(8,128)S(1)}, u32[]{:S(2)}, u32[]{:S(2)}) collective-permute-start(f32[4,96,256]{2,1,0:T(8,128)S(1)} %get-tuple-element.130), channel_id=1, source_target_pairs={{0,1},{1,0},{2,3},{3,2},{4,5},{5,4},{6,7},{7,6},{8,9},{9,8},{10,11... | collective-permute-start | bytes 1179656 | tf_op jit(solution)/shard_map/ppermute | solution.py:477
  52.9 19.1 %collective-permute-start.17 = (f32[4,64,256]{2,1,0:T(8,128)S(1)}, f32[4,64,256]{2,1,0:T(8,128)S(1)}, u32[]{:S(2)}, u32[]{:S(2)}) collective-permute-start(f32[4,64,256]{2,1,0:T(8,128)S(1)} %get-tuple-element.125), channel_id=1, source_target_pairs={{0,6},{6,0},{2,4},{4,2},{1,7},{7,1},{3,5},{5,3},{8,14},{14,8},{10,... | collective-permute-start | bytes 786440 | tf_op jit(solution)/shard_map/ppermute | solution.py:477
  66.0 9.2 %collective-permute-start.21 = (f32[4,64,256]{2,1,0:T(8,128)S(1)}, f32[4,64,256]{2,1,0:T(8,128)S(1)}, u32[]{:S(2)}, u32[]{:S(2)}) collective-permute-start(f32[4,64,256]{2,1,0:T(8,128)S(1)} %get-tuple-element.134), channel_id=1, source_target_pairs={{0,1},{1,0},{2,3},{3,2},{4,5},{5,4},{6,7},{7,6},{8,9},{9,8},{10,11... | collective-permute-start | bytes 786440 | tf_op jit(solution)/shard_map/ppermute | solution.py:477
  66.8 9.1 %collective-permute-start.14 = (f32[2,80,256]{2,1,0:T(8,128)S(1)}, f32[2,80,256]{2,1,0:T(8,128)S(1)}, u32[]{:S(2)}, u32[]{:S(2)}) collective-permute-start(f32[2,80,256]{2,1,0:T(8,128)S(1)} %get-tuple-element.118), channel_id=1, source_target_pairs={{0,6},{6,0},{2,4},{4,2},{1,7},{7,1},{3,5},{5,3},{8,14},{14,8},{10,... | collective-permute-start | bytes 491528 | tf_op jit(solution)/shard_map/ppermute | solution.py:477
  69.9 8.8 %collective-permute-start.12 = (f32[2,112,256]{2,1,0:T(8,128)S(1)}, f32[2,112,256]{2,1,0:T(8,128)S(1)}, u32[]{:S(2)}, u32[]{:S(2)}) collective-permute-start(f32[2,112,256]{2,1,0:T(8,128)S(1)} %get-tuple-element.114), channel_id=1, source_target_pairs={{0,6},{6,0},{2,4},{4,2},{1,7},{7,1},{3,5},{5,3},{8,14},{14,8},{10,... | collective-permute-start | bytes 688136 | tf_op jit(solution)/shard_map/ppermute | solution.py:477
  70.5 10.8 %collective-permute-start.16 = (f32[2,96,256]{2,1,0:T(8,128)S(1)}, f32[2,96,256]{2,1,0:T(8,128)S(1)}, u32[]{:S(2)}, u32[]{:S(2)}) collective-permute-start(f32[2,96,256]{2,1,0:T(8,128)S(1)} %get-tuple-element.123), channel_id=1, source_target_pairs={{0,1},{1,0},{2,3},{3,2},{4,5},{5,4},{6,7},{7,6},{8,9},{9,8},{10,11... | collective-permute-start | bytes 589832 | tf_op jit(solution)/shard_map/ppermute | solution.py:477
  72.0 11.9 %collective-permute-start.20 = (f32[2,96,256]{2,1,0:T(8,128)S(1)}, f32[2,96,256]{2,1,0:T(8,128)S(1)}, u32[]{:S(2)}, u32[]{:S(2)}) collective-permute-start(f32[2,96,256]{2,1,0:T(8,128)S(1)} %get-tuple-element.132), channel_id=1, source_target_pairs={{0,2},{2,0},{4,6},{6,4},{1,3},{3,1},{5,7},{7,5},{8,10},{10,8},{12,... | collective-permute-start | bytes 589832 | tf_op jit(solution)/shard_map/ppermute | solution.py:477
  75.2 6.1 %collective-permute-start.18 = (f32[2,64,256]{2,1,0:T(8,128)S(1)}, f32[2,64,256]{2,1,0:T(8,128)S(1)}, u32[]{:S(2)}, u32[]{:S(2)}) collective-permute-start(f32[2,64,256]{2,1,0:T(8,128)S(1)} %get-tuple-element.127), channel_id=1, source_target_pairs={{0,1},{1,0},{2,3},{3,2},{4,5},{5,4},{6,7},{7,6},{8,9},{9,8},{10,11... | collective-permute-start | bytes 393224 | tf_op jit(solution)/shard_map/ppermute | solution.py:477
  75.8 8.0 %collective-permute-start.22 = (f32[2,64,256]{2,1,0:T(8,128)S(1)}, f32[2,64,256]{2,1,0:T(8,128)S(1)}, u32[]{:S(2)}, u32[]{:S(2)}) collective-permute-start(f32[2,64,256]{2,1,0:T(8,128)S(1)} %get-tuple-element.136), channel_id=1, source_target_pairs={{0,2},{2,0},{4,6},{6,4},{1,3},{3,1},{5,7},{7,5},{8,10},{10,8},{12,... | collective-permute-start | bytes 393224 | tf_op jit(solution)/shard_map/ppermute | solution.py:477
  78.7 11.8 %collective-permute-start.23 = (f32[192,256]{1,0:T(8,128)S(1)}, f32[192,256]{1,0:T(8,128)S(1)}, u32[]{:S(2)}, u32[]{:S(2)}) collective-permute-start(f32[192,256]{1,0:T(8,128)S(1)} %get-tuple-element.138), channel_id=1, source_target_pairs={{0,1},{1,0},{2,3},{3,2},{4,5},{5,4},{6,7},{7,6},{8,9},{9,8},{10,11... | collective-permute-start | bytes 589832 | tf_op jit(solution)/shard_map/ppermute | solution.py:477
  81.3 5.8 %collective-permute-start.24 = (f32[160,256]{1,0:T(8,128)S(1)}, f32[160,256]{1,0:T(8,128)S(1)}, u32[]{:S(2)}, u32[]{:S(2)}) collective-permute-start(f32[160,256]{1,0:T(8,128)S(1)} %get-tuple-element.139), channel_id=1, source_target_pairs={{0,2},{2,0},{4,6},{6,4},{1,3},{3,1},{5,7},{7,5},{8,10},{10,8},{12,... | collective-permute-start | bytes 491528 | tf_op jit(solution)/shard_map/ppermute | solution.py:477
  83.9 6.6 %collective-permute-start.25 = (f32[160,256]{1,0:T(8,128)S(1)}, f32[160,256]{1,0:T(8,128)S(1)}, u32[]{:S(2)}, u32[]{:S(2)}) collective-permute-start(f32[160,256]{1,0:T(8,128)S(1)} %get-tuple-element.140), channel_id=1, source_target_pairs={{0,6},{6,0},{2,4},{4,2},{1,7},{7,1},{3,5},{5,3},{8,14},{14,8},{10,... | collective-permute-start | bytes 491528 | tf_op jit(solution)/shard_map/ppermute | solution.py:477

commit v6 on v5

--- a/solution.py
+++ b/solution.py
@@ -93,7 +93,9 @@
     log_out[...] = log
     log_cols[...] = jnp.transpose(jnp.concatenate([log] * (128 // (2 * heads)), axis=0))
     total = jnp.where(ahead, log[:, rows - 1 :], log[:, :1])
-    to_end = (jnp.exp(total - log) * step).astype(BF16)
+    to_end = jnp.exp(total - log) * step
+    to_end = jnp.transpose(jnp.concatenate([to_end] * (128 // (2 * heads)), axis=0))
+    lane = lax.broadcasted_iota(jnp.int32, (rows, 128), 1)
     decay = jnp.exp(total)
     d_fwd = jnp.sum(pick * decay[:heads], axis=0, keepdims=True)
     d_bwd = jnp.sum(pick * decay[heads:], axis=0, keepdims=True)
@@ -104,7 +106,10 @@
     copies[4 + len(chunks)].wait()
     mine = lax.axis_index("core") == 0
     for source, inputs, proj, b in ((seq, in_f, proj_f, 0), (flipped, in_b, proj_b, 1)):
-        weight = dot(to_end[b * heads : (b + 1) * heads], pick.astype(BF16), ((0,), (0,)))
+        spread = []
+        for h in range(b * heads, (b + 1) * heads, 2):
+            spread.append(jnp.where(lane < 64, to_end[:, h : h + 1], to_end[:, h + 1 : h + 2]))
+        weight = jnp.concatenate(spread, axis=1)
         values = dot(source[...], input_w[...]).astype(BF16)
         inputs[...] = values
         weighted = (values.astype(F32) * weight).astype(BF16)

time: 91.5 us -> 91.6 us (level)
  no operation moved by 1% of the time
where the time goes in v6:
time: 91.6 us; the launch traced here: 91.3 us
  starting transfers between devices  41.7 us (46%)
  waiting for transfers between devices  28.9 us (32%)
  Pallas kernels  20.6 us (22%)
    ppermute x15, waiting for transfers between devices, travel(): return lax.ppermute(value, axis, pairs)  22.6 us
    ppermute x9, starting transfers between devices, shifted(): lax.ppermute(v, axis, [(j, (j + k) % 4) for j in range(4)])  21.3 us
    pallas_call x22, Pallas kernels, call(): pl.pallas_call(kernel, out_shape=outs, in_specs=specs, out_specs=[VMEM_SP...  20.6 us
    ppermute x15, starting transfers between devices, travel(): return lax.ppermute(value, axis, pairs)  20.2 us
    ppermute x9, waiting for transfers between devices, shifted(): lax.ppermute(v, axis, [(j, (j + k) % 4) for j in range(4)])  4.67 us
  transfers between devices with their start and end apart: 26, of which 10 were waited for; matrix products, arithmetic and copies ran while one was open for 0% of the time, Pallas kernels for 11%

profile of v6, /device:TPU:8, one launch (start us, length us, event | category | flops | bytes accessed | tf_op | source)
XLA Modules:
  0.0 91.3 jit_solution(1976018268492334489)
XLA Ops:
  0.0 7.5 %shard_map.91 = (bf16[512,2048]{1,0:T(8,128)(2,1)S(1)}, bf16[512,2048]{1,0:T(8,128)(2,1)S(1)}, bf16[512,512]{1,0:T(8,128)(2,1)S(1)}, bf16[512,512]{1,0:T(8,128)(...) custom-call(bf16[512,2048]{1,0:T(8,128)(2,1)} %seq_hbm.1, ...), custom_call_target="tpu_custom_call" | custom-call | flops 3221225472 | bytes 5275712 | tf_op jit(solution)/shard_map/pallas_call | solution.py:383
  7.5 0.1 collective-permute-start
  7.6 1.5 %collective-permute-done.got.other = f32[136,512]{1,0:T(8,128)S(1)} collective-permute-done((f32[136,512]{1,0:T(8,128)S(1)}, f32[136,512]{1,0:T(8,128)S(1)}, u32[]{:S(2)}, u32[]{:S(2)}) %collective-permute-start) | collective-permute-done | bytes 278560 | tf_op jit(solution)/shard_map/ppermute | solution.py:425
  9.1 0.1 shard_map.96
  9.2 1.7 %collective-permute-start.1 = (f32[136,128]{1,0:T(8,128)S(1)}, f32[136,128]{1,0:T(8,128)S(1)}, u32[]{:S(2)}, u32[]{:S(2)}) collective-permute-start(f32[136,128]{1,0:T(8,128)S(1)} %get-tuple-element.96), channel_id=1, source_target_pairs={{0,16},{16,32},{32,48},{48,0},{1,17},{17,33},{33,49},{49,1},{2,18}... | collective-permute-start | bytes 208904 | tf_op jit(solution)/shard_map/ppermute | solution.py:396
  10.9 2.6 %collective-permute-start.2 = (f32[136,128]{1,0:T(8,128)S(1)}, f32[136,128]{1,0:T(8,128)S(1)}, u32[]{:S(2)}, u32[]{:S(2)}) collective-permute-start(f32[136,128]{1,0:T(8,128)S(1)} %get-tuple-element.97), channel_id=1, source_target_pairs={{0,32},{16,48},{32,0},{48,16},{1,33},{17,49},{33,1},{49,17},{2,34}... | collective-permute-start | bytes 208904 | tf_op jit(solution)/shard_map/ppermute | solution.py:396
  13.5 0.7 collective-permute-start.3
  14.2 2.9 %collective-permute-done.2.got2 = f32[136,128]{1,0:T(8,128)S(1)} collective-permute-done((f32[136,128]{1,0:T(8,128)S(1)}, f32[136,128]{1,0:T(8,128)S(1)}, u32[]{:S(2)}, u32[]{:S(2)}) %collective-permute-start.2) | collective-permute-done | bytes 69664 | tf_op jit(solution)/shard_map/ppermute | solution.py:396
  17.2 0.8 collective-permute-done.3.got3
  18.0 2.5 %collective-permute-start.4 = (f32[72,128]{1,0:T(8,128)S(1)}, f32[72,128]{1,0:T(8,128)S(1)}, u32[]{:S(2)}, u32[]{:S(2)}) collective-permute-start(f32[72,128]{1,0:T(8,128)S(1)} %get-tuple-element.100), channel_id=1, source_target_pairs={{0,64},{64,128},{128,192},{192,0},{1,65},{65,129},{129,193},{193,1... | collective-permute-start | bytes 110600 | tf_op jit(solution)/shard_map/ppermute | solution.py:396
  20.5 5.4 %collective-permute-start.5 = (f32[72,128]{1,0:T(8,128)S(1)}, f32[72,128]{1,0:T(8,128)S(1)}, u32[]{:S(2)}, u32[]{:S(2)}) collective-permute-start(f32[72,128]{1,0:T(8,128)S(1)} %get-tuple-element.101), channel_id=1, source_target_pairs={{0,128},{64,192},{128,0},{192,64},{1,129},{65,193},{129,1},{193,65... | collective-permute-start | bytes 110600 | tf_op jit(solution)/shard_map/ppermute | solution.py:396
  25.9 2.7 %collective-permute-start.6 = (f32[72,128]{1,0:T(8,128)S(1)}, f32[72,128]{1,0:T(8,128)S(1)}, u32[]{:S(2)}, u32[]{:S(2)}) collective-permute-start(f32[72,128]{1,0:T(8,128)S(1)} %get-tuple-element.102), channel_id=1, source_target_pairs={{0,192},{64,0},{128,64},{192,128},{1,193},{65,1},{129,65},{193,129... | collective-permute-start | bytes 110600 | tf_op jit(solution)/shard_map/ppermute | solution.py:396
  28.6 2.2 %shard_map.94 = (bf16[512,256]{1,0:T(8,128)(2,1)S(1)}, bf16[512,256]{1,0:T(8,128)(2,1)S(1)}, f32[512,512]{1,0:T(8,128)S(1)}) custom-call(bf16[512,2048]{1,0:T(8,128)(2,1)S(1)} %get-tuple-element.85.refs_0_, bf16[2048,512]{1,0:T(8,128)(2,1)S(1)} %copy-done, bf16[512,512]{1,0:T(8,128)(2,1)S(1)} %get-tuple-element.86.refs_2_, ...), custom_call_target="tpu_custom_call" | custom-call | flops 1073741824 | bytes 5308448 | tf_op jit(solution)/shard_map/pallas_call | solution.py:383
  30.9 0.1 shard_map.98
  31.0 1.5 %collective-permute-start.7 = (f32[128,128]{1,0:T(8,128)S(1)}, f32[128,128]{1,0:T(8,128)S(1)}, u32[]{:S(2)}, u32[]{:S(2)}) collective-permute-start(f32[128,128]{1,0:T(8,128)S(1)} %get-tuple-element.104), channel_id=1, source_target_pairs={{0,16},{16,32},{32,48},{48,0},{1,17},{17,33},{33,49},{49,1},{2,18}... | collective-permute-start | bytes 196616 | tf_op jit(solution)/shard_map/ppermute | solution.py:396
  32.5 2.8 %collective-permute-start.8 = (f32[128,128]{1,0:T(8,128)S(1)}, f32[128,128]{1,0:T(8,128)S(1)}, u32[]{:S(2)}, u32[]{:S(2)}) collective-permute-start(f32[128,128]{1,0:T(8,128)S(1)} %get-tuple-element.105), channel_id=1, source_target_pairs={{0,32},{16,48},{32,0},{48,16},{1,33},{17,49},{33,1},{49,17},{2,34}... | collective-permute-start | bytes 196616 | tf_op jit(solution)/shard_map/ppermute | solution.py:396
  35.3 1.3 %collective-permute-start.9 = (f32[128,128]{1,0:T(8,128)S(1)}, f32[128,128]{1,0:T(8,128)S(1)}, u32[]{:S(2)}, u32[]{:S(2)}) collective-permute-start(f32[128,128]{1,0:T(8,128)S(1)} %get-tuple-element.106), channel_id=1, source_target_pairs={{0,48},{16,0},{32,16},{48,32},{1,49},{17,1},{33,17},{49,33},{2,50}... | collective-permute-start | bytes 196616 | tf_op jit(solution)/shard_map/ppermute | solution.py:396
  36.7 2.0 %shard_map.95 = (bf16[512,256]{1,0:T(8,128)(2,1)S(1)}, bf16[512,256]{1,0:T(8,128)(2,1)S(1)}) custom-call(bf16[512,2048]{1,0:T(8,128)(2,1)S(1)} %get-tuple-element.85.refs_0_, bf16[2048,512]{1,0:T(8,128)(2,1)S(1)} %copy-done, bf16[512,512]{1,0:T(8,128)(2,1)S(1)} %get-tuple-element.86.refs_2_, bf16[512,256]{1,0:T(8,128)(2,1)S(1)} %get-tuple-element.87.refs_3_.refs_9_, ...), custom_call_target="tpu_custom_call" | custom-call | flops 1073741824 | bytes 6357024 | tf_op jit(solution)/shard_map/pallas_call | solution.py:383
  38.7 1.0 %collective-permute-done.9.got3 = f32[128,128]{1,0:T(8,128)S(1)} collective-permute-done((f32[128,128]{1,0:T(8,128)S(1)}, f32[128,128]{1,0:T(8,128)S(1)}, u32[]{:S(2)}, u32[]{:S(2)}) %collective-permute-start.9) | collective-permute-done | bytes 65568 | tf_op jit(solution)/shard_map/ppermute | solution.py:396
  39.6 0.1 shard_map.99
  39.7 0.1 collective-permute-start.10
  39.8 0.7 shard_map.100
  40.6 0.9 shard_map.92
  41.4 2.9 %shard_map.93 = (bf16[512,256]{1,0:T(8,128)(2,1)S(1)}, bf16[512,256]{1,0:T(8,128)(2,1)S(1)}, bf16[512,256]{1,0:T(8,128)(2,1)S(1)}, bf16[512,256]{1,0:T(8,128)(2,1)S(1)}) custom-call(bf16[512,2048]{1,0:T(8,128)(2,1)S(1)} %get-tuple-element.73.source.refs_0_, bf16[2048,512]{1,0:T(8,128)(2,1)S(1)} %copy-done, bf16[512,512]{1,0:T(8,128)(2,1)S(1)} %get-tuple-element.74.refs_2_, ...), custom_call_target="tpu_custom_call" | custom-call | flops 2147483648 | bytes 6619168 | tf_op jit(solution)/shard_map/pallas_call | solution.py:383
  44.4 1.7 %shard_map.101 = (f32[4,112,256]{2,1,0:T(8,128)S(1)}, f32[4,96,256]{2,1,0:T(8,128)S(1)}, f32[4,96,256]{2,1,0:T(8,128)S(1)}, f32[4,112,256]{2,1,0:T(8,128)S(1)}, ...) custom-call(bf16[512,256]{1,0:T(8,128)(2,1)S(1)} %get-tuple-element.81.refs_0_, ...), custom_call_target="tpu_custom_call" | custom-call | flops 1275068416 | bytes 7340032 | tf_op jit(solution)/shard_map/pallas_call | solution.py:383
  46.1 1.6 %collective-permute-start.11 = (f32[4,112,256]{2,1,0:T(8,128)S(1)}, f32[4,112,256]{2,1,0:T(8,128)S(1)}, u32[]{:S(2)}, u32[]{:S(2)}) collective-permute-start(f32[4,112,256]{2,1,0:T(8,128)S(1)} %get-tuple-element.112), channel_id=1, source_target_pairs={{0,2},{2,0},{4,6},{6,4},{1,3},{3,1},{5,7},{7,5},{8,10},{10,8},{12,... | collective-permute-start | bytes 1376264 | tf_op jit(solution)/shard_map/ppermute | solution.py:482
  47.7 1.2 %shard_map.103 = (f32[4,80,256]{2,1,0:T(8,128)S(1)}, f32[4,64,256]{2,1,0:T(8,128)S(1)}, f32[4,64,256]{2,1,0:T(8,128)S(1)}, f32[4,80,256]{2,1,0:T(8,128)S(1)}, f3...) custom-call(bf16[512,256]{1,0:T(8,128)(2,1)S(1)} %get-tuple-element.81.refs_0_, ...), custom_call_target="tpu_custom_call" | custom-call | flops 872415232 | bytes 7340032 | tf_op jit(solution)/shard_map/pallas_call | solution.py:383
  48.9 0.6 collective-permute-start.13
  49.5 2.8 %collective-permute-start.15 = (f32[4,96,256]{2,1,0:T(8,128)S(1)}, f32[4,96,256]{2,1,0:T(8,128)S(1)}, u32[]{:S(2)}, u32[]{:S(2)}) collective-permute-start(f32[4,96,256]{2,1,0:T(8,128)S(1)} %get-tuple-element.121), channel_id=1, source_target_pairs={{0,6},{6,0},{2,4},{4,2},{1,7},{7,1},{3,5},{5,3},{8,14},{14,8},{10,... | collective-permute-start | bytes 1179656 | tf_op jit(solution)/shard_map/ppermute | solution.py:482
  52.3 0.7 collective-permute-start.19
  53.0 0.5 collective-permute-start.17
  53.5 12.6 %collective-permute-done.13.came = f32[4,80,256]{2,1,0:T(8,128)S(1)} collective-permute-done((f32[4,80,256]{2,1,0:T(8,128)S(1)}, f32[4,80,256]{2,1,0:T(8,128)S(1)}, u32[]{:S(2)}, u32[]{:S(2)}) %collective-permute-start.13) | collective-permute-done | bytes 327712 | tf_op jit(solution)/shard_map/ppermute | solution.py:482
  66.1 0.7 collective-permute-start.21
  66.9 2.8 %collective-permute-start.14 = (f32[2,80,256]{2,1,0:T(8,128)S(1)}, f32[2,80,256]{2,1,0:T(8,128)S(1)}, u32[]{:S(2)}, u32[]{:S(2)}) collective-permute-start(f32[2,80,256]{2,1,0:T(8,128)S(1)} %get-tuple-element.118), channel_id=1, source_target_pairs={{0,6},{6,0},{2,4},{4,2},{1,7},{7,1},{3,5},{5,3},{8,14},{14,8},{10,... | collective-permute-start | bytes 491528 | tf_op jit(solution)/shard_map/ppermute | solution.py:482
  69.8 0.6 collective-permute-start.12
  70.4 1.4 %collective-permute-start.16 = (f32[2,96,256]{2,1,0:T(8,128)S(1)}, f32[2,96,256]{2,1,0:T(8,128)S(1)}, u32[]{:S(2)}, u32[]{:S(2)}) collective-permute-start(f32[2,96,256]{2,1,0:T(8,128)S(1)} %get-tuple-element.123), channel_id=1, source_target_pairs={{0,1},{1,0},{2,3},{3,2},{4,5},{5,4},{6,7},{7,6},{8,9},{9,8},{10,11... | collective-permute-start | bytes 589832 | tf_op jit(solution)/shard_map/ppermute | solution.py:482
  71.9 0.4 collective-permute-start.20
  72.3 3.0 %collective-permute-done.21.came = f32[4,64,256]{2,1,0:T(8,128)S(1)} collective-permute-done((f32[4,64,256]{2,1,0:T(8,128)S(1)}, f32[4,64,256]{2,1,0:T(8,128)S(1)}, u32[]{:S(2)}, u32[]{:S(2)}) %collective-permute-start.21) | collective-permute-done | bytes 262176 | tf_op jit(solution)/shard_map/ppermute | solution.py:482
  75.3 0.7 collective-permute-start.18
  76.0 1.6 %collective-permute-start.22 = (f32[2,64,256]{2,1,0:T(8,128)S(1)}, f32[2,64,256]{2,1,0:T(8,128)S(1)}, u32[]{:S(2)}, u32[]{:S(2)}) collective-permute-start(f32[2,64,256]{2,1,0:T(8,128)S(1)} %get-tuple-element.136), channel_id=1, source_target_pairs={{0,2},{2,0},{4,6},{6,4},{1,3},{3,1},{5,7},{7,5},{8,10},{10,8},{12,... | collective-permute-start | bytes 393224 | tf_op jit(solution)/shard_map/ppermute | solution.py:482
  77.6 0.9 %collective-permute-done.12.came_a = f32[2,112,256]{2,1,0:T(8,128)S(1)} collective-permute-done((f32[2,112,256]{2,1,0:T(8,128)S(1)}, f32[2,112,256]{2,1,0:T(8,128)S(1)}, u32[]{:S(2)}, u32[]{:S(2)}) %collective-permute-start.12) | collective-permute-done | bytes 229408 | tf_op jit(solution)/shard_map/ppermute | solution.py:482
  78.6 1.4 %collective-permute-start.23 = (f32[192,256]{1,0:T(8,128)S(1)}, f32[192,256]{1,0:T(8,128)S(1)}, u32[]{:S(2)}, u32[]{:S(2)}) collective-permute-start(f32[192,256]{1,0:T(8,128)S(1)} %get-tuple-element.138), channel_id=1, source_target_pairs={{0,1},{1,0},{2,3},{3,2},{4,5},{5,4},{6,7},{7,6},{8,9},{9,8},{10,11... | collective-permute-start | bytes 589832 | tf_op jit(solution)/shard_map/ppermute | solution.py:482
  80.0 1.6 %collective-permute-done.18.came_b = f32[2,64,256]{2,1,0:T(8,128)S(1)} collective-permute-done((f32[2,64,256]{2,1,0:T(8,128)S(1)}, f32[2,64,256]{2,1,0:T(8,128)S(1)}, u32[]{:S(2)}, u32[]{:S(2)}) %collective-permute-start.18) | collective-permute-done | bytes 131104 | tf_op jit(solution)/shard_map/ppermute | solution.py:482
  81.6 2.3 %collective-permute-start.24 = (f32[160,256]{1,0:T(8,128)S(1)}, f32[160,256]{1,0:T(8,128)S(1)}, u32[]{:S(2)}, u32[]{:S(2)}) collective-permute-start(f32[160,256]{1,0:T(8,128)S(1)} %get-tuple-element.139), channel_id=1, source_target_pairs={{0,2},{2,0},{4,6},{6,4},{1,3},{3,1},{5,7},{7,5},{8,10},{10,8},{12,... | collective-permute-start | bytes 491528 | tf_op jit(solution)/shard_map/ppermute | solution.py:482
  84.0 2.2 %collective-permute-start.25 = (f32[160,256]{1,0:T(8,128)S(1)}, f32[160,256]{1,0:T(8,128)S(1)}, u32[]{:S(2)}, u32[]{:S(2)}) collective-permute-start(f32[160,256]{1,0:T(8,128)S(1)} %get-tuple-element.140), channel_id=1, source_target_pairs={{0,6},{6,0},{2,4},{4,2},{1,7},{7,1},{3,5},{5,3},{8,14},{14,8},{10,... | collective-permute-start | bytes 491528 | tf_op jit(solution)/shard_map/ppermute | solution.py:482
  86.2 1.1 %collective-permute-done.24.refs_4_ = f32[160,256]{1,0:T(8,128)S(1)} collective-permute-done((f32[160,256]{1,0:T(8,128)S(1)}, f32[160,256]{1,0:T(8,128)S(1)}, u32[]{:S(2)}, u32[]{:S(2)}) %collective-permute-start.24) | collective-permute-done | bytes 163872 | tf_op jit(solution)/shard_map/ppermute | solution.py:482
  87.2 3.4 %collective-permute-done.25.refs_5_ = f32[160,256]{1,0:T(8,128)S(1)} collective-permute-done((f32[160,256]{1,0:T(8,128)S(1)}, f32[160,256]{1,0:T(8,128)S(1)}, u32[]{:S(2)}, u32[]{:S(2)}) %collective-permute-start.25) | collective-permute-done | bytes 163872 | tf_op jit(solution)/shard_map/ppermute | solution.py:482
  90.6 0.8 shard_map.112
  (32 shorter events, 0.5 us)
Async XLA Ops:
  0.0 28.6 %copy-start = (bf16[2048,512]{1,0:T(8,128)(2,1)S(1)}, bf16[2048,512]{1,0:T(8,128)(2,1)}, u32[]{:S(2)}) copy-start(bf16[2048,512]{1,0:T(8,128)(2,1)} %refs_1_.5) | copy-start | bytes 6291460
  0.0 28.6 %copy-start.2 = (f32[8]{0:T(128)S(1)}, f32[8]{0:T(128)}, u32[]{:S(2)}) copy-start(f32[8]{0:T(128)} %refs_7_.5) | copy-start | bytes 100
  7.5 1.6 %collective-permute-start = (f32[136,512]{1,0:T(8,128)S(1)}, f32[136,512]{1,0:T(8,128)S(1)}, u32[]{:S(2)}, u32[]{:S(2)}) collective-permute-start(f32[136,512]{1,0:T(8,128)S(1)} %get-tuple-element.94), channel_id=1, source_target_pairs={{0,8},{8,0},{1,9},{9,1},{2,10},{10,2},{3,11},{11,3},{4,12},{12,4},... | collective-permute-start | bytes 835592 | tf_op jit(solution)/shard_map/ppermute | solution.py:425
  9.2 5.0 %collective-permute-start.1 = (f32[136,128]{1,0:T(8,128)S(1)}, f32[136,128]{1,0:T(8,128)S(1)}, u32[]{:S(2)}, u32[]{:S(2)}) collective-permute-start(f32[136,128]{1,0:T(8,128)S(1)} %get-tuple-element.96), channel_id=1, source_target_pairs={{0,16},{16,32},{32,48},{48,0},{1,17},{17,33},{33,49},{49,1},{2,18}... | collective-permute-start | bytes 208904 | tf_op jit(solution)/shard_map/ppermute | solution.py:396
  10.9 6.3 %collective-permute-start.2 = (f32[136,128]{1,0:T(8,128)S(1)}, f32[136,128]{1,0:T(8,128)S(1)}, u32[]{:S(2)}, u32[]{:S(2)}) collective-permute-start(f32[136,128]{1,0:T(8,128)S(1)} %get-tuple-element.97), channel_id=1, source_target_pairs={{0,32},{16,48},{32,0},{48,16},{1,33},{17,49},{33,1},{49,17},{2,34}... | collective-permute-start | bytes 208904 | tf_op jit(solution)/shard_map/ppermute | solution.py:396
  13.5 4.4 %collective-permute-start.3 = (f32[136,128]{1,0:T(8,128)S(1)}, f32[136,128]{1,0:T(8,128)S(1)}, u32[]{:S(2)}, u32[]{:S(2)}) collective-permute-start(f32[136,128]{1,0:T(8,128)S(1)} %get-tuple-element.98), channel_id=1, source_target_pairs={{0,48},{16,0},{32,16},{48,32},{1,49},{17,1},{33,17},{49,33},{2,50}... | collective-permute-start | bytes 208904 | tf_op jit(solution)/shard_map/ppermute | solution.py:396
  18.0 12.9 %collective-permute-start.4 = (f32[72,128]{1,0:T(8,128)S(1)}, f32[72,128]{1,0:T(8,128)S(1)}, u32[]{:S(2)}, u32[]{:S(2)}) collective-permute-start(f32[72,128]{1,0:T(8,128)S(1)} %get-tuple-element.100), channel_id=1, source_target_pairs={{0,64},{64,128},{128,192},{192,0},{1,65},{65,129},{129,193},{193,1... | collective-permute-start | bytes 110600 | tf_op jit(solution)/shard_map/ppermute | solution.py:396
  20.5 10.3 %collective-permute-start.5 = (f32[72,128]{1,0:T(8,128)S(1)}, f32[72,128]{1,0:T(8,128)S(1)}, u32[]{:S(2)}, u32[]{:S(2)}) collective-permute-start(f32[72,128]{1,0:T(8,128)S(1)} %get-tuple-element.101), channel_id=1, source_target_pairs={{0,128},{64,192},{128,0},{192,64},{1,129},{65,193},{129,1},{193,65... | collective-permute-start | bytes 110600 | tf_op jit(solution)/shard_map/ppermute | solution.py:396
  25.9 5.0 %collective-permute-start.6 = (f32[72,128]{1,0:T(8,128)S(1)}, f32[72,128]{1,0:T(8,128)S(1)}, u32[]{:S(2)}, u32[]{:S(2)}) collective-permute-start(f32[72,128]{1,0:T(8,128)S(1)} %get-tuple-element.102), channel_id=1, source_target_pairs={{0,192},{64,0},{128,64},{192,128},{1,193},{65,1},{129,65},{193,129... | collective-permute-start | bytes 110600 | tf_op jit(solution)/shard_map/ppermute | solution.py:396
  31.0 7.7 %collective-permute-start.7 = (f32[128,128]{1,0:T(8,128)S(1)}, f32[128,128]{1,0:T(8,128)S(1)}, u32[]{:S(2)}, u32[]{:S(2)}) collective-permute-start(f32[128,128]{1,0:T(8,128)S(1)} %get-tuple-element.104), channel_id=1, source_target_pairs={{0,16},{16,32},{32,48},{48,0},{1,17},{17,33},{33,49},{49,1},{2,18}... | collective-permute-start | bytes 196616 | tf_op jit(solution)/shard_map/ppermute | solution.py:396
  32.5 6.1 %collective-permute-start.8 = (f32[128,128]{1,0:T(8,128)S(1)}, f32[128,128]{1,0:T(8,128)S(1)}, u32[]{:S(2)}, u32[]{:S(2)}) collective-permute-start(f32[128,128]{1,0:T(8,128)S(1)} %get-tuple-element.105), channel_id=1, source_target_pairs={{0,32},{16,48},{32,0},{48,16},{1,33},{17,49},{33,1},{49,17},{2,34}... | collective-permute-start | bytes 196616 | tf_op jit(solution)/shard_map/ppermute | solution.py:396
  35.3 4.3 %collective-permute-start.9 = (f32[128,128]{1,0:T(8,128)S(1)}, f32[128,128]{1,0:T(8,128)S(1)}, u32[]{:S(2)}, u32[]{:S(2)}) collective-permute-start(f32[128,128]{1,0:T(8,128)S(1)} %get-tuple-element.106), channel_id=1, source_target_pairs={{0,48},{16,0},{32,16},{48,32},{1,49},{17,1},{33,17},{49,33},{2,50}... | collective-permute-start | bytes 196616 | tf_op jit(solution)/shard_map/ppermute | solution.py:396
  36.7 3.2 %copy-start.1 = (bf16[512,2048]{1,0:T(8,128)(2,1)S(1)}, bf16[512,2048]{1,0:T(8,128)(2,1)}, u32[]{:S(2)}) copy-start(bf16[512,2048]{1,0:T(8,128)(2,1)} %out_w.1) | copy-start | bytes 6291460
  39.7 4.6 %collective-permute-start.10 = (f32[128,512]{1,0:T(8,128)S(1)}, f32[128,512]{1,0:T(8,128)S(1)}, u32[]{:S(2)}, u32[]{:S(2)}) collective-permute-start(f32[128,512]{1,0:T(8,128)S(1)} %get-tuple-element.108), channel_id=1, source_target_pairs={{0,8},{8,0},{1,9},{9,1},{2,10},{10,2},{3,11},{11,3},{4,12},{12,4},... | collective-permute-start | bytes 786440 | tf_op jit(solution)/shard_map/ppermute | solution.py:466
  46.1 20.8 %collective-permute-start.11 = (f32[4,112,256]{2,1,0:T(8,128)S(1)}, f32[4,112,256]{2,1,0:T(8,128)S(1)}, u32[]{:S(2)}, u32[]{:S(2)}) collective-permute-start(f32[4,112,256]{2,1,0:T(8,128)S(1)} %get-tuple-element.112), channel_id=1, source_target_pairs={{0,2},{2,0},{4,6},{6,4},{1,3},{3,1},{5,7},{7,5},{8,10},{10,8},{12,... | collective-permute-start | bytes 1376264 | tf_op jit(solution)/shard_map/ppermute | solution.py:482
  48.9 17.2 %collective-permute-start.13 = (f32[4,80,256]{2,1,0:T(8,128)S(1)}, f32[4,80,256]{2,1,0:T(8,128)S(1)}, u32[]{:S(2)}, u32[]{:S(2)}) collective-permute-start(f32[4,80,256]{2,1,0:T(8,128)S(1)} %get-tuple-element.116), channel_id=1, source_target_pairs={{0,2},{2,0},{4,6},{6,4},{1,3},{3,1},{5,7},{7,5},{8,10},{10,8},{12,... | collective-permute-start | bytes 983048 | tf_op jit(solution)/shard_map/ppermute | solution.py:482
  49.5 20.2 %collective-permute-start.15 = (f32[4,96,256]{2,1,0:T(8,128)S(1)}, f32[4,96,256]{2,1,0:T(8,128)S(1)}, u32[]{:S(2)}, u32[]{:S(2)}) collective-permute-start(f32[4,96,256]{2,1,0:T(8,128)S(1)} %get-tuple-element.121), channel_id=1, source_target_pairs={{0,6},{6,0},{2,4},{4,2},{1,7},{7,1},{3,5},{5,3},{8,14},{14,8},{10,... | collective-permute-start | bytes 1179656 | tf_op jit(solution)/shard_map/ppermute | solution.py:482
  52.3 18.1 %collective-permute-start.19 = (f32[4,96,256]{2,1,0:T(8,128)S(1)}, f32[4,96,256]{2,1,0:T(8,128)S(1)}, u32[]{:S(2)}, u32[]{:S(2)}) collective-permute-start(f32[4,96,256]{2,1,0:T(8,128)S(1)} %get-tuple-element.130), channel_id=1, source_target_pairs={{0,1},{1,0},{2,3},{3,2},{4,5},{5,4},{6,7},{7,6},{8,9},{9,8},{10,11... | collective-permute-start | bytes 1179656 | tf_op jit(solution)/shard_map/ppermute | solution.py:482
  53.0 18.9 %collective-permute-start.17 = (f32[4,64,256]{2,1,0:T(8,128)S(1)}, f32[4,64,256]{2,1,0:T(8,128)S(1)}, u32[]{:S(2)}, u32[]{:S(2)}) collective-permute-start(f32[4,64,256]{2,1,0:T(8,128)S(1)} %get-tuple-element.125), channel_id=1, source_target_pairs={{0,6},{6,0},{2,4},{4,2},{1,7},{7,1},{3,5},{5,3},{8,14},{14,8},{10,... | collective-permute-start | bytes 786440 | tf_op jit(solution)/shard_map/ppermute | solution.py:482
  66.1 9.2 %collective-permute-start.21 = (f32[4,64,256]{2,1,0:T(8,128)S(1)}, f32[4,64,256]{2,1,0:T(8,128)S(1)}, u32[]{:S(2)}, u32[]{:S(2)}) collective-permute-start(f32[4,64,256]{2,1,0:T(8,128)S(1)} %get-tuple-element.134), channel_id=1, source_target_pairs={{0,1},{1,0},{2,3},{3,2},{4,5},{5,4},{6,7},{7,6},{8,9},{9,8},{10,11... | collective-permute-start | bytes 786440 | tf_op jit(solution)/shard_map/ppermute | solution.py:482
  66.9 9.2 %collective-permute-start.14 = (f32[2,80,256]{2,1,0:T(8,128)S(1)}, f32[2,80,256]{2,1,0:T(8,128)S(1)}, u32[]{:S(2)}, u32[]{:S(2)}) collective-permute-start(f32[2,80,256]{2,1,0:T(8,128)S(1)} %get-tuple-element.118), channel_id=1, source_target_pairs={{0,6},{6,0},{2,4},{4,2},{1,7},{7,1},{3,5},{5,3},{8,14},{14,8},{10,... | collective-permute-start | bytes 491528 | tf_op jit(solution)/shard_map/ppermute | solution.py:482
  69.8 8.8 %collective-permute-start.12 = (f32[2,112,256]{2,1,0:T(8,128)S(1)}, f32[2,112,256]{2,1,0:T(8,128)S(1)}, u32[]{:S(2)}, u32[]{:S(2)}) collective-permute-start(f32[2,112,256]{2,1,0:T(8,128)S(1)} %get-tuple-element.114), channel_id=1, source_target_pairs={{0,6},{6,0},{2,4},{4,2},{1,7},{7,1},{3,5},{5,3},{8,14},{14,8},{10,... | collective-permute-start | bytes 688136 | tf_op jit(solution)/shard_map/ppermute | solution.py:482
  70.4 11.2 %collective-permute-start.16 = (f32[2,96,256]{2,1,0:T(8,128)S(1)}, f32[2,96,256]{2,1,0:T(8,128)S(1)}, u32[]{:S(2)}, u32[]{:S(2)}) collective-permute-start(f32[2,96,256]{2,1,0:T(8,128)S(1)} %get-tuple-element.123), channel_id=1, source_target_pairs={{0,1},{1,0},{2,3},{3,2},{4,5},{5,4},{6,7},{7,6},{8,9},{9,8},{10,11... | collective-permute-start | bytes 589832 | tf_op jit(solution)/shard_map/ppermute | solution.py:482
  71.9 12.1 %collective-permute-start.20 = (f32[2,96,256]{2,1,0:T(8,128)S(1)}, f32[2,96,256]{2,1,0:T(8,128)S(1)}, u32[]{:S(2)}, u32[]{:S(2)}) collective-permute-start(f32[2,96,256]{2,1,0:T(8,128)S(1)} %get-tuple-element.132), channel_id=1, source_target_pairs={{0,2},{2,0},{4,6},{6,4},{1,3},{3,1},{5,7},{7,5},{8,10},{10,8},{12,... | collective-permute-start | bytes 589832 | tf_op jit(solution)/shard_map/ppermute | solution.py:482
  75.3 6.3 %collective-permute-start.18 = (f32[2,64,256]{2,1,0:T(8,128)S(1)}, f32[2,64,256]{2,1,0:T(8,128)S(1)}, u32[]{:S(2)}, u32[]{:S(2)}) collective-permute-start(f32[2,64,256]{2,1,0:T(8,128)S(1)} %get-tuple-element.127), channel_id=1, source_target_pairs={{0,1},{1,0},{2,3},{3,2},{4,5},{5,4},{6,7},{7,6},{8,9},{9,8},{10,11... | collective-permute-start | bytes 393224 | tf_op jit(solution)/shard_map/ppermute | solution.py:482
  76.0 7.9 %collective-permute-start.22 = (f32[2,64,256]{2,1,0:T(8,128)S(1)}, f32[2,64,256]{2,1,0:T(8,128)S(1)}, u32[]{:S(2)}, u32[]{:S(2)}) collective-permute-start(f32[2,64,256]{2,1,0:T(8,128)S(1)} %get-tuple-element.136), channel_id=1, source_target_pairs={{0,2},{2,0},{4,6},{6,4},{1,3},{3,1},{5,7},{7,5},{8,10},{10,8},{12,... | collective-permute-start | bytes 393224 | tf_op jit(solution)/shard_map/ppermute | solution.py:482
  78.6 12.0 %collective-permute-start.23 = (f32[192,256]{1,0:T(8,128)S(1)}, f32[192,256]{1,0:T(8,128)S(1)}, u32[]{:S(2)}, u32[]{:S(2)}) collective-permute-start(f32[192,256]{1,0:T(8,128)S(1)} %get-tuple-element.138), channel_id=1, source_target_pairs={{0,1},{1,0},{2,3},{3,2},{4,5},{5,4},{6,7},{7,6},{8,9},{9,8},{10,11... | collective-permute-start | bytes 589832 | tf_op jit(solution)/shard_map/ppermute | solution.py:482
  81.6 5.6 %collective-permute-start.24 = (f32[160,256]{1,0:T(8,128)S(1)}, f32[160,256]{1,0:T(8,128)S(1)}, u32[]{:S(2)}, u32[]{:S(2)}) collective-permute-start(f32[160,256]{1,0:T(8,128)S(1)} %get-tuple-element.139), channel_id=1, source_target_pairs={{0,2},{2,0},{4,6},{6,4},{1,3},{3,1},{5,7},{7,5},{8,10},{10,8},{12,... | collective-permute-start | bytes 491528 | tf_op jit(solution)/shard_map/ppermute | solution.py:482
  84.0 6.6 %collective-permute-start.25 = (f32[160,256]{1,0:T(8,128)S(1)}, f32[160,256]{1,0:T(8,128)S(1)}, u32[]{:S(2)}, u32[]{:S(2)}) collective-permute-start(f32[160,256]{1,0:T(8,128)S(1)} %get-tuple-element.140), channel_id=1, source_target_pairs={{0,6},{6,0},{2,4},{4,2},{1,7},{7,1},{3,5},{5,3},{8,14},{14,8},{10,... | collective-permute-start | bytes 491528 | tf_op jit(solution)/shard_map/ppermute | solution.py:482
